TPU v7x, 128 devices: a whole 4x4x4 slice. The times are simulated.
128 devices in a mesh: row: 16 (over z, y), col: 8 (over x, core).
Axes of the slice: x: 4, y: 4, z: 4, core: 2. Of those that a mesh axis runs over, the one named last changes fastest.
Arguments:
- trailing: float32 [16384, 16384], P('row', 'col'), may hold values from -40 to 40, as said below
- factor_one: float32 [16384, 512], P(('row', 'col')), may hold values from -0.0390625 to 0.0390625
- inverse_one: float32 [512, 512], replicated, may hold values from -1 to 2, as said below
- factor_two_top: float32 [512, 512], replicated, may hold values from -0.0390625 to 0.0390625
- factor_two: float32 [16384, 512], P(('row', 'col')), may hold values from -0.0390625 to 0.0390625
- inverse_two: float32 [512, 512], replicated, may hold values from -1 to 2, as said below
- structure_one: int32 [96], replicated, may hold values from 0 to 127, as said below
- structure_two: int32 [94], replicated, may hold values from 0 to 127, as said below
Outputs:
- column_one: float32 [16384, 512], P(('row', 'col'))
- diagonal_one: float32 [512, 512], replicated
- column_two: float32 [16384, 512], P(('row', 'col'))
- cross_two: float32 [512, 512], replicated
- diagonal_two: float32 [512, 512], replicated
Inputs may be any that keep to these rules, and one draw needn't show every extreme that they name: `trailing`: symmetric. `inverse_one`: lower triangular, diagonal between 1 and 2. `inverse_two`: lower triangular, diagonal between 1 and 2. `structure_one`: distinct, rising; lists block 0 and the last block. `structure_two`: distinct, rising, each also listed in structure_one; lists block 0 and the last block.
All inputs are finite; a program needn't handle non-finite values.
Results may differ from a plain program's by a relative error of at most 0.0003.
Values sent between devices are 32-bit elements; how exact they have to be, the bound alone decides.
No kernel may reach another device: no remote copies, remote signals or barrier semaphores. Data moves between devices by JAX's collectives and lax.ppermute only.
A program may use at most 128 MiB of HBM per device.

v0:
```python
import jax
import jax.numpy as jnp
from jax import lax
from jax.sharding import PartitionSpec as P

BLK = 128


def spread(x, axis, root):
    mine = lax.axis_index(axis) == root
    return lax.psum(jnp.where(mine, x, jnp.zeros_like(x)), axis)


def product(left, right):
    return jnp.dot(left, right, precision=lax.Precision.HIGHEST, preferred_element_type=jnp.float32)


def block_flags(structure, first_row, count):
    blocks = (first_row + jnp.arange(count, dtype=jnp.int32)) // BLK
    hits = jnp.any(blocks[:, None] == structure[None, :], axis=1)
    return hits.astype(jnp.float32)[:, None]


def panel_apart(normal, col_index, spread_count):
    row_block = lax.all_gather(normal, "col", axis=0, tiled=True)
    pieces = []
    for offset in range(spread_count):
        pieces.append(spread(row_block, "row", col_index * spread_count + offset))
    return (row_block, jnp.concatenate(pieces, axis=0))


def sweep(trailing, col_block, own_normal):
    summed = lax.psum_scatter(-product(trailing, col_block), "col", scatter_dimension=0, tiled=True)
    quad_part = product(own_normal.T, summed)
    return (summed, quad_part)


def body(
    trailing,
    factor_one,
    inverse_one,
    factor_two_top,
    factor_two,
    inverse_two,
    structure_one,
    structure_two,
):
    piece_rows = factor_one.shape[0]
    spread_count = lax.axis_size("row") // lax.axis_size("col")
    row_index = lax.axis_index("row")
    col_index = lax.axis_index("col")
    first_row = (row_index * lax.axis_size("col") + col_index) * piece_rows
    mask_one = block_flags(structure_one, first_row, piece_rows)
    mask_two = block_flags(structure_two, first_row, piece_rows)
    normal_one = mask_one * product(factor_one, inverse_one)
    normal_two = mask_two * product(factor_two, inverse_two)
    rows_one, cols_one = panel_apart(normal_one, col_index, spread_count)
    rows_two, cols_two = panel_apart(normal_two, col_index, spread_count)
    summed_one, quad_one = sweep(trailing, cols_one, normal_one)
    column_one = mask_one * summed_one
    diag_total = lax.psum(quad_one, ("row", "col"))
    diagonal_one = product(inverse_one.T, inverse_one) - diag_total
    normal_top = product(factor_two_top, inverse_two)
    summed_two, quad_two = sweep(trailing, cols_two, normal_two)
    local_part = -product(column_one, normal_top)
    column_two = mask_two * (local_part + summed_two)
    cross_total, second_total = lax.psum(
        (product(column_one.T, normal_two), product(normal_two.T, local_part) + quad_two),
        ("row", "col"),
    )
    cross_two = -(product(diagonal_one, normal_top) + cross_total)
    diagonal_two = (
        product(inverse_two.T, inverse_two) - product(normal_top.T, cross_two) - second_total
    )
    return (column_one, diagonal_one, column_two, cross_two, diagonal_two)


def solution(mesh):
    return jax.shard_map(
        body,
        mesh=mesh,
        in_specs=(
            P("row", "col"),
            P(("row", "col"), None),
            P(),
            P(),
            P(("row", "col"), None),
            P(),
            P(),
            P(),
        ),
        out_specs=(P(("row", "col"), None), P(), P(("row", "col"), None), P(), P()),
        check_vma=False,
    )
```

profile of v0, /device:TPU:1, one launch (start us, length us, event | category | flops | bytes accessed | tf_op | source)
XLA Modules:
  0.0 474.7 jit_solution(2318638378639296707)
XLA Ops:
  7.2 0.0 copy-start
  7.2 0.0 all-gather.5.cloned.1.call-start
  7.3 0.9 compare_reduce_fusion
  8.2 0.3 copy-done
  8.4 2.4 convolution_multiply_fusion
  10.8 0.0 all-gather.5.cloned.1.call-update
  10.8 0.0 all-gather.3.cloned.1.call-start
  10.9 0.7 compare_reduce_fusion.1
  11.6 2.4 convolution_multiply_fusion.1
  14.0 0.0 all-gather.3.cloned.1.call-update
  14.0 0.0 all-reduce.7.cloned.1.call-start
  14.1 25.6 %all-gather.5.cloned.1.call-done = f32[1024,512]{1,0:T(8,128)} async-done(((f32[128,512]{1,0:T(8,128)}), f32[1024,512]{1,0:T(8,128)}) %all-gather.5.cloned.1.call-update) | async-done | bytes 2097168 | tf_op jit(solution)/shard_map/all_gather | solution.py:25
  39.7 4.2 broadcast_select_fusion.1
  43.9 23.5 %all-gather.3.cloned.1.call-done = f32[1024,512]{1,0:T(8,128)} async-done(((f32[128,512]{1,0:T(8,128)}), f32[1024,512]{1,0:T(8,128)}) %all-gather.3.cloned.1.call-update) | async-done | bytes 2097168 | tf_op jit(solution)/shard_map/all_gather | solution.py:25
  67.5 4.2 broadcast_select_fusion.3
  71.6 0.0 all-reduce.7.cloned.1.call-update
  71.7 0.0 reduce-scatter.3.cloned.1.call-start
  71.7 142.3 %all-reduce.7.cloned.1.call-done = (f32[1024,512]{1,0:T(8,128)}, f32[1024,512]{1,0:T(8,128)}, f32[1024,512]{1,0:T(8,128)}, f32[1024,512]{1,0:T(8,128)}) async-done(((f32[1024,512]{1,0:T(8,128)}, f32[1024,512]{1,0:T(8,128)}, f32[1024,512]{1,0:T(8,128)}, f32[1024,512]{1,0:T(8,128)}), (f32[1024,512]{1,0:T(8,128)}, f32[1024,512]{1,0:T(8,128)}, f32[1024,512]{1,0:T(8,128)}, ...) | async-done | bytes 8388624 | tf_op jit(solution)/shard_map/psum | solution.py:11
  214.0 17.6 %negate_bitcast_fusion.1 = f32[1024,512]{1,0:T(8,128)} fusion(f32[1024,2048]{1,0:T(8,128)} %param.8, f32[1024,512]{1,0:T(8,128)} %get-tuple-element.8, f32[1024,512]{1,0:T(8,128)} %get-tuple-element.9), kind=kOutput, calls=%fused_computation.9 | convolution fusion | flops 12886474752 | bytes 14680064 | tf_op jit(solution)/shard_map/dot_general | solution.py:15
  231.7 0.0 reduce-scatter.3.cloned.1.call-update
  231.7 0.0 reduce-scatter.5.cloned.1.call-start
  231.8 17.7 %negate_bitcast_fusion = f32[1024,512]{1,0:T(8,128)} fusion(f32[1024,2048]{1,0:T(8,128)} %param.8, f32[1024,512]{1,0:T(8,128)} %get-tuple-element.10, f32[1024,512]{1,0:T(8,128)} %get-tuple-element.11), kind=kOutput, calls=%fused_computation.8 | convolution fusion | flops 12886474752 | bytes 14680064 | tf_op jit(solution)/shard_map/dot_general | solution.py:15
  249.4 0.0 reduce-scatter.5.cloned.1.call-update
  249.5 0.0 copy-start.2
  249.5 0.2 all-reduce.5.cloned.1.call-start
  249.7 3.1 fusion.17
  252.8 9.0 %reduce-scatter.3.cloned.1.call-done = f32[128,512]{1,0:T(8,128)} async-done(((f32[1024,512]{1,0:T(8,128)}), f32[128,512]{1,0:T(8,128)}) %reduce-scatter.3.cloned.1.call-update) | async-done | bytes 262160 | tf_op jit(solution)/shard_map/reduce_scatter | solution.py:33
  261.8 1.0 broadcast_multiply_fusion
  262.9 0.0 copy-start.6
  262.9 0.7 copy-done.6
  263.6 2.0 fusion.18
  265.6 31.1 %reduce-scatter.5.cloned.1.call-done = f32[128,512]{1,0:T(8,128)} async-done(((f32[1024,512]{1,0:T(8,128)}), f32[128,512]{1,0:T(8,128)}) %reduce-scatter.5.cloned.1.call-update) | async-done | bytes 262160 | tf_op jit(solution)/shard_map/reduce_scatter | solution.py:33
  296.7 2.5 add_multiply_fusion
  299.2 1.0 fusion.20
  300.3 2.0 fusion.16
  302.3 0.0 copy-done.9
  302.3 2.0 convolution_add_fusion.1
  304.3 0.0 all-reduce.5.cloned.1.call-update
  304.3 2.9 fusion.19
  307.2 152.7 %all-reduce.5.cloned.1.call-done = (f32[512,512]{1,0:T(8,128)}, f32[512,512]{1,0:T(8,128)}, f32[512,512]{1,0:T(8,128)}) async-done(((f32[512,512]{1,0:T(8,128)}, f32[512,512]{1,0:T(8,128)}, f32[512,512]{1,0:T(8,128)}), (f32[512,512]{1,0:T(8,128)}, f32[512,512]{1,0:T(8,128)}, f32[512,512]{1,0:T(8,128)})) %all-reduce.5.cloned.1.call-update) | async-done | bytes 3145744 | tf_op jit(solution)/shard_map/psum | solution.py:61
  459.8 3.2 convolution_subtract_fusion.1
  463.0 0.0 copy-start.5
  463.1 1.9 fusion.13
  464.9 0.0 copy-start.4
  465.0 0.0 copy-done.3
  465.0 0.0 copy-done.8
  465.0 2.9 fusion.12
  467.9 0.0 copy-done.4
  (16 shorter events, 0.1 us)
Async XLA Ops:
  7.2 1.2 copy-start
  7.2 4.4 copy-start.1
  7.2 32.5 %all-gather.5.cloned.1.call-start = ((), (), s32[]{:S(2)}) async-start(), calls=%async_computation.4 | async-start | bytes 2359296 | tf_op jit(solution)/shard_map/all_gather | solution.py:25
  10.8 56.7 %all-gather.3.cloned.1.call-start = ((), (), s32[]{:S(2)}) async-start(), calls=%async_computation.2 | async-start | bytes 2359296 | tf_op jit(solution)/shard_map/all_gather | solution.py:25
  14.0 200.0 %all-reduce.7.cloned.1.call-start = ((), (), s32[]{:S(2)}) async-start(), calls=%async_computation.7 | async-start | bytes 16777216 | tf_op jit(solution)/shard_map/psum | solution.py:11
  71.7 190.2 %reduce-scatter.3.cloned.1.call-start = ((), (), s32[]{:S(2)}) async-start(), calls=%async_computation.3 | async-start | bytes 2359296 | tf_op jit(solution)/shard_map/reduce_scatter | solution.py:33
  231.7 65.0 %reduce-scatter.5.cloned.1.call-start = ((), (), s32[]{:S(2)}) async-start(), calls=%async_computation.5 | async-start | bytes 2359296 | tf_op jit(solution)/shard_map/reduce_scatter | solution.py:33
  249.5 14.1 %copy-start.2 = (f32[128,512]{1,0:T(8,128)S(1)}, f32[128,512]{1,0:T(8,128)}, u32[]{:S(2)}) copy-start(f32[128,512]{1,0:T(8,128)} %convolution_multiply_fusion) | copy-start | bytes 786436
  249.5 210.4 %all-reduce.5.cloned.1.call-start = ((), (), s32[]{:S(2)}) async-start(), calls=%async_computation.6 | async-start | bytes 6291456 | tf_op jit(solution)/shard_map/psum | solution.py:61
  262.9 0.7 copy-start.6
  296.7 3.6 copy-start.7
  296.7 3.6 copy-start.10
  299.2 3.1 copy-start.9
  459.8 3.2 copy-start.11
  463.0 1.9 copy-start.5
  463.0 1.9 copy-start.3
  463.1 1.9 copy-start.8
  464.9 2.9 copy-start.4
Sparse Core Ops, SparseCore 0:
  10.9 28.7 all-gather.4
  42.0 25.4 all-gather.2
  71.8 142.2 all-reduce.6
  231.8 29.9 reduce-scatter.2
  264.2 32.4 reduce-scatter.4
  304.5 155.3 all-reduce.4
where the time goes:
time: 475 us
  waiting for transfers between devices  384 us (81%)
  matrix products  63.5 us (13%)
  between operations  14.3 us (3%)
  other arithmetic  11.1 us (2%)
    psum x1, waiting for transfers between devices, body(): diag_total = lax.psum(quad_one, ('row', 'col'))  153 us
    psum x1, waiting for transfers between devices, spread(): return lax.psum(jnp.where(mine, x, jnp.zeros_like(x)), axis)  142 us
    dot_general x14, matrix products, product(): jnp.dot(left, right, precision=lax.Precision.HIGHEST, preferred_element_t...  63.5 us
    all_gather x2, waiting for transfers between devices, panel_apart(): row_block = lax.all_gather(normal, 'col', axis=0, tiled=True)  49.2 us
    reduce_scatter x2, waiting for transfers between devices, sweep(): lax.psum_scatter(-product(trailing, col_block), 'col', scatter_dimension=...  40.2 us
  transfers between devices with their start and end apart: 6, of which 6 were waited for; matrix products, arithmetic and copies ran while one was open for 7% of the time, Pallas kernels for 0%

commit v1 on v0

v1 whole, which is shorter than its diff:
```python
import functools

import jax
import jax.numpy as jnp
from jax import lax
from jax.experimental import pallas as pl
from jax.experimental.pallas import tpu as pltpu
from jax.sharding import PartitionSpec as P

BLK = 128
W = 512
BOTH = ("row", "col")
SWAP = [(i, i ^ 1) for i in range(8)]
F32 = jnp.float32
BF16 = jnp.bfloat16


def product(left, right):
    return jnp.dot(left, right, precision=lax.Precision.HIGH, preferred_element_type=F32)


def product_t(left, right):
    return lax.dot_general(
        left, right, (((0,), (0,)), ((), ())), precision=lax.Precision.HIGH, preferred_element_type=F32
    )


def block_flag(structure, block):
    return jnp.any(structure == block).astype(F32)


def params():
    return pltpu.CompilerParams(vmem_limit_bytes=48 << 20)


def halves(value):
    high = value.astype(BF16)
    return high, (value - high.astype(F32)).astype(BF16)


def three(left_high, left_low, right_high, right_low):
    dot = functools.partial(jnp.dot, preferred_element_type=F32)
    return dot(left_high, right_high) + (dot(left_low, right_high) + dot(left_high, right_low))


def flip_kernel(block, high, low):
    high[...], low[...] = halves(block[...].T)


def flipped(trailing):
    rows, cols = trailing.shape
    step = 256
    out = jax.ShapeDtypeStruct((cols, rows), BF16)
    spec = pl.BlockSpec((step, rows), lambda i: (i, 0))
    return pl.pallas_call(
        flip_kernel,
        grid=(cols // step,),
        in_specs=[pl.BlockSpec((rows, step), lambda i: (0, i))],
        out_specs=[spec, spec],
        out_shape=[out, out],
        compiler_params=params(),
        name="flip",
    )(trailing)


def far_kernel(rows, places, *refs):
    pieces, flips, outs = refs[:8], refs[8:16], refs[16:]
    high, low, top, bottom = outs
    for i, piece in enumerate(pieces):
        at = pl.ds(pl.multiple_of(places[i] * BLK, BLK), BLK)
        high[at, :], low[at, :] = halves(piece[...])
    panel_high, panel_low = high[...], low[...]
    for half, out in ((0, top), (1, bottom)):
        left_high = jnp.concatenate([flips[4 * 0 + 2 * half][...], flips[4 * 0 + 2 * half + 1][...]], axis=0)
        left_low = jnp.concatenate([flips[4 + 2 * half][...], flips[4 + 2 * half + 1][...]], axis=0)
        out[...] = three(left_high, left_low, panel_high, panel_low)


def far_product(rows, places, pieces, flip_high, flip_low):
    count = flip_high.shape[1]
    whole = lambda shape: pl.BlockSpec(shape, lambda i, r, p: (0, 0))
    block = [pl.BlockSpec((BLK, count), functools.partial(lambda j, i, r, p: (r[j], 0), j)) for j in range(4)]
    return pl.pallas_call(
        far_kernel,
        grid_spec=pltpu.PrefetchScalarGridSpec(
            num_scalar_prefetch=2,
            grid=(1,),
            in_specs=[whole((BLK, W))] * 8 + block + block,
            out_specs=[whole((count, W))] * 2 + [whole((2 * BLK, W))] * 2,
        ),
        out_shape=[jax.ShapeDtypeStruct((count, W), BF16)] * 2 + [jax.ShapeDtypeStruct((2 * BLK, W), F32)] * 2,
        compiler_params=params(),
        name="far",
    )(rows, places, *pieces, *([flip_high] * 4), *([flip_low] * 4))


def near_kernel(rows, *refs):
    flips, (high, low, out) = refs[:8], refs[8:]
    left_high = jnp.concatenate([f[...] for f in flips[:4]], axis=0)
    left_low = jnp.concatenate([f[...] for f in flips[4:]], axis=0)
    out[0] = three(left_high, left_low, high[...], low[...])


def near_product(rows, panel_high, panel_low, flip_high, flip_low):
    count = flip_high.shape[1]
    whole = pl.BlockSpec((count, W), lambda i, r: (0, 0))
    block = [pl.BlockSpec((BLK, count), functools.partial(lambda j, i, r: (r[4 * i + j], 0), j)) for j in range(4)]
    return pl.pallas_call(
        near_kernel,
        grid_spec=pltpu.PrefetchScalarGridSpec(
            num_scalar_prefetch=1,
            grid=(3,),
            in_specs=block + block + [whole, whole],
            out_specs=pl.BlockSpec((1, 4 * BLK, W), lambda i, r: (i, 0, 0)),
        ),
        out_shape=jax.ShapeDtypeStruct((3, 4 * BLK, W), F32),
        compiler_params=params(),
        name="near",
    )(rows, *([flip_high] * 4), *([flip_low] * 4), panel_high, panel_low)


def col_ring(s):
    return [(i, (i + 2 * s) % 8) for i in range(8)]


def row_ring(over, s):
    if over == "z":
        return [(r, (r + 4 * s) % 16) for r in range(16)]
    return [(r, r // 4 * 4 + (r + s) % 4) for r in range(16)]


def gather_row(panel, first):
    mine = [panel] + [lax.ppermute(panel, "col", col_ring(s)) for s in (1, 3, 2)]
    mine, first = lax.optimization_barrier((mine, first))
    return mine + [lax.ppermute(piece, "col", SWAP) for piece in mine], first


def gather_places(x, k):
    places = []
    for core in (k, 1 - k):
        places += [((x + 4 - s) % 4) * 2 + core for s in (0, 1, 3, 2)]
    return jnp.stack(places).astype(jnp.int32)


def block_at(z, y, x, k):
    moved = (y // 2 + k) % 2
    upper = moved * (1 - y % 2) + (1 - moved) * (y % 2)
    return upper * 8 + (z + x) % 4 * 2 + moved


def chunk_rows(over, place, x, k):
    if over == "z":
        return [block_at(place, j, x, k) for j in range(4)]
    return [block_at(j, place, x, k) for j in range(4)]


def home_pairs():
    pairs = []
    for z in range(4):
        for y in range(4):
            for x in range(4):
                for k in range(2):
                    col = 2 * x + k
                    pairs.append(((z * 4 + y) * 8 + col, col * 16 + block_at(z, y, x, k)))
    return pairs


def sweep(pieces, places, over, place, other, x, k, flip_high, flip_low):
    chunk = lambda s: chunk_rows(over, (place + s) % 4, x, k)
    table = lambda rows: jnp.stack(rows).astype(jnp.int32)
    high, low, top, bottom = far_product(table(chunk(2)), places, pieces, flip_high, flip_low)
    top = lax.ppermute(top, "row", row_ring(over, 1))
    bottom = lax.ppermute(bottom, "row", row_ring(over, 3))
    near = near_product(table(chunk(1) + chunk(3) + chunk(0)), high, low, flip_high, flip_low)
    ahead = jnp.concatenate([near[0, : 2 * BLK] + top, near[0, 2 * BLK :]], axis=0)
    behind = jnp.concatenate([near[1, : 2 * BLK], near[1, 2 * BLK :] + bottom], axis=0)
    ahead = lax.ppermute(ahead, "row", row_ring(over, 1))
    behind = lax.ppermute(behind, "row", row_ring(over, 3))
    total = (near[2] + (ahead + behind)).reshape(4, BLK, W)
    across = "y" if over == "z" else "z"
    pick = lambda s: lax.dynamic_index_in_dim(total, (other + s) % 4, 0, keepdims=False)
    return pick(0) + sum(lax.ppermute(pick(s), "row", row_ring(across, s)) for s in (1, 2, 3))


def sum_over_all(part, k, beside):
    rows = part.shape[0]
    split = part.reshape(2, rows // 2, BLK)
    keep = lax.dynamic_index_in_dim(split, k, 0, keepdims=False)
    give = lax.dynamic_index_in_dim(split, 1 - k, 0, keepdims=False)
    kept = keep + lax.ppermute(give, "col", SWAP)
    piece = rows // 32
    mine = lax.all_to_all(kept.reshape(16, piece, BLK), "row", 0, 0, tiled=True).sum(axis=0)
    mine = mine + sum(lax.ppermute(mine, "col", col_ring(s)) for s in (1, 2, 3))
    mine, beside = lax.optimization_barrier((mine, beside))
    wide = jnp.broadcast_to(mine[None], (16, piece, BLK))
    half = lax.all_to_all(wide, "row", 0, 0, tiled=True).reshape(rows // 2, BLK)
    return half, lax.ppermute(half, "col", SWAP), beside


def finish_kernel(core, half, other, square_one, square_top, base_two, one, cross, two, total):
    rows = half.shape[0]
    k = core[0]
    total[pl.ds(pl.multiple_of(k * rows, 8), rows), :] = half[...]
    total[pl.ds(pl.multiple_of((1 - k) * rows, 8), rows), :] = other[...]
    at = 0
    for out, base in ((one, square_one), (cross, square_top), (two, base_two)):
        for j in range(4):
            cols = slice(j * BLK, (j + 1) * BLK)
            if out is cross:
                out[:, cols] = total[at : at + W, :] - base[:, cols]
                at += W
                continue
            size = W - j * BLK
            out[j * BLK :, cols] = total[at : at + size, :] + base[j * BLK :, cols]
            for i in range(j + 1, 4):
                below = total[at + (i - j) * BLK : at + (i - j + 1) * BLK, :]
                rows_i = slice(i * BLK, (i + 1) * BLK)
                out[cols, rows_i] = below.T + base[cols, rows_i]
            at += size


def finish(k, half, other, square_one, square_top, base_two):
    square = jax.ShapeDtypeStruct((W, W), F32)
    vmem = pl.BlockSpec(memory_space=pltpu.VMEM)
    return pl.pallas_call(
        finish_kernel,
        in_specs=[pl.BlockSpec(memory_space=pltpu.SMEM)] + [vmem] * 5,
        out_specs=[vmem] * 3,
        out_shape=[square] * 3,
        scratch_shapes=[pltpu.VMEM((2 * half.shape[0], BLK), F32)],
        compiler_params=params(),
        name="finish",
    )(k.reshape(1).astype(jnp.int32), half, other, square_one, square_top, base_two)


def body(
    trailing,
    factor_one,
    inverse_one,
    factor_two_top,
    factor_two,
    inverse_two,
    structure_one,
    structure_two,
):
    row = lax.axis_index("row")
    col = lax.axis_index("col")
    z, y, x, k = row // 4, row % 4, col // 2, col % 2
    mask_one = block_flag(structure_one, row * 8 + col)
    mask_two = block_flag(structure_two, row * 8 + col)
    places = gather_places(x, k)
    home_way = home_pairs()
    out_way = [(there, here) for here, there in home_way]

    normal_one = mask_one * product(factor_one, inverse_one)
    flips = flipped(trailing)
    pieces_one, flips = gather_row(normal_one, flips)
    flip_high, flip_low = flips
    normal_top = product(factor_two_top, inverse_two)
    panel_two = mask_two * product(factor_two, inverse_two) - product(normal_one, normal_top)
    moved_one = lax.ppermute(normal_one, BOTH, out_way)
    moved_two = lax.ppermute(panel_two, BOTH, out_way)
    pieces_two, moved_one = gather_row(panel_two, moved_one)

    sums_one = sweep(pieces_one, places, "z", z, y, x, k, flip_high, flip_low)
    pieces_two, moved_two = lax.optimization_barrier((pieces_two, moved_two))
    sums_two = sweep(pieces_two, places, "y", y, z, x, k, flip_high, flip_low)
    sums = jnp.concatenate([sums_one, sums_two], axis=1)

    panels = jnp.concatenate([moved_one, moved_two], axis=1)
    quad = product_t(panels, sums)
    cut = lambda first, last, j: quad[first:last, j * BLK : (j + 1) * BLK]
    parts = [cut(j * BLK, W, j) for j in range(4)]
    parts += [cut(0, W, 4 + j) for j in range(4)]
    parts += [cut(W + j * BLK, 2 * W, 4 + j) for j in range(4)]
    home = lax.ppermute(sums, BOTH, home_way)
    half, other, home = sum_over_all(jnp.concatenate(parts, axis=0), k, home)
    column_one = -mask_one * home[:, :W]
    column_two = -mask_two * home[:, W:]
    square_one = product_t(inverse_one, inverse_one)
    square_top = product(square_one, normal_top)
    base_two = product_t(inverse_two, inverse_two) + product_t(normal_top, square_top)
    diagonal_one, cross_two, diagonal_two = finish(k, half, other, square_one, square_top, base_two)
    return (column_one, diagonal_one, column_two, cross_two, diagonal_two)


def solution(mesh):
    return jax.shard_map(
        body,
        mesh=mesh,
        in_specs=(
            P("row", "col"),
            P(("row", "col"), None),
            P(),
            P(),
            P(("row", "col"), None),
            P(),
            P(),
            P(),
        ),
        out_specs=(P(("row", "col"), None), P(), P(("row", "col"), None), P(), P()),
        check_vma=False,
    )
```

time: 475 us -> 242 us (0.51)
  waiting for transfers between devices: 384 us -> 79.9 us
  starting transfers between devices: 0.43 us -> 77.1 us
  matrix products: 63.5 us -> 13.4 us
  Pallas kernels: 0 us -> 36.3 us
  local copies, waits for them, and re-layouts: 1.01 us -> 14.1 us
  between operations: 14.3 us -> 2.52 us
  other arithmetic: 11.1 us -> 18 us
    psum x2 -> x0, waiting for transfers between devices: 295 us -> none  [the longest x1 153 us: body(): diag_total = lax.psum(quad_one, ('row', 'col'))]
    ppermute x0 -> x36, starting transfers between devices: none -> 64.6 us  [the longest x2 14.3 us: sweep(): top = lax.ppermute(top, 'row', row_ring(over, 1))]
    dot_general x14 -> x9, matrix products: 63.5 us -> 13.4 us  [the longest x4 7.53 us: product_t(): lax.dot_general(left, right, (((0,), (0,)), ((), ())), precision=lax.Prec...]
    all_gather x2 -> x0, waiting for transfers between devices: 49.2 us -> none  [panel_apart(): row_block = lax.all_gather(normal, 'col', axis=0, tiled=True)]
    ppermute x0 -> x36, waiting for transfers between devices: none -> 41.6 us  [the longest x2 17.9 us: sweep(): behind = lax.ppermute(behind, 'row', row_ring(over, 3))]
    reduce_scatter x2 -> x0, waiting for transfers between devices: 40.2 us -> none  [sweep(): lax.psum_scatter(-product(trailing, col_block), 'col', scatter_dimension=...]
    all_to_all x0 -> x2, waiting for transfers between devices: none -> 38.3 us  [the longest x1 24.2 us: sum_over_all(): lax.all_to_all(kept.reshape(16, piece, BLK), 'row', 0, 0, tiled=True)]
    pallas_call x0 -> x6, Pallas kernels: none -> 36.3 us  [the longest x2 16.1 us: near_product(): pl.pallas_call(near_kernel, grid_spec=pltpu.PrefetchScalarGridSpec(num_sc...]
  transfers between devices with their start and end apart: 6 -> 38, of which waited for: 6 -> 12; matrix products, arithmetic and copies ran while one was open for 7% -> 10% of each run, Pallas kernels for 0% -> 14%
where the time goes in v1:
time: 242 us; the launch traced here: 241 us
  waiting for transfers between devices  79.9 us (33%)
  starting transfers between devices  77.1 us (32%)
  Pallas kernels  36.3 us (15%)
  other arithmetic  18 us (7%)
  local copies, waits for them, and re-layouts  14.1 us (6%)
  matrix products  13.4 us (6%)
  between operations  2.52 us (1%)
    all_to_all x1, waiting for transfers between devices, sum_over_all(): lax.all_to_all(kept.reshape(16, piece, BLK), 'row', 0, 0, tiled=True)  24.2 us
    ppermute x2, waiting for transfers between devices, sweep(): behind = lax.ppermute(behind, 'row', row_ring(over, 3))  17.9 us
    pallas_call x2, Pallas kernels, near_product(): pl.pallas_call(near_kernel, grid_spec=pltpu.PrefetchScalarGridSpec(num_sc...  16.1 us
    ppermute x2, starting transfers between devices, sweep(): top = lax.ppermute(top, 'row', row_ring(over, 1))  14.3 us
    all_to_all x1, waiting for transfers between devices, sum_over_all(): half = lax.all_to_all(wide, 'row', 0, 0, tiled=True).reshape(rows // 2, BLK)  14.1 us
    ppermute x6, waiting for transfers between devices, sweep(): lax.ppermute(pick(s), 'row', row_ring(across, s))  11.8 us
    unnamed x53, local copies, waits for them, and re-layouts  9.69 us
    pallas_call x2, Pallas kernels, far_product(): pl.pallas_call(far_kernel, grid_spec=pltpu.PrefetchScalarGridSpec(num_sca...  9.24 us
  transfers between devices with their start and end apart: 38, of which 12 were waited for; matrix products, arithmetic and copies ran while one was open for 10% of the time, Pallas kernels for 14%

profile of v1, /device:TPU:1, one launch (start us, length us, event | category | flops | bytes accessed | tf_op | source)
XLA Modules:
  0.0 241.1 jit_solution(2285590987906849388)
XLA Ops:
  0.7 1.4 compare_reduce_fusion.1
  2.7 1.8 convolution_multiply_fusion.refs_0_
  4.5 3.4 %collective-permute-start.10 = (f32[128,512]{1,0:T(8,128)S(1)}, f32[128,512]{1,0:T(8,128)S(1)}, u32[]{:S(2)}, u32[]{:S(2)}) collective-permute-start(f32[128,512]{1,0:T(8,128)S(1)} %convolution_multiply_fusion.refs_0_), channel_id=1, source_target_pairs={{0,6},{1,7},{2,0},{3,1},{4,2},{5,3},{6,4},{7,5},{8,14},{9,15},{10,... | collective-permute-start | bytes 786440 | tf_op jit(solution)/shard_map/ppermute | solution.py:133
  9.0 1.3 compare_reduce_fusion
  10.9 2.2 fusion.11
  14.0 1.6 collective-permute-start
  17.5 8.7 %flip.1 = (bf16[2048,1024]{1,0:T(8,128)(2,1)S(1)}, bf16[2048,1024]{1,0:T(8,128)(2,1)}) custom-call(f32[1024,2048]{1,0:T(8,128)} %block.1), custom_call_target="tpu_custom_call" | custom-call | tf_op jit(solution)/shard_map/flip/pallas_call | solution.py:55
  26.2 2.0 copy-done.1
  28.3 8.1 %collective-permute-start.3 = (f32[128,512]{1,0:T(8,128)S(1)}, f32[128,512]{1,0:T(8,128)}, u32[]{:S(2)}, u32[]{:S(2)}) collective-permute-start(f32[128,512]{1,0:T(8,128)S(1)} %convolution_multiply_fusion.refs_0_), channel_id=1, source_target_pairs={{0,0},{25,1},{34,2},{59,3},{68,4},{93,5},{102,6},{127,7},{8,8},{17... | collective-permute-start | bytes 786440 | tf_op jit(solution)/shard_map/ppermute | solution.py:261
  37.5 2.6 %collective-permute-done.3 = f32[128,512]{1,0:T(8,128)} collective-permute-done((f32[128,512]{1,0:T(8,128)S(1)}, f32[128,512]{1,0:T(8,128)}, u32[]{:S(2)}, u32[]{:S(2)}) %collective-permute-start.3) | collective-permute-done | bytes 262176 | tf_op jit(solution)/shard_map/ppermute | solution.py:261
  40.2 5.8 %collective-permute-start.8 = (f32[128,512]{1,0:T(8,128)S(1)}, f32[128,512]{1,0:T(8,128)}, u32[]{:S(2)}, u32[]{:S(2)}) collective-permute-start(f32[128,512]{1,0:T(8,128)S(1)} %convolution_subtract_fusion.refs_0_), channel_id=1, source_target_pairs={{0,0},{25,1},{34,2},{59,3},{68,4},{93,5},{102,6},{127,7},{8,8},{17... | collective-permute-start | bytes 786440 | tf_op jit(solution)/shard_map/ppermute | solution.py:262
  54.1 4.8 %far.2 = (bf16[1024,512]{1,0:T(8,128)(2,1)S(1)}, bf16[1024,512]{1,0:T(8,128)(2,1)S(1)}, f32[256,512]{1,0:T(8,128)}, f32[256,512]{1,0:T(8,128)S(1)}) custom-call(s32[4]{0:T(128)S(1)} %pad_add_fusion.rows, s32[8]{0:T(128)S(1)} %stack.161.places, f32[128,512]{1,0:T(8,128)S(1)} %convolution_multiply_fusion.refs_0_, ...), custom_call_target="tpu_custom_call" | custom-call | tf_op jit(solution)/shard_map/far/pallas_call | solution.py:83
  58.9 13.9 %collective-permute-start.16 = (f32[256,512]{1,0:T(8,128)}, f32[256,512]{1,0:T(8,128)S(1)}, u32[]{:S(2)}, u32[]{:S(2)}) collective-permute-start(f32[256,512]{1,0:T(8,128)} %get-tuple-element.56), channel_id=1, source_target_pairs={{0,32},{8,40},{16,48},{24,56},{32,64},{40,72},{48,80},{56,88},{64,... | collective-permute-start | bytes 1572872 | tf_op jit(solution)/shard_map/ppermute | solution.py:172
  72.8 4.2 %collective-permute-start.18 = (f32[256,512]{1,0:T(8,128)S(1)}, f32[256,512]{1,0:T(8,128)S(1)}, u32[]{:S(2)}, u32[]{:S(2)}) collective-permute-start(f32[256,512]{1,0:T(8,128)S(1)} %get-tuple-element.57), channel_id=1, source_target_pairs={{0,96},{8,104},{16,112},{24,120},{32,0},{40,8},{48,16},{56,24},{64... | collective-permute-start | bytes 1572872 | tf_op jit(solution)/shard_map/ppermute | solution.py:173
  77.0 4.5 %far.3 = (bf16[1024,512]{1,0:T(8,128)(2,1)S(1)}, bf16[1024,512]{1,0:T(8,128)(2,1)S(1)}, f32[256,512]{1,0:T(8,128)S(1)}, f32[256,512]{1,0:T(8,128)S(1)}) custom-call(s32[4]{0:T(128)S(1)} %pad_add_fusion.1.rows, s32[8]{0:T(128)S(1)} %stack.161.places, f32[128,512]{1,0:T(8,128)S(1)} %convolution_subtract_fusion.refs_0_, ...), custom_call_target="tpu_custom_call" | custom-call | tf_op jit(solution)/shard_map/far/pallas_call | solution.py:83
  81.8 2.4 collective-permute-start.25
  84.2 7.8 %near.2 = f32[3,512,512]{2,1,0:T(8,128)S(1)} custom-call(s32[12]{0:T(128)S(1)} %stack.147.rows, bf16[2048,1024]{1,0:T(8,128)(2,1)} %copy-done.1, bf16[2048,1024]{1,0:T(8,128)(2,1)} %copy-done.1, bf16[2048,1024]{1,0:T(8,128)(2,1)} %copy-done.1, bf16[2048,1024]{1,0:T(8,128)(2,1)} %copy-done.1, ...), custom_call_target="tpu_custom_call" | custom-call | tf_op jit(solution)/shard_map/near/pallas_call | solution.py:108
  92.0 8.3 %near.3 = f32[3,512,512]{2,1,0:T(8,128)S(1)} custom-call(s32[12]{0:T(128)S(1)} %stack.174.rows, bf16[2048,1024]{1,0:T(8,128)(2,1)} %copy-done.1, bf16[2048,1024]{1,0:T(8,128)(2,1)} %copy-done.1, bf16[2048,1024]{1,0:T(8,128)(2,1)} %copy-done.1, bf16[2048,1024]{1,0:T(8,128)(2,1)} %copy-done.1, ...), custom_call_target="tpu_custom_call" | custom-call | tf_op jit(solution)/shard_map/near/pallas_call | solution.py:108
  100.8 1.4 pad_maximum_fusion.1
  102.2 1.4 collective-permute-start.19
  107.0 1.5 collective-permute-start.24
  108.5 17.9 %collective-permute-done.19 = f32[512,512]{1,0:T(8,128)} collective-permute-done((f32[512,512]{1,0:T(8,128)}, f32[512,512]{1,0:T(8,128)}, u32[]{:S(2)}, u32[]{:S(2)}) %collective-permute-start.19) | collective-permute-done | bytes 1048608 | tf_op jit(solution)/shard_map/ppermute | solution.py:178
  126.3 3.1 %collective-permute-done.17 = f32[512,512]{1,0:T(8,128)} collective-permute-done((f32[512,512]{1,0:T(8,128)}, f32[512,512]{1,0:T(8,128)}, u32[]{:S(2)}, u32[]{:S(2)}) %collective-permute-start.17) | collective-permute-done | bytes 1048608 | tf_op jit(solution)/shard_map/ppermute | solution.py:177
  129.4 2.2 fusion.1
  132.4 1.5 collective-permute-start.21
  133.9 1.2 collective-permute-start.22
  135.1 2.2 fusion
  138.6 2.4 collective-permute-done.20
  141.4 2.4 %collective-permute-done.21 = f32[128,512]{1,0:T(8,128)} collective-permute-done((f32[128,512]{1,0:T(8,128)}, f32[128,512]{1,0:T(8,128)}, u32[]{:S(2)}, u32[]{:S(2)}) %collective-permute-start.21) | collective-permute-done | bytes 262176 | tf_op jit(solution)/shard_map/ppermute | solution.py:182
  143.9 2.3 collective-permute-done.22
  146.1 1.2 bitcast_add_fusion.2
  147.3 4.6 %collective-permute-done.27 = f32[128,512]{1,0:T(8,128)} collective-permute-done((f32[128,512]{1,0:T(8,128)}, f32[128,512]{1,0:T(8,128)}, u32[]{:S(2)}, u32[]{:S(2)}) %collective-permute-start.27) | collective-permute-done | bytes 262176 | tf_op jit(solution)/shard_map/ppermute | solution.py:182
  152.0 1.2 bitcast_add_fusion.1
  153.9 2.9 %fusion.6 = f32[1024,1024]{1,0:T(8,128)S(1)} fusion(f32[128,512]{1,0:T(8,128)} %collective-permute-done.8, f32[128,512]{1,0:T(8,128)} %collective-permute-done.3, f32[128,512]{1,0:T(8,128)S(1)} %bitcast_add_fusion.1, f32[128,512]{1,0:T(8,128)S(1)} %bitcast_add_fusion.2), kind=kOutput, calls=%fused_computation.26 | convolution fusion | flops 805568512 | bytes 5242880 | tf_op jit(solution)/shard_map/dot_general | solution.py:23
  158.3 2.7 %collective-permute-start.30 = (f32[2304,128]{1,0:T(8,128)}, f32[2304,128]{1,0:T(8,128)}, u32[]{:S(2)}, u32[]{:S(2)}) collective-permute-start(f32[2304,128]{1,0:T(8,128)} %dynamic-slice_bitcast_fusion), channel_id=1, source_target_pairs={{0,1},{1,0},{2,3},{3,2},{4,5},{5,4},{6,7},{7,6},{8,9},{9,8},{10,11... | collective-permute-start | bytes 3538952 | tf_op jit(solution)/shard_map/ppermute | solution.py:190
  161.1 2.8 %collective-permute-done.30 = f32[2304,128]{1,0:T(8,128)} collective-permute-done((f32[2304,128]{1,0:T(8,128)}, f32[2304,128]{1,0:T(8,128)}, u32[]{:S(2)}, u32[]{:S(2)}) %collective-permute-start.30) | collective-permute-done | bytes 1179680 | tf_op jit(solution)/shard_map/ppermute | solution.py:190
  163.9 2.4 bitcast_add_fusion
  166.3 5.6 %all-to-all-start = ((f32[16,144,128]{2,1,0:T(8,128)}), f32[16,144,128]{2,1,0:T(8,128)S(1)}, u32[]{:S(2)}, u32[]{:S(2)}) async-start(f32[16,144,128]{2,1,0:T(8,128)} %bitcast.63), calls=%async_computation | async-start | bytes 2359296 | tf_op jit(solution)/shard_map/all_to_all | solution.py:192
  172.0 4.5 %collective-permute-start.34 = (f32[128,1024]{1,0:T(8,128)S(1)}, f32[128,1024]{1,0:T(8,128)S(1)}, u32[]{:S(2)}, u32[]{:S(2)}) collective-permute-start(f32[128,1024]{1,0:T(8,128)S(1)} %pad_maximum_fusion.4), channel_id=1, source_target_pairs={{0,0},{1,25},{2,34},{3,59},{4,68},{5,93},{6,102},{7,127},{8,8},{9,... | collective-permute-start | bytes 1572872 | tf_op jit(solution)/shard_map/ppermute | solution.py:276
  176.4 24.2 %all-to-all-done = f32[16,144,128]{2,1,0:T(8,128)S(1)} async-done(((f32[16,144,128]{2,1,0:T(8,128)}), f32[16,144,128]{2,1,0:T(8,128)S(1)}, u32[]{:S(2)}, u32[]{:S(2)}) %all-to-all-start) | async-done | bytes 1179680 | tf_op jit(solution)/shard_map/all_to_all | solution.py:192
  201.3 2.2 collective-permute-start.33
  203.5 2.5 %collective-permute-done.31 = f32[144,128]{1,0:T(8,128)S(1)} collective-permute-done((f32[144,128]{1,0:T(8,128)S(1)}, f32[144,128]{1,0:T(8,128)S(1)}, u32[]{:S(2)}, u32[]{:S(2)}) %collective-permute-start.31) | collective-permute-done | bytes 73760 | tf_op jit(solution)/shard_map/ppermute | solution.py:193
  206.9 1.2 broadcast_in_dim.2
  208.1 6.9 %all-to-all-start.1 = ((f32[16,144,128]{2,1,0:T(8,128)}), f32[16,144,128]{2,1,0:T(8,128)S(1)}, u32[]{:S(2)}, u32[]{:S(2)}) async-start(f32[16,144,128]{2,1,0:T(8,128)} %broadcast_in_dim.2), calls=%async_computation.1 | async-start | bytes 2359296 | tf_op jit(solution)/shard_map/all_to_all | solution.py:196
  215.0 2.6 %fusion.12.square_one = f32[512,512]{1,0:T(8,128)S(1)} fusion(f32[512,512]{1,0:T(8,128)} %param.10), kind=kOutput, calls=%fused_computation.60 | convolution fusion | flops 805306368 | bytes 2097152 | tf_op jit(solution)/shard_map/dot_general | solution.py:23
  217.6 14.1 %all-to-all-done.1 = f32[16,144,128]{2,1,0:T(8,128)S(1)} async-done(((f32[16,144,128]{2,1,0:T(8,128)}), f32[16,144,128]{2,1,0:T(8,128)S(1)}, u32[]{:S(2)}, u32[]{:S(2)}) %all-to-all-start.1) | async-done | bytes 1179680 | tf_op jit(solution)/shard_map/all_to_all | solution.py:196
  231.7 3.3 %collective-permute-start.35 = (f32[2304,128]{1,0:T(8,128)S(1)}, f32[2304,128]{1,0:T(8,128)S(1)}, u32[]{:S(2)}, u32[]{:S(2)}) collective-permute-start(f32[2304,128]{1,0:T(8,128)S(1)} %bitcast.114), channel_id=1, source_target_pairs={{0,1},{1,0},{2,3},{3,2},{4,5},{5,4},{6,7},{7,6},{8,9},{9,8},{10,11... | collective-permute-start | bytes 3538952 | tf_op jit(solution)/shard_map/ppermute | solution.py:197
  238.9 2.2 finish.1
  (125 shorter events, 27.3 us)
Async XLA Ops:
  0.6 10.3 %copy-start = (f32[512,512]{1,0:T(8,128)S(1)}, f32[512,512]{1,0:T(8,128)}, u32[]{:S(2)}) copy-start(f32[512,512]{1,0:T(8,128)} %param.13) | copy-start | bytes 3145732
  2.7 10.5 %copy-start.20 = (f32[128,512]{1,0:T(8,128)S(1)}, f32[128,512]{1,0:T(8,128)}, u32[]{:S(2)}) copy-start(f32[128,512]{1,0:T(8,128)} %param.12) | copy-start | bytes 786436
  4.5 12.3 %collective-permute-start.10 = (f32[128,512]{1,0:T(8,128)S(1)}, f32[128,512]{1,0:T(8,128)S(1)}, u32[]{:S(2)}, u32[]{:S(2)}) collective-permute-start(f32[128,512]{1,0:T(8,128)S(1)} %convolution_multiply_fusion.refs_0_), channel_id=1, source_target_pairs={{0,6},{1,7},{2,0},{3,1},{4,2},{5,3},{6,4},{7,5},{8,14},{9,15},{10,... | collective-permute-start | bytes 786440 | tf_op jit(solution)/shard_map/ppermute | solution.py:133
  7.8 20.4 %collective-permute-start.11 = (f32[128,512]{1,0:T(8,128)S(1)}, f32[128,512]{1,0:T(8,128)S(1)}, u32[]{:S(2)}, u32[]{:S(2)}) collective-permute-start(f32[128,512]{1,0:T(8,128)S(1)} %convolution_multiply_fusion.refs_0_), channel_id=1, source_target_pairs={{0,4},{1,5},{2,6},{3,7},{4,0},{5,1},{6,2},{7,3},{8,12},{9,13},{10,... | collective-permute-start | bytes 786440 | tf_op jit(solution)/shard_map/ppermute | solution.py:133
  8.4 28.1 %collective-permute-start.9 = (f32[128,512]{1,0:T(8,128)S(1)}, f32[128,512]{1,0:T(8,128)S(1)}, u32[]{:S(2)}, u32[]{:S(2)}) collective-permute-start(f32[128,512]{1,0:T(8,128)S(1)} %convolution_multiply_fusion.refs_0_), channel_id=1, source_target_pairs={{0,2},{1,3},{2,4},{3,5},{4,6},{5,7},{6,0},{7,1},{8,10},{9,11},{10,... | collective-permute-start | bytes 786440 | tf_op jit(solution)/shard_map/ppermute | solution.py:133
  13.2 3.6 %copy-start.12 = (f32[512,512]{1,0:T(8,128)}, f32[512,512]{1,0:T(8,128)S(1)}, u32[]{:S(2)}) copy-start(f32[512,512]{1,0:T(8,128)S(1)} %fusion.11) | copy-start | bytes 3145732
  14.0 22.5 %collective-permute-start = (f32[128,512]{1,0:T(8,128)S(1)}, f32[128,512]{1,0:T(8,128)S(1)}, u32[]{:S(2)}, u32[]{:S(2)}) collective-permute-start(f32[128,512]{1,0:T(8,128)S(1)} %convolution_subtract_fusion.refs_0_), channel_id=1, source_target_pairs={{0,2},{1,3},{2,4},{3,5},{4,6},{5,7},{6,0},{7,1},{8,10},{9,11},{10,... | collective-permute-start | bytes 786440 | tf_op jit(solution)/shard_map/ppermute | solution.py:133
  15.6 21.4 %collective-permute-start.1 = (f32[128,512]{1,0:T(8,128)S(1)}, f32[128,512]{1,0:T(8,128)S(1)}, u32[]{:S(2)}, u32[]{:S(2)}) collective-permute-start(f32[128,512]{1,0:T(8,128)S(1)} %convolution_subtract_fusion.refs_0_), channel_id=1, source_target_pairs={{0,6},{1,7},{2,0},{3,1},{4,2},{5,3},{6,4},{7,5},{8,14},{9,15},{10,... | collective-permute-start | bytes 786440 | tf_op jit(solution)/shard_map/ppermute | solution.py:133
  16.8 20.3 %collective-permute-start.2 = (f32[128,512]{1,0:T(8,128)S(1)}, f32[128,512]{1,0:T(8,128)S(1)}, u32[]{:S(2)}, u32[]{:S(2)}) collective-permute-start(f32[128,512]{1,0:T(8,128)S(1)} %convolution_subtract_fusion.refs_0_), channel_id=1, source_target_pairs={{0,4},{1,5},{2,6},{3,7},{4,0},{5,1},{6,2},{7,3},{8,12},{9,13},{10,... | collective-permute-start | bytes 786440 | tf_op jit(solution)/shard_map/ppermute | solution.py:133
  28.3 11.9 %collective-permute-start.3 = (f32[128,512]{1,0:T(8,128)S(1)}, f32[128,512]{1,0:T(8,128)}, u32[]{:S(2)}, u32[]{:S(2)}) collective-permute-start(f32[128,512]{1,0:T(8,128)S(1)} %convolution_multiply_fusion.refs_0_), channel_id=1, source_target_pairs={{0,0},{25,1},{34,2},{59,3},{68,4},{93,5},{102,6},{127,7},{8,8},{17... | collective-permute-start | bytes 786440 | tf_op jit(solution)/shard_map/ppermute | solution.py:261
  36.4 9.6 %collective-permute-start.12 = (f32[128,512]{1,0:T(8,128)S(1)}, f32[128,512]{1,0:T(8,128)S(1)}, u32[]{:S(2)}, u32[]{:S(2)}) collective-permute-start(f32[128,512]{1,0:T(8,128)S(1)} %convolution_multiply_fusion.refs_0_), channel_id=1, source_target_pairs={{0,1},{1,0},{2,3},{3,2},{4,5},{5,4},{6,7},{7,6},{8,9},{9,8},{10,11... | collective-permute-start | bytes 786440 | tf_op jit(solution)/shard_map/ppermute | solution.py:135
  36.5 10.2 %collective-permute-start.13 = (f32[128,512]{1,0:T(8,128)S(1)}, f32[128,512]{1,0:T(8,128)S(1)}, u32[]{:S(2)}, u32[]{:S(2)}) collective-permute-start(f32[128,512]{1,0:T(8,128)S(1)} %collective-permute-done.9.refs_1_), channel_id=1, source_target_pairs={{0,1},{1,0},{2,3},{3,2},{4,5},{5,4},{6,7},{7,6},{8,9},{9,8},{10,11... | collective-permute-start | bytes 786440 | tf_op jit(solution)/shard_map/ppermute | solution.py:135
  37.0 10.9 %collective-permute-start.14 = (f32[128,512]{1,0:T(8,128)S(1)}, f32[128,512]{1,0:T(8,128)S(1)}, u32[]{:S(2)}, u32[]{:S(2)}) collective-permute-start(f32[128,512]{1,0:T(8,128)S(1)} %collective-permute-done.10.refs_2_), channel_id=1, source_target_pairs={{0,1},{1,0},{2,3},{3,2},{4,5},{5,4},{6,7},{7,6},{8,9},{9,8},{10,11... | collective-permute-start | bytes 786440 | tf_op jit(solution)/shard_map/ppermute | solution.py:135
  37.1 11.5 %collective-permute-start.15 = (f32[128,512]{1,0:T(8,128)S(1)}, f32[128,512]{1,0:T(8,128)S(1)}, u32[]{:S(2)}, u32[]{:S(2)}) collective-permute-start(f32[128,512]{1,0:T(8,128)S(1)} %collective-permute-done.11.refs_3_), channel_id=1, source_target_pairs={{0,1},{1,0},{2,3},{3,2},{4,5},{5,4},{6,7},{7,6},{8,9},{9,8},{10,11... | collective-permute-start | bytes 786440 | tf_op jit(solution)/shard_map/ppermute | solution.py:135
  40.2 18.7 %collective-permute-start.8 = (f32[128,512]{1,0:T(8,128)S(1)}, f32[128,512]{1,0:T(8,128)}, u32[]{:S(2)}, u32[]{:S(2)}) collective-permute-start(f32[128,512]{1,0:T(8,128)S(1)} %convolution_subtract_fusion.refs_0_), channel_id=1, source_target_pairs={{0,0},{25,1},{34,2},{59,3},{68,4},{93,5},{102,6},{127,7},{8,8},{17... | collective-permute-start | bytes 786440 | tf_op jit(solution)/shard_map/ppermute | solution.py:262
  46.7 26.1 %collective-permute-start.4 = (f32[128,512]{1,0:T(8,128)S(1)}, f32[128,512]{1,0:T(8,128)S(1)}, u32[]{:S(2)}, u32[]{:S(2)}) collective-permute-start(f32[128,512]{1,0:T(8,128)S(1)} %convolution_subtract_fusion.refs_0_), channel_id=1, source_target_pairs={{0,1},{1,0},{2,3},{3,2},{4,5},{5,4},{6,7},{7,6},{8,9},{9,8},{10,11... | collective-permute-start | bytes 786440 | tf_op jit(solution)/shard_map/ppermute | solution.py:135
  47.4 29.6 %collective-permute-start.5 = (f32[128,512]{1,0:T(8,128)S(1)}, f32[128,512]{1,0:T(8,128)}, u32[]{:S(2)}, u32[]{:S(2)}) collective-permute-start(f32[128,512]{1,0:T(8,128)S(1)} %collective-permute-done.refs_1_), channel_id=1, source_target_pairs={{0,1},{1,0},{2,3},{3,2},{4,5},{5,4},{6,7},{7,6},{8,9},{9,8},{10,11... | collective-permute-start | bytes 786440 | tf_op jit(solution)/shard_map/ppermute | solution.py:135
  48.6 28.4 %collective-permute-start.6 = (f32[128,512]{1,0:T(8,128)S(1)}, f32[128,512]{1,0:T(8,128)}, u32[]{:S(2)}, u32[]{:S(2)}) collective-permute-start(f32[128,512]{1,0:T(8,128)S(1)} %collective-permute-done.1.refs_2_), channel_id=1, source_target_pairs={{0,1},{1,0},{2,3},{3,2},{4,5},{5,4},{6,7},{7,6},{8,9},{9,8},{10,11... | collective-permute-start | bytes 786440 | tf_op jit(solution)/shard_map/ppermute | solution.py:135
  49.4 27.7 %collective-permute-start.7 = (f32[128,512]{1,0:T(8,128)S(1)}, f32[128,512]{1,0:T(8,128)}, u32[]{:S(2)}, u32[]{:S(2)}) collective-permute-start(f32[128,512]{1,0:T(8,128)S(1)} %collective-permute-done.2.refs_3_), channel_id=1, source_target_pairs={{0,1},{1,0},{2,3},{3,2},{4,5},{5,4},{6,7},{7,6},{8,9},{9,8},{10,11... | collective-permute-start | bytes 786440 | tf_op jit(solution)/shard_map/ppermute | solution.py:135
  58.9 41.6 %collective-permute-start.16 = (f32[256,512]{1,0:T(8,128)}, f32[256,512]{1,0:T(8,128)S(1)}, u32[]{:S(2)}, u32[]{:S(2)}) collective-permute-start(f32[256,512]{1,0:T(8,128)} %get-tuple-element.56), channel_id=1, source_target_pairs={{0,32},{8,40},{16,48},{24,56},{32,64},{40,72},{48,80},{56,88},{64,... | collective-permute-start | bytes 1572872 | tf_op jit(solution)/shard_map/ppermute | solution.py:172
  72.8 27.7 %collective-permute-start.18 = (f32[256,512]{1,0:T(8,128)S(1)}, f32[256,512]{1,0:T(8,128)S(1)}, u32[]{:S(2)}, u32[]{:S(2)}) collective-permute-start(f32[256,512]{1,0:T(8,128)S(1)} %get-tuple-element.57), channel_id=1, source_target_pairs={{0,96},{8,104},{16,112},{24,120},{32,0},{40,8},{48,16},{56,24},{64... | collective-permute-start | bytes 1572872 | tf_op jit(solution)/shard_map/ppermute | solution.py:173
  81.5 23.2 %collective-permute-start.23 = (f32[256,512]{1,0:T(8,128)S(1)}, f32[256,512]{1,0:T(8,128)S(1)}, u32[]{:S(2)}, u32[]{:S(2)}) collective-permute-start(f32[256,512]{1,0:T(8,128)S(1)} %get-tuple-element.68), channel_id=1, source_target_pairs={{0,8},{8,16},{16,24},{24,0},{32,40},{40,48},{48,56},{56,32},{64,72... | collective-permute-start | bytes 1572872 | tf_op jit(solution)/shard_map/ppermute | solution.py:172
  81.8 22.9 %collective-permute-start.25 = (f32[256,512]{1,0:T(8,128)S(1)}, f32[256,512]{1,0:T(8,128)S(1)}, u32[]{:S(2)}, u32[]{:S(2)}) collective-permute-start(f32[256,512]{1,0:T(8,128)S(1)} %get-tuple-element.69), channel_id=1, source_target_pairs={{0,24},{8,0},{16,8},{24,16},{32,56},{40,32},{48,40},{56,48},{64,88... | collective-permute-start | bytes 1572872 | tf_op jit(solution)/shard_map/ppermute | solution.py:173
  92.0 8.5 %copy-start.3 = (f32[3,512,512]{2,1,0:T(8,128)}, f32[3,512,512]{2,1,0:T(8,128)S(1)}, u32[]{:S(2)}) copy-start(f32[3,512,512]{2,1,0:T(8,128)S(1)} %near.2) | copy-start | bytes 9437188
  100.3 4.4 %copy-start.2 = (f32[3,512,512]{2,1,0:T(8,128)}, f32[3,512,512]{2,1,0:T(8,128)S(1)}, u32[]{:S(2)}) copy-start(f32[3,512,512]{2,1,0:T(8,128)S(1)} %near.3) | copy-start | bytes 9437188
  102.2 24.1 %collective-permute-start.19 = (f32[512,512]{1,0:T(8,128)}, f32[512,512]{1,0:T(8,128)}, u32[]{:S(2)}, u32[]{:S(2)}) collective-permute-start(f32[512,512]{1,0:T(8,128)} %pad_maximum_fusion.1), channel_id=1, source_target_pairs={{0,96},{8,104},{16,112},{24,120},{32,0},{40,8},{48,16},{56,24},{64... | collective-permute-start | bytes 3145736 | tf_op jit(solution)/shard_map/ppermute | solution.py:178
  104.6 24.8 %collective-permute-start.17 = (f32[512,512]{1,0:T(8,128)}, f32[512,512]{1,0:T(8,128)}, u32[]{:S(2)}, u32[]{:S(2)}) collective-permute-start(f32[512,512]{1,0:T(8,128)} %pad_maximum_fusion), channel_id=1, source_target_pairs={{0,32},{8,40},{16,48},{24,56},{32,64},{40,72},{48,80},{56,88},{64,... | collective-permute-start | bytes 3145736 | tf_op jit(solution)/shard_map/ppermute | solution.py:177
  106.0 29.1 %collective-permute-start.26 = (f32[512,512]{1,0:T(8,128)}, f32[512,512]{1,0:T(8,128)}, u32[]{:S(2)}, u32[]{:S(2)}) collective-permute-start(f32[512,512]{1,0:T(8,128)} %pad_maximum_fusion.3), channel_id=1, source_target_pairs={{0,24},{8,0},{16,8},{24,16},{32,56},{40,32},{48,40},{56,48},{64,88... | collective-permute-start | bytes 3145736 | tf_op jit(solution)/shard_map/ppermute | solution.py:178
  107.0 28.1 %collective-permute-start.24 = (f32[512,512]{1,0:T(8,128)}, f32[512,512]{1,0:T(8,128)}, u32[]{:S(2)}, u32[]{:S(2)}) collective-permute-start(f32[512,512]{1,0:T(8,128)} %pad_maximum_fusion.2), channel_id=1, source_target_pairs={{0,8},{8,16},{16,24},{24,0},{32,40},{40,48},{48,56},{56,32},{64,72... | collective-permute-start | bytes 3145736 | tf_op jit(solution)/shard_map/ppermute | solution.py:177
  132.4 8.7 %collective-permute-start.20 = (f32[128,512]{1,0:T(8,128)S(1)}, f32[128,512]{1,0:T(8,128)}, u32[]{:S(2)}, u32[]{:S(2)}) collective-permute-start(f32[128,512]{1,0:T(8,128)S(1)} %get-tuple-element.85), channel_id=1, source_target_pairs={{0,8},{8,16},{16,24},{24,0},{32,40},{40,48},{48,56},{56,32},{64,72... | collective-permute-start | bytes 786440 | tf_op jit(solution)/shard_map/ppermute | solution.py:182
  132.4 11.5 %collective-permute-start.21 = (f32[128,512]{1,0:T(8,128)}, f32[128,512]{1,0:T(8,128)}, u32[]{:S(2)}, u32[]{:S(2)}) collective-permute-start(f32[128,512]{1,0:T(8,128)} %get-tuple-element.83), channel_id=1, source_target_pairs={{0,16},{8,24},{16,0},{24,8},{32,48},{40,56},{48,32},{56,40},{64,80... | collective-permute-start | bytes 786440 | tf_op jit(solution)/shard_map/ppermute | solution.py:182
  133.9 12.3 %collective-permute-start.22 = (f32[128,512]{1,0:T(8,128)S(1)}, f32[128,512]{1,0:T(8,128)}, u32[]{:S(2)}, u32[]{:S(2)}) collective-permute-start(f32[128,512]{1,0:T(8,128)S(1)} %get-tuple-element.84), channel_id=1, source_target_pairs={{0,24},{8,0},{16,8},{24,16},{32,56},{40,32},{48,40},{56,48},{64,88... | collective-permute-start | bytes 786440 | tf_op jit(solution)/shard_map/ppermute | solution.py:182
  138.2 13.8 %collective-permute-start.27 = (f32[128,512]{1,0:T(8,128)}, f32[128,512]{1,0:T(8,128)}, u32[]{:S(2)}, u32[]{:S(2)}) collective-permute-start(f32[128,512]{1,0:T(8,128)} %get-tuple-element.88), channel_id=1, source_target_pairs={{0,32},{8,40},{16,48},{24,56},{32,64},{40,72},{48,80},{56,88},{64,... | collective-permute-start | bytes 786440 | tf_op jit(solution)/shard_map/ppermute | solution.py:182
  138.2 13.8 %collective-permute-start.28 = (f32[128,512]{1,0:T(8,128)}, f32[128,512]{1,0:T(8,128)}, u32[]{:S(2)}, u32[]{:S(2)}) collective-permute-start(f32[128,512]{1,0:T(8,128)} %get-tuple-element.86), channel_id=1, source_target_pairs={{0,64},{8,72},{16,80},{24,88},{32,96},{40,104},{48,112},{56,120},{... | collective-permute-start | bytes 786440 | tf_op jit(solution)/shard_map/ppermute | solution.py:182
  141.0 10.9 %collective-permute-start.29 = (f32[128,512]{1,0:T(8,128)}, f32[128,512]{1,0:T(8,128)}, u32[]{:S(2)}, u32[]{:S(2)}) collective-permute-start(f32[128,512]{1,0:T(8,128)} %get-tuple-element.87), channel_id=1, source_target_pairs={{0,96},{8,104},{16,112},{24,120},{32,0},{40,8},{48,16},{56,24},{64... | collective-permute-start | bytes 786440 | tf_op jit(solution)/shard_map/ppermute | solution.py:182
  147.3 5.8 %copy-start.14 = (f32[128,512]{1,0:T(8,128)}, f32[128,512]{1,0:T(8,128)S(1)}, u32[]{:S(2)}) copy-start(f32[128,512]{1,0:T(8,128)S(1)} %bitcast_add_fusion.2) | copy-start | bytes 786436
  158.3 5.6 %collective-permute-start.30 = (f32[2304,128]{1,0:T(8,128)}, f32[2304,128]{1,0:T(8,128)}, u32[]{:S(2)}, u32[]{:S(2)}) collective-permute-start(f32[2304,128]{1,0:T(8,128)} %dynamic-slice_bitcast_fusion), channel_id=1, source_target_pairs={{0,1},{1,0},{2,3},{3,2},{4,5},{5,4},{6,7},{7,6},{8,9},{9,8},{10,11... | collective-permute-start | bytes 3538952 | tf_op jit(solution)/shard_map/ppermute | solution.py:190
  166.3 5.6 %copy-start.15 = (f32[128,512]{1,0:T(8,128)S(1)}, f32[128,512]{1,0:T(8,128)}, u32[]{:S(2)}) copy-start(f32[128,512]{1,0:T(8,128)} %copy-done.14) | copy-start | bytes 786436
  166.3 5.6 %copy-start.17 = (f32[128,512]{1,0:T(8,128)S(1)}, f32[128,512]{1,0:T(8,128)}, u32[]{:S(2)}) copy-start(f32[128,512]{1,0:T(8,128)} %copy-done.16) | copy-start | bytes 786436
  166.3 34.4 %all-to-all-start = ((f32[16,144,128]{2,1,0:T(8,128)}), f32[16,144,128]{2,1,0:T(8,128)S(1)}, u32[]{:S(2)}, u32[]{:S(2)}) async-start(f32[16,144,128]{2,1,0:T(8,128)} %bitcast.63), calls=%async_computation | async-start | bytes 2359296 | tf_op jit(solution)/shard_map/all_to_all | solution.py:192
  172.0 34.9 %collective-permute-start.34 = (f32[128,1024]{1,0:T(8,128)S(1)}, f32[128,1024]{1,0:T(8,128)S(1)}, u32[]{:S(2)}, u32[]{:S(2)}) collective-permute-start(f32[128,1024]{1,0:T(8,128)S(1)} %pad_maximum_fusion.4), channel_id=1, source_target_pairs={{0,0},{1,25},{2,34},{3,59},{4,68},{5,93},{6,102},{7,127},{8,8},{9,... | collective-permute-start | bytes 1572872 | tf_op jit(solution)/shard_map/ppermute | solution.py:276
  200.7 5.3 %collective-permute-start.31 = (f32[144,128]{1,0:T(8,128)S(1)}, f32[144,128]{1,0:T(8,128)S(1)}, u32[]{:S(2)}, u32[]{:S(2)}) collective-permute-start(f32[144,128]{1,0:T(8,128)S(1)} %reduce_sum.9), channel_id=1, source_target_pairs={{0,2},{1,3},{2,4},{3,5},{4,6},{5,7},{6,0},{7,1},{8,10},{9,11},{10,... | collective-permute-start | bytes 221192 | tf_op jit(solution)/shard_map/ppermute | solution.py:193
  200.8 5.2 %collective-permute-start.32 = (f32[144,128]{1,0:T(8,128)S(1)}, f32[144,128]{1,0:T(8,128)S(1)}, u32[]{:S(2)}, u32[]{:S(2)}) collective-permute-start(f32[144,128]{1,0:T(8,128)S(1)} %reduce_sum.9), channel_id=1, source_target_pairs={{0,4},{1,5},{2,6},{3,7},{4,0},{5,1},{6,2},{7,3},{8,12},{9,13},{10,... | collective-permute-start | bytes 221192 | tf_op jit(solution)/shard_map/ppermute | solution.py:193
  201.3 5.6 %collective-permute-start.33 = (f32[144,128]{1,0:T(8,128)S(1)}, f32[144,128]{1,0:T(8,128)S(1)}, u32[]{:S(2)}, u32[]{:S(2)}) collective-permute-start(f32[144,128]{1,0:T(8,128)S(1)} %reduce_sum.9), channel_id=1, source_target_pairs={{0,6},{1,7},{2,0},{3,1},{4,2},{5,3},{6,4},{7,5},{8,14},{9,15},{10,... | collective-permute-start | bytes 221192 | tf_op jit(solution)/shard_map/ppermute | solution.py:193
  206.9 8.1 %copy-start.18 = (f32[128,1024]{1,0:T(8,128)}, f32[128,1024]{1,0:T(8,128)S(1)}, u32[]{:S(2)}) copy-start(f32[128,1024]{1,0:T(8,128)S(1)} %collective-permute-done.34) | copy-start | bytes 1572868
  208.1 23.6 %all-to-all-start.1 = ((f32[16,144,128]{2,1,0:T(8,128)}), f32[16,144,128]{2,1,0:T(8,128)S(1)}, u32[]{:S(2)}, u32[]{:S(2)}) async-start(f32[16,144,128]{2,1,0:T(8,128)} %broadcast_in_dim.2), calls=%async_computation.1 | async-start | bytes 2359296 | tf_op jit(solution)/shard_map/all_to_all | solution.py:196
  231.7 4.3 %copy-start.13 = (f32[512,512]{1,0:T(8,128)S(1)}, f32[512,512]{1,0:T(8,128)}, u32[]{:S(2)}) copy-start(f32[512,512]{1,0:T(8,128)} %copy-done.12) | copy-start | bytes 3145732
  231.7 7.2 %collective-permute-start.35 = (f32[2304,128]{1,0:T(8,128)S(1)}, f32[2304,128]{1,0:T(8,128)S(1)}, u32[]{:S(2)}, u32[]{:S(2)}) collective-permute-start(f32[2304,128]{1,0:T(8,128)S(1)} %bitcast.114), channel_id=1, source_target_pairs={{0,1},{1,0},{2,3},{3,2},{4,5},{5,4},{6,7},{7,6},{8,9},{9,8},{10,11... | collective-permute-start | bytes 3538952 | tf_op jit(solution)/shard_map/ppermute | solution.py:197
  (11 other events, 10.4 us)

commit v2 on v0

v2 whole, which is shorter than its diff:
```python
import functools

import jax
import jax.numpy as jnp
from jax import lax
from jax.experimental import pallas as pl
from jax.experimental.pallas import tpu as pltpu
from jax.sharding import PartitionSpec as P

BLK = 128
W = 512
BOTH = ("row", "col")
SWAP = [(i, i ^ 1) for i in range(8)]
F32 = jnp.float32
BF16 = jnp.bfloat16


def product(left, right):
    return jnp.dot(left, right, precision=lax.Precision.HIGH, preferred_element_type=F32)


def product_t(left, right):
    return lax.dot_general(
        left, right, (((0,), (0,)), ((), ())), precision=lax.Precision.HIGH, preferred_element_type=F32
    )


def block_flag(structure, block):
    return jnp.any(structure == block).astype(F32)


def params(mib):
    return pltpu.CompilerParams(vmem_limit_bytes=mib << 20)


def pinned(value, space=pltpu.HBM):
    return pltpu.with_memory_space_constraint(value, space)


def halves(value):
    high = value.astype(BF16)
    return high, (value - high.astype(F32)).astype(BF16)


def three(left_high, left_low, right_high, right_low):
    dot = functools.partial(jnp.dot, preferred_element_type=F32)
    return dot(left_high, right_high) + (dot(left_low, right_high) + dot(left_high, right_low))


def flip_kernel(blocks, left, right, high, low):
    for i, block in enumerate((left, right)):
        high[0, i], low[0, i] = halves(block[...].T)


def flipped(trailing, blocks):
    rows = trailing.shape[0]
    out = pltpu.HBM((4, 4, BLK, rows), BF16)
    spec = pl.BlockSpec((1, 2, BLK, rows), lambda i, b: (i // 2, i % 2, 0, 0))
    return pl.pallas_call(
        flip_kernel,
        grid_spec=pltpu.PrefetchScalarGridSpec(
            num_scalar_prefetch=1,
            grid=(8,),
            in_specs=[
                pl.BlockSpec((rows, BLK), lambda i, b: (0, b[2 * i])),
                pl.BlockSpec((rows, BLK), lambda i, b: (0, b[2 * i + 1])),
            ],
            out_specs=[spec, spec],
        ),
        out_shape=[out, out],
        compiler_params=params(12),
        name="flip",
    )(blocks, trailing, trailing)


def far_kernel(chunks, places, *refs):
    pieces, (flip_high, flip_low), (high, low, top, bottom) = refs[:8], refs[8:10], refs[10:]
    for i in range(8):
        at = pl.ds(pl.multiple_of(places[i] * BLK, BLK), BLK)
        high[at, :], low[at, :] = halves(pieces[i][...])
    out = chunk_product(flip_high, flip_low, high, low)
    top[...] = out[: 2 * BLK]
    bottom[...] = out[2 * BLK :]


def chunk_product(flip_high, flip_low, high, low):
    shape = (4 * BLK, flip_high.shape[-1])
    return three(flip_high[...].reshape(shape), flip_low[...].reshape(shape), high[...], low[...])


def near_kernel(chunks, flip_high, flip_low, high, low, *outs):
    for s in range(3):

        @pl.when(pl.program_id(0) == s)
        def _():
            outs[s][...] = chunk_product(flip_high, flip_low, high, low)


def flip_specs(over, count):
    if over == "z":
        return [pl.BlockSpec((1, 4, BLK, count), lambda i, c, *p: (c[i], 0, 0, 0))] * 2
    return [pl.BlockSpec((4, 1, BLK, count), lambda i, c, *p: (0, c[i], 0, 0))] * 2


def whole(shape):
    return pl.BlockSpec(shape, lambda i, *p: (0, 0))


def far_product(which, chunks, places, pieces, flip_high, flip_low):
    count = flip_high.shape[-1]
    return pl.pallas_call(
        far_kernel,
        grid_spec=pltpu.PrefetchScalarGridSpec(
            num_scalar_prefetch=2,
            grid=(1,),
            in_specs=[pl.BlockSpec((BLK, W), lambda i, *p: (0, which))] * 8 + flip_specs("zy"[which], count),
            out_specs=[whole((count, W))] * 2 + [whole((2 * BLK, W))] * 2,
        ),
        out_shape=[pltpu.HBM((count, W), BF16)] * 2 + [jax.ShapeDtypeStruct((2 * BLK, W), F32)] * 2,
        compiler_params=params(22),
        name="far",
    )(chunks, places, *pieces, pinned(flip_high), pinned(flip_low))


def near_product(which, chunks, panel_high, panel_low, flip_high, flip_low):
    count = flip_high.shape[-1]
    return pl.pallas_call(
        near_kernel,
        grid_spec=pltpu.PrefetchScalarGridSpec(
            num_scalar_prefetch=1,
            grid=(3,),
            in_specs=flip_specs("zy"[which], count) + [whole((count, W))] * 2,
            out_specs=[whole((4 * BLK, W))] * 3,
        ),
        out_shape=[jax.ShapeDtypeStruct((4 * BLK, W), F32)] * 3,
        compiler_params=params(22),
        name="near",
    )(chunks, pinned(flip_high), pinned(flip_low), pinned(panel_high), pinned(panel_low))


def join_kernel(ahead, behind, top, bottom, ahead_out, behind_out):
    ahead_out[...] = ahead[...] + top[...]
    behind_out[...] = behind[...] + bottom[...]


def join(ahead, behind, top, bottom):
    half = (2 * BLK, W)
    upper, lower = pl.BlockSpec(half, lambda i: (0, 0)), pl.BlockSpec(half, lambda i: (1, 0))
    return pl.pallas_call(
        join_kernel,
        grid=(1,),
        in_specs=[upper, lower, upper, upper],
        out_specs=[upper, lower],
        out_shape=[jax.ShapeDtypeStruct(ahead.shape, F32)] * 2,
        input_output_aliases={0: 0, 1: 1},
        compiler_params=params(10),
        name="join",
    )(ahead, behind, top, bottom)


def fold_kernel(place, own, one, other, *refs):
    outs, total = refs[:4], refs[4]
    total[...] = own[...] + (one[...] + other[...])
    for s, out in enumerate(outs):
        out[...] = total[pl.ds(pl.multiple_of((place[0] + s) % 4 * BLK, BLK), BLK), :]


def fold(place, *chunks):
    vmem = pl.BlockSpec(memory_space=pltpu.VMEM)
    return pl.pallas_call(
        fold_kernel,
        in_specs=[pl.BlockSpec(memory_space=pltpu.SMEM)] + [vmem] * 3,
        out_specs=[vmem] * 4,
        out_shape=[jax.ShapeDtypeStruct((BLK, W), F32)] * 4,
        scratch_shapes=[pltpu.VMEM((4 * BLK, W), F32)],
        compiler_params=params(10),
        name="fold",
    )(place.reshape(1).astype(jnp.int32), *chunks)


def col_ring(s):
    return [(i, (i + 2 * s) % 8) for i in range(8)]


def row_ring(over, s):
    if over == "z":
        return [(r, (r + 4 * s) % 16) for r in range(16)]
    return [(r, r // 4 * 4 + (r + s) % 4) for r in range(16)]


def gather_row(panel):
    return [panel] + [lax.ppermute(panel, "col", col_ring(s)) for s in (1, 3, 2)]


def gather_places(x, k):
    places = []
    for core in (k, 1 - k):
        places += [((x + 4 - s) % 4) * 2 + core for s in (0, 1, 3, 2)]
    return jnp.stack(places).astype(jnp.int32)


def block_at(z, y, x, k):
    moved = (y // 2 + k) % 2
    upper = moved * (1 - y % 2) + (1 - moved) * (y % 2)
    return upper * 8 + (z + x) % 4 * 2 + moved


def home_pairs():
    pairs = []
    for z in range(4):
        for y in range(4):
            for x in range(4):
                for k in range(2):
                    col = 2 * x + k
                    pairs.append(((z * 4 + y) * 8 + col, col * 16 + block_at(z, y, x, k)))
    return pairs


def table(rows):
    return jnp.stack(rows).astype(jnp.int32)


def strip_kernel(col, part, high_one, low_one, high_two, low_two, out, whole_strip):
    rows = part.shape[0] * BLK
    right_high, right_low = halves(part[...].reshape(rows, BLK))
    for i, (high, low) in enumerate(((high_one, low_one), (high_two, low_two))):
        dot = lambda left, right: lax.dot_general(left, right, (((0,), (0,)), ((), ())), preferred_element_type=F32)
        total = dot(low[...], right_high) + dot(high[...], right_low)
        whole_strip[i * W : (i + 1) * W] = dot(high[...], right_high) + total
    for i in range(5):
        at = pl.multiple_of((col[0] + i) % 8 * BLK, BLK)
        out[i * BLK : (i + 1) * BLK] = whole_strip[pl.ds(at, BLK)]


def strip(col, part, panels):
    vmem = pl.BlockSpec(memory_space=pltpu.VMEM)
    return pl.pallas_call(
        strip_kernel,
        in_specs=[pl.BlockSpec(memory_space=pltpu.SMEM)] + [vmem] * 5,
        out_specs=vmem,
        out_shape=jax.ShapeDtypeStruct((5 * BLK, BLK), F32),
        scratch_shapes=[pltpu.VMEM((8 * BLK, BLK), F32)],
        compiler_params=params(16),
        name="strip",
    )(col.reshape(1).astype(jnp.int32), part, *panels)


def sum_over_rows(part):
    piece = part.shape[0] // 16
    mine = lax.all_to_all(part.reshape(16, piece, BLK), "row", 0, 0, tiled=True).sum(axis=0)
    wide = jnp.broadcast_to(mine[None], (16, piece, BLK))
    return lax.all_to_all(wide, "row", 0, 0, tiled=True).reshape(part.shape)


def finish_kernel(places, *refs):
    strips, (square_one, square_top, base_two), (one, cross, two), total = refs[:8], refs[8:11], refs[11:14], refs[14]
    rows = 5 * BLK
    for i, piece in enumerate(strips):
        total[pl.ds(pl.multiple_of(places[i] * rows, BLK), rows), :] = piece[...]

    def block(r, q):
        if (r - q) % 8 <= 4:
            at = q * rows + (r - q) % 8 * BLK
            return total[at : at + BLK, :]
        at = r * rows + (q - r) % 8 * BLK
        return total[at : at + BLK, :].T

    for i in range(4):
        for j in range(4):
            at = (slice(i * BLK, (i + 1) * BLK), slice(j * BLK, (j + 1) * BLK))
            one[at] = square_one[at] + block(i, j)
            cross[at] = block(i, 4 + j) - square_top[at]
            two[at] = base_two[at] + block(4 + i, 4 + j)


def finish(places, strips, bases):
    square = jax.ShapeDtypeStruct((W, W), F32)
    vmem = pl.BlockSpec(memory_space=pltpu.VMEM)
    return pl.pallas_call(
        finish_kernel,
        in_specs=[pl.BlockSpec(memory_space=pltpu.SMEM)] + [vmem] * 11,
        out_specs=[vmem] * 3,
        out_shape=[square] * 3,
        scratch_shapes=[pltpu.VMEM((8 * 5 * BLK, BLK), F32)],
        compiler_params=params(16),
        name="finish",
    )(places, *strips, *bases)


def body(
    trailing,
    factor_one,
    inverse_one,
    factor_two_top,
    factor_two,
    inverse_two,
    structure_one,
    structure_two,
):
    row = lax.axis_index("row")
    col = lax.axis_index("col")
    z, y, x, k = row // 4, row % 4, col // 2, col % 2
    mask_one = block_flag(structure_one, row * 8 + col)
    mask_two = block_flag(structure_two, row * 8 + col)
    places = gather_places(x, k)
    home_way = home_pairs()

    normal_one = mask_one * product(factor_one, inverse_one)
    normal_top = product(factor_two_top, inverse_two)
    panel_two = mask_two * product(factor_two, inverse_two) - product(normal_one, normal_top)
    pieces = gather_row(jnp.concatenate([normal_one, panel_two], axis=1))
    trailing, pieces[0] = lax.optimization_barrier((trailing, pieces[0]))
    flips = flipped(trailing, table([block_at(i // 4, i % 4, x, k) for i in range(16)]))
    pieces, flips = lax.optimization_barrier((pieces, flips))
    pieces += [lax.ppermute(piece, "col", SWAP) for piece in pieces]

    def forward(over):
        return lambda value: lax.ppermute(value, "row", row_ring(over, 1))

    def backward(over):
        return lambda value: lax.ppermute(value, "row", row_ring(over, 3))

    def chunks(place, shifts):
        return table([(place + s) % 4 for s in shifts])

    def light(across, picks):
        return picks[0] + sum(lax.ppermute(picks[s], "row", row_ring(across, s)) for s in (1, 2, 3))

    order = lax.optimization_barrier
    high, low, top_one, bottom_one = far_product(0, chunks(z, [2]), places, pieces, *flips)
    panels = [high, low]
    top_one, bottom_one = forward("z")(top_one), backward("z")(bottom_one)
    high, low, top_two, bottom_two = far_product(1, chunks(y, [2]), places, pieces, *flips)
    panels += [high, low]
    top_two, bottom_two = forward("y")(top_two), backward("y")(bottom_two)
    ahead, behind, own_one = near_product(0, chunks(z, [1, 3, 0]), *panels[:2], *flips)
    ahead, behind = join(ahead, behind, top_one, bottom_one)
    rest_one = (forward("z")(ahead), backward("z")(behind))
    ahead, behind, own_two = near_product(1, chunks(y, [1, 3, 0]), *panels[2:], *flips)
    ahead, behind = join(ahead, behind, top_two, bottom_two)
    rest_two = (forward("y")(ahead), backward("y")(behind))
    own_one, own_two = order((own_one, own_two))

    sums_one = lax.ppermute(light("y", fold(y, own_one, *rest_one)), BOTH, home_way)
    sums_two = lax.ppermute(light("z", fold(z, own_two, *rest_two)), BOTH, home_way)
    column_one = -mask_one * sums_one
    column_two = -mask_two * sums_two

    square_one = product_t(inverse_one, inverse_one)
    square_top = product(square_one, normal_top)
    base_two = product_t(inverse_two, inverse_two) + product_t(normal_top, square_top)
    cut = lambda sums, j: sums[:, j * BLK : (j + 1) * BLK]
    part = jnp.stack([cut(sums, j) for sums in (sums_one, sums_two) for j in range(4)])
    part = lax.all_to_all(part, "col", 0, 0, tiled=True)
    total = sum_over_rows(strip(col, part, panels))
    strips = [total] + [lax.ppermute(total, "col", col_ring(s)) for s in (1, 3, 2)]
    strips += [lax.ppermute(piece, "col", SWAP) for piece in strips]
    diagonal_one, cross_two, diagonal_two = finish(places, strips, (square_one, square_top, base_two))
    return (column_one, diagonal_one, column_two, cross_two, diagonal_two)


def solution(mesh):
    return jax.shard_map(
        body,
        mesh=mesh,
        in_specs=(
            P("row", "col"),
            P(("row", "col"), None),
            P(),
            P(),
            P(("row", "col"), None),
            P(),
            P(),
            P(),
        ),
        out_specs=(P(("row", "col"), None), P(), P(("row", "col"), None), P(), P()),
        check_vma=False,
    )
```

time: 475 us -> 211 us (0.44)
  waiting for transfers between devices: 384 us -> 60.3 us
  starting transfers between devices: 0.43 us -> 63 us
  matrix products: 63.5 us -> 12.5 us
  Pallas kernels: 0 us -> 45.2 us
  blocking collectives: 0 us -> 17.6 us
  between operations: 14.3 us -> 2.38 us
  other arithmetic: 11.1 us -> 4.57 us
    psum x2 -> x0, waiting for transfers between devices: 295 us -> none  [the longest x1 153 us: body(): diag_total = lax.psum(quad_one, ('row', 'col'))]
    ppermute x0 -> x30, starting transfers between devices: none -> 55.3 us  [the longest x4 13.6 us: body(): strips += [lax.ppermute(piece, 'col', SWAP) for piece in strips]]
    dot_general x14 -> x8, matrix products: 63.5 us -> 12.5 us  [the longest x5 6.86 us: product(): jnp.dot(left, right, precision=lax.Precision.HIGH, preferred_element_type...]
    ppermute x0 -> x30, waiting for transfers between devices: none -> 49.6 us  [the longest x1 12.2 us: body(): lax.ppermute(light('z', fold(z, own_two, *rest_two)), BOTH, home_way)]
    all_gather x2 -> x0, waiting for transfers between devices: 49.2 us -> none  [panel_apart(): row_block = lax.all_gather(normal, 'col', axis=0, tiled=True)]
    pallas_call x0 -> x11, Pallas kernels: none -> 45.2 us  [the longest x2 16.4 us: near_product(): pl.pallas_call(near_kernel, grid_spec=pltpu.PrefetchScalarGridSpec(num_sc...]
    reduce_scatter x2 -> x0, waiting for transfers between devices: 40.2 us -> none  [sweep(): lax.psum_scatter(-product(trailing, col_block), 'col', scatter_dimension=...]
    all_to_all x0 -> x1, blocking collectives: none -> 17.6 us  [body(): part = lax.all_to_all(part, 'col', 0, 0, tiled=True)]
  transfers between devices with their start and end apart: 6 -> 32, of which waited for: 6 -> 15; matrix products, arithmetic and copies ran while one was open for 7% -> 5% of each run, Pallas kernels for 0% -> 16%
where the time goes in v2:
time: 211 us; the launch traced here: 210 us
  starting transfers between devices  63 us (30%)
  waiting for transfers between devices  60.3 us (29%)
  Pallas kernels  45.2 us (21%)
  blocking collectives  17.6 us (8%)
  matrix products  12.5 us (6%)
  other arithmetic  4.57 us (2%)
  local copies, waits for them, and re-layouts  4.46 us (2%)
  between operations  2.38 us (1%)
    all_to_all x1, blocking collectives, body(): part = lax.all_to_all(part, 'col', 0, 0, tiled=True)  17.6 us
    pallas_call x2, Pallas kernels, near_product(): pl.pallas_call(near_kernel, grid_spec=pltpu.PrefetchScalarGridSpec(num_sc...  16.4 us
    ppermute x4, starting transfers between devices, body(): strips += [lax.ppermute(piece, 'col', SWAP) for piece in strips]  13.6 us
    ppermute x1, waiting for transfers between devices, body(): lax.ppermute(light('z', fold(z, own_two, *rest_two)), BOTH, home_way)  12.2 us
    ppermute x3, waiting for transfers between devices, gather_row(): lax.ppermute(panel, 'col', col_ring(s))  11.4 us
    pallas_call x2, Pallas kernels, far_product(): pl.pallas_call(far_kernel, grid_spec=pltpu.PrefetchScalarGridSpec(num_sca...  11 us
    ppermute x6, starting transfers between devices, light(): lax.ppermute(picks[s], 'row', row_ring(across, s))  9.72 us
    ppermute x4, waiting for transfers between devices, backward(): return lambda value: lax.ppermute(value, 'row', row_ring(over, 3))  9.7 us
  transfers between devices with their start and end apart: 32, of which 15 were waited for; matrix products, arithmetic and copies ran while one was open for 5% of the time, Pallas kernels for 16%

profile of v2, /device:TPU:1, one launch (start us, length us, event | category | flops | bytes accessed | tf_op | source)
XLA Modules:
  0.0 210.0 jit_solution(17089037585208591900)
XLA Ops:
  0.7 1.4 compare_reduce_fusion.1
  2.8 1.3 compare_reduce_fusion
  4.7 2.2 %fusion.8 = f32[512,512]{1,0:T(8,128)S(1)} fusion(f32[512,512]{1,0:T(8,128)} %param.11, f32[512,512]{1,0:T(8,128)S(1)} %copy-done), kind=kOutput, calls=%fused_computation.29 | convolution fusion | flops 805306368 | bytes 3145728 | tf_op jit(solution)/shard_map/dot_general | solution.py:19
  7.0 1.6 convolution_multiply_fusion
  9.5 2.1 %collective-permute-start = (f32[128,1024]{1,0:T(8,128)S(1)}, f32[128,1024]{1,0:T(8,128)S(1)}, u32[]{:S(2)}, u32[]{:S(2)}) collective-permute-start(f32[128,1024]{1,0:T(8,128)S(1)} %pad_maximum_fusion.refs_0_), channel_id=1, source_target_pairs={{0,2},{1,3},{2,4},{3,5},{4,6},{5,7},{6,0},{7,1},{8,10},{9,11},{10,... | collective-permute-start | bytes 1572872 | tf_op jit(solution)/shard_map/ppermute | solution.py:192
  11.6 1.4 collective-permute-start.1
  12.9 1.6 collective-permute-start.2
  14.7 3.4 %copy-done.1 = f32[1024,2048]{1,0:T(8,128)S(1)} copy-done((f32[1024,2048]{1,0:T(8,128)S(1)}, f32[1024,2048]{1,0:T(8,128)}, u32[]{:S(2)}) %copy-start.1) | copy-done | bytes 8388632
  18.1 7.1 %flip.1 = (bf16[4,4,128,1024]{3,2,1,0:T(8,128)(2,1)}, bf16[4,4,128,1024]{3,2,1,0:T(8,128)(2,1)}) custom-call(s32[16]{0:T(128)S(1)} %stack.155.blocks, f32[1024,2048]{1,0:T(8,128)S(1)} %copy-done.1, f32[1024,2048]{1,0:T(8,128)S(1)} %copy-done.1), custom_call_target="tpu_custom_call" | custom-call | tf_op jit(solution)/shard_map/flip/pallas_call | solution.py:59
  25.2 11.4 %collective-permute-done.2.refs_3_ = f32[128,1024]{1,0:T(8,128)S(1)} collective-permute-done((f32[128,1024]{1,0:T(8,128)S(1)}, f32[128,1024]{1,0:T(8,128)S(1)}, u32[]{:S(2)}, u32[]{:S(2)}) %collective-permute-start.2) | collective-permute-done | bytes 524320 | tf_op jit(solution)/shard_map/ppermute | solution.py:192
  36.6 1.5 collective-permute-start.3
  42.1 5.5 %far.2 = (bf16[1024,512]{1,0:T(8,128)(2,1)}, bf16[1024,512]{1,0:T(8,128)(2,1)}, f32[256,512]{1,0:T(8,128)}, f32[256,512]{1,0:T(8,128)}) custom-call(s32[1]{0:T(128)} %bitcast.20.chunks, s32[8]{0:T(128)S(1)} %stack.165.places, f32[128,1024]{1,0:T(8,128)S(1)} %pad_maximum_fusion.refs_0_, f32[128,1024]{1,0:T(8,128)S(1)} %collective-permute-done.refs_1_, ...), custom_call_target="tpu_custom_call" | custom-call | tf_op jit(solution)/shard_map/far/pallas_call | solution.py:111
  47.6 1.6 collective-permute-start.7
  49.2 2.1 %collective-permute-start.8 = (f32[256,512]{1,0:T(8,128)}, f32[256,512]{1,0:T(8,128)}, u32[]{:S(2)}, u32[]{:S(2)}) collective-permute-start(f32[256,512]{1,0:T(8,128)} %get-tuple-element.66), channel_id=1, source_target_pairs={{0,96},{8,104},{16,112},{24,120},{32,0},{40,8},{48,16},{56,24},{64... | collective-permute-start | bytes 1572872 | tf_op jit(solution)/shard_map/ppermute | solution.py:321
  51.3 5.5 %far.3 = (bf16[1024,512]{1,0:T(8,128)(2,1)}, bf16[1024,512]{1,0:T(8,128)(2,1)}, f32[256,512]{1,0:T(8,128)}, f32[256,512]{1,0:T(8,128)}) custom-call(s32[1]{0:T(128)} %bitcast.32.chunks, s32[8]{0:T(128)S(1)} %stack.165.places, f32[128,1024]{1,0:T(8,128)S(1)} %pad_maximum_fusion.refs_0_, f32[128,1024]{1,0:T(8,128)S(1)} %collective-permute-done.refs_1_, ...), custom_call_target="tpu_custom_call" | custom-call | tf_op jit(solution)/shard_map/far/pallas_call | solution.py:111
  58.1 1.5 collective-permute-start.16
  59.7 8.2 %near.2 = (f32[512,512]{1,0:T(8,128)S(1)}, f32[512,512]{1,0:T(8,128)S(1)}, f32[512,512]{1,0:T(8,128)S(1)}) custom-call(s32[3]{0:T(128)S(1)} %pad_add_fusion.chunks, bf16[4,4,128,1024]{3,2,1,0:T(8,128)(2,1)} %get-tuple-element.50.refs_8_.flip_high, bf16[4,4,128,1024]{3,2,1,0:T(8,128)(2,1)} %get-tuple-element.51.refs_9_.flip_low, ...), custom_call_target="tpu_custom_call" | custom-call | tf_op jit(solution)/shard_map/near/pallas_call | solution.py:127
  67.9 1.7 join.2
  69.7 1.5 collective-permute-start.10
  71.3 8.2 %near.3 = (f32[512,512]{1,0:T(8,128)S(1)}, f32[512,512]{1,0:T(8,128)S(1)}, f32[512,512]{1,0:T(8,128)S(1)}) custom-call(s32[3]{0:T(128)S(1)} %pad_add_fusion.1.chunks, bf16[4,4,128,1024]{3,2,1,0:T(8,128)(2,1)} %get-tuple-element.50.refs_8_.flip_high, bf16[4,4,128,1024]{3,2,1,0:T(8,128)(2,1)} %get-tuple-element.51.refs_9_.flip_low, ...), custom_call_target="tpu_custom_call" | custom-call | tf_op jit(solution)/shard_map/near/pallas_call | solution.py:127
  79.5 1.4 join.3
  81.0 2.7 %collective-permute-start.18 = (f32[512,512]{1,0:T(8,128)S(1)}, f32[512,512]{1,0:T(8,128)S(1)}, u32[]{:S(2)}, u32[]{:S(2)}) collective-permute-start(f32[512,512]{1,0:T(8,128)S(1)} %get-tuple-element.79), channel_id=1, source_target_pairs={{0,24},{8,0},{16,8},{24,16},{32,56},{40,32},{48,40},{56,48},{64,88... | collective-permute-start | bytes 3145736 | tf_op jit(solution)/shard_map/ppermute | solution.py:321
  83.7 9.7 %collective-permute-done.10.other = f32[512,512]{1,0:T(8,128)} collective-permute-done((f32[512,512]{1,0:T(8,128)S(1)}, f32[512,512]{1,0:T(8,128)}, u32[]{:S(2)}, u32[]{:S(2)}) %collective-permute-start.10) | collective-permute-done | bytes 1048608 | tf_op jit(solution)/shard_map/ppermute | solution.py:321
  93.4 2.1 collective-permute-done.9.one
  95.5 1.8 fold.2
  97.4 2.6 %collective-permute-start.12 = (f32[128,512]{1,0:T(8,128)S(1)}, f32[128,512]{1,0:T(8,128)S(1)}, u32[]{:S(2)}, u32[]{:S(2)}) collective-permute-start(f32[128,512]{1,0:T(8,128)S(1)} %get-tuple-element.71), channel_id=1, source_target_pairs={{0,16},{8,24},{16,0},{24,8},{32,48},{40,56},{48,32},{56,40},{64,80... | collective-permute-start | bytes 786440 | tf_op jit(solution)/shard_map/ppermute | solution.py:327
  101.1 4.1 %collective-permute-done.17.one = f32[512,512]{1,0:T(8,128)S(1)} collective-permute-done((f32[512,512]{1,0:T(8,128)S(1)}, f32[512,512]{1,0:T(8,128)S(1)}, u32[]{:S(2)}, u32[]{:S(2)}) %collective-permute-start.17) | collective-permute-done | bytes 1048608 | tf_op jit(solution)/shard_map/ppermute | solution.py:318
  105.8 3.3 %collective-permute-start.20 = (f32[128,512]{1,0:T(8,128)S(1)}, f32[128,512]{1,0:T(8,128)S(1)}, u32[]{:S(2)}, u32[]{:S(2)}) collective-permute-start(f32[128,512]{1,0:T(8,128)S(1)} %get-tuple-element.82), channel_id=1, source_target_pairs={{0,64},{8,72},{16,80},{24,88},{32,96},{40,104},{48,112},{56,120},{... | collective-permute-start | bytes 786440 | tf_op jit(solution)/shard_map/ppermute | solution.py:327
  109.1 1.8 collective-permute-done.11
  110.9 2.4 %collective-permute-start.21 = (f32[128,512]{1,0:T(8,128)S(1)}, f32[128,512]{1,0:T(8,128)S(1)}, u32[]{:S(2)}, u32[]{:S(2)}) collective-permute-start(f32[128,512]{1,0:T(8,128)S(1)} %get-tuple-element.83), channel_id=1, source_target_pairs={{0,96},{8,104},{16,112},{24,120},{32,0},{40,8},{48,16},{56,24},{64... | collective-permute-start | bytes 786440 | tf_op jit(solution)/shard_map/ppermute | solution.py:327
  113.2 3.0 %collective-permute-done.12 = f32[128,512]{1,0:T(8,128)S(1)} collective-permute-done((f32[128,512]{1,0:T(8,128)S(1)}, f32[128,512]{1,0:T(8,128)S(1)}, u32[]{:S(2)}, u32[]{:S(2)}) %collective-permute-start.12) | collective-permute-done | bytes 262176 | tf_op jit(solution)/shard_map/ppermute | solution.py:327
  116.4 4.4 %collective-permute-start.14 = (f32[128,512]{1,0:T(8,128)S(1)}, f32[128,512]{1,0:T(8,128)S(1)}, u32[]{:S(2)}, u32[]{:S(2)}) collective-permute-start(f32[128,512]{1,0:T(8,128)S(1)} %add_add_fusion.1), channel_id=1, source_target_pairs={{0,0},{1,25},{2,34},{3,59},{4,68},{5,93},{6,102},{7,127},{8,8},{9,... | collective-permute-start | bytes 786440 | tf_op jit(solution)/shard_map/ppermute | solution.py:344
  120.9 6.9 %collective-permute-start.22 = (f32[128,512]{1,0:T(8,128)S(1)}, f32[128,512]{1,0:T(8,128)S(1)}, u32[]{:S(2)}, u32[]{:S(2)}) collective-permute-start(f32[128,512]{1,0:T(8,128)S(1)} %add_add_fusion), channel_id=1, source_target_pairs={{0,0},{1,25},{2,34},{3,59},{4,68},{5,93},{6,102},{7,127},{8,8},{9,... | collective-permute-start | bytes 786440 | tf_op jit(solution)/shard_map/ppermute | solution.py:345
  127.9 1.7 collective-permute-done.14
  129.7 12.2 %collective-permute-done.22 = f32[128,512]{1,0:T(8,128)S(1)} collective-permute-done((f32[128,512]{1,0:T(8,128)S(1)}, f32[128,512]{1,0:T(8,128)S(1)}, u32[]{:S(2)}, u32[]{:S(2)}) %collective-permute-start.22) | collective-permute-done | bytes 262176 | tf_op jit(solution)/shard_map/ppermute | solution.py:345
  142.0 17.6 %all_to_all.15.part = f32[8,128,128]{2,1,0:T(8,128)S(1)} all-to-all(f32[8,128,128]{2,1,0:T(8,128)S(1)} %fusion), channel_id=1, replica_groups=mesh['row'=16,'col'=8] {'col'}, dimensions={0} | all-to-all | bytes 1048576 | tf_op jit(solution)/shard_map/all_to_all | solution.py:354
  159.6 2.6 %strip.1 = f32[640,128]{1,0:T(8,128)} custom-call(s32[1]{0:T(128)} %bitcast.33.col, f32[8,128,128]{2,1,0:T(8,128)S(1)} %all_to_all.15.part, bf16[1024,512]{1,0:T(8,128)(2,1)S(1)} %copy-done.2, bf16[1024,512]{1,0:T(8,128)(2,1)S(1)} %copy-done.3, bf16[1024,512]{1,0:T(8,128)(2,1)S(1)} %copy-done.4, bf16[1024,512]{1,0:T(8,128)(2,1)S(1)} %copy-done.5), custom_call_target="tpu_custom_call" | custom-call | tf_op jit(solution)/shard_map/strip/pallas_call | solution.py:237
  162.2 4.2 %all-to-all-start.1 = ((f32[16,40,128]{2,1,0:T(8,128)}), f32[16,40,128]{2,1,0:T(8,128)S(1)}, u32[]{:S(2)}, u32[]{:S(2)}) async-start(f32[16,40,128]{2,1,0:T(8,128)} %bitcast.43), calls=%async_computation.1 | async-start | bytes 655360 | tf_op jit(solution)/shard_map/all_to_all | solution.py:250
  167.4 7.0 %all-to-all-done.1 = f32[16,40,128]{2,1,0:T(8,128)S(1)} async-done(((f32[16,40,128]{2,1,0:T(8,128)}), f32[16,40,128]{2,1,0:T(8,128)S(1)}, u32[]{:S(2)}, u32[]{:S(2)}) %all-to-all-start.1) | async-done | bytes 327712 | tf_op jit(solution)/shard_map/all_to_all | solution.py:250
  175.2 3.5 %all-to-all-start.2 = ((f32[16,40,128]{2,1,0:T(8,128)}), f32[16,40,128]{2,1,0:T(8,128)S(1)}, u32[]{:S(2)}, u32[]{:S(2)}) async-start(f32[16,40,128]{2,1,0:T(8,128)} %broadcast_in_dim.2), calls=%async_computation.2 | async-start | bytes 655360 | tf_op jit(solution)/shard_map/all_to_all | solution.py:252
  178.8 2.0 fusion.11
  180.8 2.2 %fusion.10.refs_9_ = f32[512,512]{1,0:T(8,128)S(1)} fusion(f32[512,512]{1,0:T(8,128)S(1)} %fusion.9.refs_8_, f32[512,512]{1,0:T(8,128)} %copy-done.8), kind=kOutput, calls=%fused_computation.31 | convolution fusion | flops 805306368 | bytes 3145728 | tf_op jit(solution)/shard_map/dot_general | solution.py:19
  183.0 3.6 %all-to-all-done.2 = f32[16,40,128]{2,1,0:T(8,128)S(1)} async-done(((f32[16,40,128]{2,1,0:T(8,128)}), f32[16,40,128]{2,1,0:T(8,128)S(1)}, u32[]{:S(2)}, u32[]{:S(2)}) %all-to-all-start.2) | async-done | bytes 327712 | tf_op jit(solution)/shard_map/all_to_all | solution.py:252
  186.9 2.4 %collective-permute-start.24 = (f32[640,128]{1,0:T(8,128)S(1)}, f32[640,128]{1,0:T(8,128)S(1)}, u32[]{:S(2)}, u32[]{:S(2)}) collective-permute-start(f32[640,128]{1,0:T(8,128)S(1)} %bitcast.86), channel_id=1, source_target_pairs={{0,6},{1,7},{2,0},{3,1},{4,2},{5,3},{6,4},{7,5},{8,14},{9,15},{10,... | collective-permute-start | bytes 983048 | tf_op jit(solution)/shard_map/ppermute | solution.py:356
  189.3 2.6 %convolution_add_fusion.refs_10_ = f32[512,512]{1,0:T(8,128)S(1)} fusion(f32[512,512]{1,0:T(8,128)} %fusion.11, f32[512,512]{1,0:T(8,128)} %copy-done.8, f32[512,512]{1,0:T(8,128)S(1)} %fusion.10.refs_9_), kind=kOutput, calls=%fused_computation | convolution fusion | flops 805568512 | bytes 4194304 | tf_op jit(solution)/shard_map/dot_general | solution.py:23
  191.9 4.1 %collective-permute-start.26 = (f32[640,128]{1,0:T(8,128)S(1)}, f32[640,128]{1,0:T(8,128)S(1)}, u32[]{:S(2)}, u32[]{:S(2)}) collective-permute-start(f32[640,128]{1,0:T(8,128)S(1)} %bitcast.88), channel_id=1, source_target_pairs={{0,1},{1,0},{2,3},{3,2},{4,5},{5,4},{6,7},{7,6},{8,9},{9,8},{10,11... | collective-permute-start | bytes 983048 | tf_op jit(solution)/shard_map/ppermute | solution.py:357
  196.0 9.0 %collective-permute-start.27 = (f32[640,128]{1,0:T(8,128)S(1)}, f32[640,128]{1,0:T(8,128)S(1)}, u32[]{:S(2)}, u32[]{:S(2)}) collective-permute-start(f32[640,128]{1,0:T(8,128)S(1)} %collective-permute-done.23.refs_1_), channel_id=1, source_target_pairs={{0,1},{1,0},{2,3},{3,2},{4,5},{5,4},{6,7},{7,6},{8,9},{9,8},{10,11... | collective-permute-start | bytes 983048 | tf_op jit(solution)/shard_map/ppermute | solution.py:357
  207.2 2.8 %finish.1 = (f32[512,512]{1,0:T(8,128)}, f32[512,512]{1,0:T(8,128)}, f32[512,512]{1,0:T(8,128)}) custom-call(s32[8]{0:T(128)S(1)} %stack.165.places, f32[640,128]{1,0:T(8,128)S(1)} %bitcast.89, f32[640,128]{1,0:T(8,128)S(1)} %collective-permute-done.23.refs_1_, f32[640,128]{1,0:T(8,128)S(1)} %collective-permute-done.24.refs_2_, ...), custom_call_target="tpu_custom_call" | custom-call | tf_op jit(solution)/shard_map/finish/pallas_call | solution.py:279
  (89 shorter events, 12.9 us)
Async XLA Ops:
  0.6 4.1 %copy-start = (f32[512,512]{1,0:T(8,128)S(1)}, f32[512,512]{1,0:T(8,128)}, u32[]{:S(2)}) copy-start(f32[512,512]{1,0:T(8,128)} %param.13) | copy-start | bytes 3145732
  0.6 7.9 %copy-start.9 = (f32[512,512]{1,0:T(8,128)S(1)}, f32[512,512]{1,0:T(8,128)}, u32[]{:S(2)}) copy-start(f32[512,512]{1,0:T(8,128)} %param.10) | copy-start | bytes 3145732
  0.7 7.9 %copy-start.15 = (f32[128,512]{1,0:T(8,128)S(1)}, f32[128,512]{1,0:T(8,128)}, u32[]{:S(2)}) copy-start(f32[128,512]{1,0:T(8,128)} %param.9) | copy-start | bytes 786436
  7.0 4.6 %copy-start.8 = (f32[512,512]{1,0:T(8,128)}, f32[512,512]{1,0:T(8,128)S(1)}, u32[]{:S(2)}) copy-start(f32[512,512]{1,0:T(8,128)S(1)} %fusion.8) | copy-start | bytes 3145732
  9.5 15.7 %collective-permute-start = (f32[128,1024]{1,0:T(8,128)S(1)}, f32[128,1024]{1,0:T(8,128)S(1)}, u32[]{:S(2)}, u32[]{:S(2)}) collective-permute-start(f32[128,1024]{1,0:T(8,128)S(1)} %pad_maximum_fusion.refs_0_), channel_id=1, source_target_pairs={{0,2},{1,3},{2,4},{3,5},{4,6},{5,7},{6,0},{7,1},{8,10},{9,11},{10,... | collective-permute-start | bytes 1572872 | tf_op jit(solution)/shard_map/ppermute | solution.py:192
  11.6 13.6 %collective-permute-start.1 = (f32[128,1024]{1,0:T(8,128)S(1)}, f32[128,1024]{1,0:T(8,128)S(1)}, u32[]{:S(2)}, u32[]{:S(2)}) collective-permute-start(f32[128,1024]{1,0:T(8,128)S(1)} %pad_maximum_fusion.refs_0_), channel_id=1, source_target_pairs={{0,6},{1,7},{2,0},{3,1},{4,2},{5,3},{6,4},{7,5},{8,14},{9,15},{10,... | collective-permute-start | bytes 1572872 | tf_op jit(solution)/shard_map/ppermute | solution.py:192
  12.9 23.7 %collective-permute-start.2 = (f32[128,1024]{1,0:T(8,128)S(1)}, f32[128,1024]{1,0:T(8,128)S(1)}, u32[]{:S(2)}, u32[]{:S(2)}) collective-permute-start(f32[128,1024]{1,0:T(8,128)S(1)} %pad_maximum_fusion.refs_0_), channel_id=1, source_target_pairs={{0,4},{1,5},{2,6},{3,7},{4,0},{5,1},{6,2},{7,3},{8,12},{9,13},{10,... | collective-permute-start | bytes 1572872 | tf_op jit(solution)/shard_map/ppermute | solution.py:192
  14.7 3.4 %copy-start.1 = (f32[1024,2048]{1,0:T(8,128)S(1)}, f32[1024,2048]{1,0:T(8,128)}, u32[]{:S(2)}) copy-start(f32[1024,2048]{1,0:T(8,128)} %right) | copy-start | bytes 25165828
  36.6 3.2 %collective-permute-start.3 = (f32[128,1024]{1,0:T(8,128)S(1)}, f32[128,1024]{1,0:T(8,128)}, u32[]{:S(2)}, u32[]{:S(2)}) collective-permute-start(f32[128,1024]{1,0:T(8,128)S(1)} %pad_maximum_fusion.refs_0_), channel_id=1, source_target_pairs={{0,1},{1,0},{2,3},{3,2},{4,5},{5,4},{6,7},{7,6},{8,9},{9,8},{10,11... | collective-permute-start | bytes 1572872 | tf_op jit(solution)/shard_map/ppermute | solution.py:315
  38.1 2.4 %collective-permute-start.4 = (f32[128,1024]{1,0:T(8,128)S(1)}, f32[128,1024]{1,0:T(8,128)}, u32[]{:S(2)}, u32[]{:S(2)}) collective-permute-start(f32[128,1024]{1,0:T(8,128)S(1)} %collective-permute-done.refs_1_), channel_id=1, source_target_pairs={{0,1},{1,0},{2,3},{3,2},{4,5},{5,4},{6,7},{7,6},{8,9},{9,8},{10,11... | collective-permute-start | bytes 1572872 | tf_op jit(solution)/shard_map/ppermute | solution.py:315
  38.1 3.2 %collective-permute-start.5 = (f32[128,1024]{1,0:T(8,128)S(1)}, f32[128,1024]{1,0:T(8,128)}, u32[]{:S(2)}, u32[]{:S(2)}) collective-permute-start(f32[128,1024]{1,0:T(8,128)S(1)} %collective-permute-done.1.refs_2_), channel_id=1, source_target_pairs={{0,1},{1,0},{2,3},{3,2},{4,5},{5,4},{6,7},{7,6},{8,9},{9,8},{10,11... | collective-permute-start | bytes 1572872 | tf_op jit(solution)/shard_map/ppermute | solution.py:315
  38.7 3.4 %collective-permute-start.6 = (f32[128,1024]{1,0:T(8,128)S(1)}, f32[128,1024]{1,0:T(8,128)}, u32[]{:S(2)}, u32[]{:S(2)}) collective-permute-start(f32[128,1024]{1,0:T(8,128)S(1)} %collective-permute-done.2.refs_3_), channel_id=1, source_target_pairs={{0,1},{1,0},{2,3},{3,2},{4,5},{5,4},{6,7},{7,6},{8,9},{9,8},{10,11... | collective-permute-start | bytes 1572872 | tf_op jit(solution)/shard_map/ppermute | solution.py:315
  47.6 20.4 %collective-permute-start.7 = (f32[256,512]{1,0:T(8,128)}, f32[256,512]{1,0:T(8,128)}, u32[]{:S(2)}, u32[]{:S(2)}) collective-permute-start(f32[256,512]{1,0:T(8,128)} %get-tuple-element.65), channel_id=1, source_target_pairs={{0,32},{8,40},{16,48},{24,56},{32,64},{40,72},{48,80},{56,88},{64,... | collective-permute-start | bytes 1572872 | tf_op jit(solution)/shard_map/ppermute | solution.py:318
  49.2 18.7 %collective-permute-start.8 = (f32[256,512]{1,0:T(8,128)}, f32[256,512]{1,0:T(8,128)}, u32[]{:S(2)}, u32[]{:S(2)}) collective-permute-start(f32[256,512]{1,0:T(8,128)} %get-tuple-element.66), channel_id=1, source_target_pairs={{0,96},{8,104},{16,112},{24,120},{32,0},{40,8},{48,16},{56,24},{64... | collective-permute-start | bytes 1572872 | tf_op jit(solution)/shard_map/ppermute | solution.py:321
  56.9 22.7 %collective-permute-start.15 = (f32[256,512]{1,0:T(8,128)}, f32[256,512]{1,0:T(8,128)}, u32[]{:S(2)}, u32[]{:S(2)}) collective-permute-start(f32[256,512]{1,0:T(8,128)} %get-tuple-element.76), channel_id=1, source_target_pairs={{0,8},{8,16},{16,24},{24,0},{32,40},{40,48},{48,56},{56,32},{64,72... | collective-permute-start | bytes 1572872 | tf_op jit(solution)/shard_map/ppermute | solution.py:318
  58.1 21.4 %collective-permute-start.16 = (f32[256,512]{1,0:T(8,128)}, f32[256,512]{1,0:T(8,128)}, u32[]{:S(2)}, u32[]{:S(2)}) collective-permute-start(f32[256,512]{1,0:T(8,128)} %get-tuple-element.77), channel_id=1, source_target_pairs={{0,24},{8,0},{16,8},{24,16},{32,56},{40,32},{48,40},{56,48},{64,88... | collective-permute-start | bytes 1572872 | tf_op jit(solution)/shard_map/ppermute | solution.py:321
  67.9 3.3 %copy-start.6 = (f32[512,512]{1,0:T(8,128)}, f32[512,512]{1,0:T(8,128)S(1)}, u32[]{:S(2)}) copy-start(f32[512,512]{1,0:T(8,128)S(1)} %get-tuple-element.62.own) | copy-start | bytes 3145732
  69.7 23.7 %collective-permute-start.10 = (f32[512,512]{1,0:T(8,128)S(1)}, f32[512,512]{1,0:T(8,128)}, u32[]{:S(2)}, u32[]{:S(2)}) collective-permute-start(f32[512,512]{1,0:T(8,128)S(1)} %get-tuple-element.68), channel_id=1, source_target_pairs={{0,96},{8,104},{16,112},{24,120},{32,0},{40,8},{48,16},{56,24},{64... | collective-permute-start | bytes 3145736 | tf_op jit(solution)/shard_map/ppermute | solution.py:321
  71.2 24.3 %collective-permute-start.9 = (f32[512,512]{1,0:T(8,128)S(1)}, f32[512,512]{1,0:T(8,128)}, u32[]{:S(2)}, u32[]{:S(2)}) collective-permute-start(f32[512,512]{1,0:T(8,128)S(1)} %get-tuple-element.67), channel_id=1, source_target_pairs={{0,32},{8,40},{16,48},{24,56},{32,64},{40,72},{48,80},{56,88},{64,... | collective-permute-start | bytes 3145736 | tf_op jit(solution)/shard_map/ppermute | solution.py:318
  71.3 24.2 %copy-start.7 = (f32[512,512]{1,0:T(8,128)S(1)}, f32[512,512]{1,0:T(8,128)}, u32[]{:S(2)}) copy-start(f32[512,512]{1,0:T(8,128)} %copy-done.6) | copy-start | bytes 3145732
  80.9 24.2 %collective-permute-start.17 = (f32[512,512]{1,0:T(8,128)S(1)}, f32[512,512]{1,0:T(8,128)S(1)}, u32[]{:S(2)}, u32[]{:S(2)}) collective-permute-start(f32[512,512]{1,0:T(8,128)S(1)} %get-tuple-element.78), channel_id=1, source_target_pairs={{0,8},{8,16},{16,24},{24,0},{32,40},{40,48},{48,56},{56,32},{64,72... | collective-permute-start | bytes 3145736 | tf_op jit(solution)/shard_map/ppermute | solution.py:318
  81.0 24.1 %collective-permute-start.18 = (f32[512,512]{1,0:T(8,128)S(1)}, f32[512,512]{1,0:T(8,128)S(1)}, u32[]{:S(2)}, u32[]{:S(2)}) collective-permute-start(f32[512,512]{1,0:T(8,128)S(1)} %get-tuple-element.79), channel_id=1, source_target_pairs={{0,24},{8,0},{16,8},{24,16},{32,56},{40,32},{48,40},{56,48},{64,88... | collective-permute-start | bytes 3145736 | tf_op jit(solution)/shard_map/ppermute | solution.py:321
  97.3 62.3 %copy-start.2 = (bf16[1024,512]{1,0:T(8,128)(2,1)S(1)}, bf16[1024,512]{1,0:T(8,128)(2,1)}, u32[]{:S(2)}) copy-start(bf16[1024,512]{1,0:T(8,128)(2,1)} %get-tuple-element.56.high.high_one) | copy-start | bytes 3145732
  97.3 62.2 %copy-start.3 = (bf16[1024,512]{1,0:T(8,128)(2,1)S(1)}, bf16[1024,512]{1,0:T(8,128)(2,1)}, u32[]{:S(2)}) copy-start(bf16[1024,512]{1,0:T(8,128)(2,1)} %get-tuple-element.57.low.low_one) | copy-start | bytes 3145732
  97.3 62.2 %copy-start.4 = (bf16[1024,512]{1,0:T(8,128)(2,1)S(1)}, bf16[1024,512]{1,0:T(8,128)(2,1)}, u32[]{:S(2)}) copy-start(bf16[1024,512]{1,0:T(8,128)(2,1)} %get-tuple-element.59.high.high_two) | copy-start | bytes 3145732
  97.3 62.2 %copy-start.5 = (bf16[1024,512]{1,0:T(8,128)(2,1)S(1)}, bf16[1024,512]{1,0:T(8,128)(2,1)}, u32[]{:S(2)}) copy-start(bf16[1024,512]{1,0:T(8,128)(2,1)} %get-tuple-element.60.low.low_two) | copy-start | bytes 3145732
  97.3 13.5 %collective-permute-start.11 = (f32[128,512]{1,0:T(8,128)S(1)}, f32[128,512]{1,0:T(8,128)S(1)}, u32[]{:S(2)}, u32[]{:S(2)}) collective-permute-start(f32[128,512]{1,0:T(8,128)S(1)} %get-tuple-element.70), channel_id=1, source_target_pairs={{0,8},{8,16},{16,24},{24,0},{32,40},{40,48},{48,56},{56,32},{64,72... | collective-permute-start | bytes 786440 | tf_op jit(solution)/shard_map/ppermute | solution.py:327
  97.4 18.8 %collective-permute-start.12 = (f32[128,512]{1,0:T(8,128)S(1)}, f32[128,512]{1,0:T(8,128)S(1)}, u32[]{:S(2)}, u32[]{:S(2)}) collective-permute-start(f32[128,512]{1,0:T(8,128)S(1)} %get-tuple-element.71), channel_id=1, source_target_pairs={{0,16},{8,24},{16,0},{24,8},{32,48},{40,56},{48,32},{56,40},{64,80... | collective-permute-start | bytes 786440 | tf_op jit(solution)/shard_map/ppermute | solution.py:327
  100.0 16.3 %collective-permute-start.13 = (f32[128,512]{1,0:T(8,128)S(1)}, f32[128,512]{1,0:T(8,128)S(1)}, u32[]{:S(2)}, u32[]{:S(2)}) collective-permute-start(f32[128,512]{1,0:T(8,128)S(1)} %get-tuple-element.72), channel_id=1, source_target_pairs={{0,24},{8,0},{16,8},{24,16},{32,56},{40,32},{48,40},{56,48},{64,88... | collective-permute-start | bytes 786440 | tf_op jit(solution)/shard_map/ppermute | solution.py:327
  105.5 15.3 %collective-permute-start.19 = (f32[128,512]{1,0:T(8,128)S(1)}, f32[128,512]{1,0:T(8,128)S(1)}, u32[]{:S(2)}, u32[]{:S(2)}) collective-permute-start(f32[128,512]{1,0:T(8,128)S(1)} %get-tuple-element.81), channel_id=1, source_target_pairs={{0,32},{8,40},{16,48},{24,56},{32,64},{40,72},{48,80},{56,88},{64,... | collective-permute-start | bytes 786440 | tf_op jit(solution)/shard_map/ppermute | solution.py:327
  105.8 15.0 %collective-permute-start.20 = (f32[128,512]{1,0:T(8,128)S(1)}, f32[128,512]{1,0:T(8,128)S(1)}, u32[]{:S(2)}, u32[]{:S(2)}) collective-permute-start(f32[128,512]{1,0:T(8,128)S(1)} %get-tuple-element.82), channel_id=1, source_target_pairs={{0,64},{8,72},{16,80},{24,88},{32,96},{40,104},{48,112},{56,120},{... | collective-permute-start | bytes 786440 | tf_op jit(solution)/shard_map/ppermute | solution.py:327
  110.9 9.9 %collective-permute-start.21 = (f32[128,512]{1,0:T(8,128)S(1)}, f32[128,512]{1,0:T(8,128)S(1)}, u32[]{:S(2)}, u32[]{:S(2)}) collective-permute-start(f32[128,512]{1,0:T(8,128)S(1)} %get-tuple-element.83), channel_id=1, source_target_pairs={{0,96},{8,104},{16,112},{24,120},{32,0},{40,8},{48,16},{56,24},{64... | collective-permute-start | bytes 786440 | tf_op jit(solution)/shard_map/ppermute | solution.py:327
  116.4 13.2 %collective-permute-start.14 = (f32[128,512]{1,0:T(8,128)S(1)}, f32[128,512]{1,0:T(8,128)S(1)}, u32[]{:S(2)}, u32[]{:S(2)}) collective-permute-start(f32[128,512]{1,0:T(8,128)S(1)} %add_add_fusion.1), channel_id=1, source_target_pairs={{0,0},{1,25},{2,34},{3,59},{4,68},{5,93},{6,102},{7,127},{8,8},{9,... | collective-permute-start | bytes 786440 | tf_op jit(solution)/shard_map/ppermute | solution.py:344
  120.9 45.5 %copy-start.10 = (f32[512,512]{1,0:T(8,128)S(1)}, f32[512,512]{1,0:T(8,128)}, u32[]{:S(2)}) copy-start(f32[512,512]{1,0:T(8,128)} %param.10) | copy-start | bytes 3145732
  120.9 21.0 %collective-permute-start.22 = (f32[128,512]{1,0:T(8,128)S(1)}, f32[128,512]{1,0:T(8,128)S(1)}, u32[]{:S(2)}, u32[]{:S(2)}) collective-permute-start(f32[128,512]{1,0:T(8,128)S(1)} %add_add_fusion), channel_id=1, source_target_pairs={{0,0},{1,25},{2,34},{3,59},{4,68},{5,93},{6,102},{7,127},{8,8},{9,... | collective-permute-start | bytes 786440 | tf_op jit(solution)/shard_map/ppermute | solution.py:345
  129.6 32.6 %copy-start.11 = (f32[128,512]{1,0:T(8,128)}, f32[128,512]{1,0:T(8,128)S(1)}, u32[]{:S(2)}) copy-start(f32[128,512]{1,0:T(8,128)S(1)} %collective-permute-done.14) | copy-start | bytes 786436
  141.9 20.3 %copy-start.13 = (f32[128,512]{1,0:T(8,128)}, f32[128,512]{1,0:T(8,128)S(1)}, u32[]{:S(2)}) copy-start(f32[128,512]{1,0:T(8,128)S(1)} %collective-permute-done.22) | copy-start | bytes 786436
  162.2 12.3 %all-to-all-start.1 = ((f32[16,40,128]{2,1,0:T(8,128)}), f32[16,40,128]{2,1,0:T(8,128)S(1)}, u32[]{:S(2)}, u32[]{:S(2)}) async-start(f32[16,40,128]{2,1,0:T(8,128)} %bitcast.43), calls=%async_computation.1 | async-start | bytes 655360 | tf_op jit(solution)/shard_map/all_to_all | solution.py:250
  175.2 11.4 %all-to-all-start.2 = ((f32[16,40,128]{2,1,0:T(8,128)}), f32[16,40,128]{2,1,0:T(8,128)S(1)}, u32[]{:S(2)}, u32[]{:S(2)}) async-start(f32[16,40,128]{2,1,0:T(8,128)} %broadcast_in_dim.2), calls=%async_computation.2 | async-start | bytes 655360 | tf_op jit(solution)/shard_map/all_to_all | solution.py:252
  186.6 18.9 %copy-start.14 = (f32[128,512]{1,0:T(8,128)S(1)}, f32[128,512]{1,0:T(8,128)}, u32[]{:S(2)}) copy-start(f32[128,512]{1,0:T(8,128)} %copy-done.13) | copy-start | bytes 786436
  186.6 19.6 %copy-start.12 = (f32[128,512]{1,0:T(8,128)S(1)}, f32[128,512]{1,0:T(8,128)}, u32[]{:S(2)}) copy-start(f32[128,512]{1,0:T(8,128)} %copy-done.11) | copy-start | bytes 786436
  186.6 9.4 %collective-permute-start.23 = (f32[640,128]{1,0:T(8,128)S(1)}, f32[640,128]{1,0:T(8,128)S(1)}, u32[]{:S(2)}, u32[]{:S(2)}) collective-permute-start(f32[640,128]{1,0:T(8,128)S(1)} %bitcast.85), channel_id=1, source_target_pairs={{0,2},{1,3},{2,4},{3,5},{4,6},{5,7},{6,0},{7,1},{8,10},{9,11},{10,... | collective-permute-start | bytes 983048 | tf_op jit(solution)/shard_map/ppermute | solution.py:356
  186.9 18.1 %collective-permute-start.24 = (f32[640,128]{1,0:T(8,128)S(1)}, f32[640,128]{1,0:T(8,128)S(1)}, u32[]{:S(2)}, u32[]{:S(2)}) collective-permute-start(f32[640,128]{1,0:T(8,128)S(1)} %bitcast.86), channel_id=1, source_target_pairs={{0,6},{1,7},{2,0},{3,1},{4,2},{5,3},{6,4},{7,5},{8,14},{9,15},{10,... | collective-permute-start | bytes 983048 | tf_op jit(solution)/shard_map/ppermute | solution.py:356
  189.3 15.7 %collective-permute-start.25 = (f32[640,128]{1,0:T(8,128)S(1)}, f32[640,128]{1,0:T(8,128)S(1)}, u32[]{:S(2)}, u32[]{:S(2)}) collective-permute-start(f32[640,128]{1,0:T(8,128)S(1)} %bitcast.87), channel_id=1, source_target_pairs={{0,4},{1,5},{2,6},{3,7},{4,0},{5,1},{6,2},{7,3},{8,12},{9,13},{10,... | collective-permute-start | bytes 983048 | tf_op jit(solution)/shard_map/ppermute | solution.py:356
  191.9 15.1 %collective-permute-start.26 = (f32[640,128]{1,0:T(8,128)S(1)}, f32[640,128]{1,0:T(8,128)S(1)}, u32[]{:S(2)}, u32[]{:S(2)}) collective-permute-start(f32[640,128]{1,0:T(8,128)S(1)} %bitcast.88), channel_id=1, source_target_pairs={{0,1},{1,0},{2,3},{3,2},{4,5},{5,4},{6,7},{7,6},{8,9},{9,8},{10,11... | collective-permute-start | bytes 983048 | tf_op jit(solution)/shard_map/ppermute | solution.py:357
  196.0 11.0 %collective-permute-start.27 = (f32[640,128]{1,0:T(8,128)S(1)}, f32[640,128]{1,0:T(8,128)S(1)}, u32[]{:S(2)}, u32[]{:S(2)}) collective-permute-start(f32[640,128]{1,0:T(8,128)S(1)} %collective-permute-done.23.refs_1_), channel_id=1, source_target_pairs={{0,1},{1,0},{2,3},{3,2},{4,5},{5,4},{6,7},{7,6},{8,9},{9,8},{10,11... | collective-permute-start | bytes 983048 | tf_op jit(solution)/shard_map/ppermute | solution.py:357
  205.0 2.0 collective-permute-start.28
  205.0 2.2 %collective-permute-start.29 = (f32[640,128]{1,0:T(8,128)S(1)}, f32[640,128]{1,0:T(8,128)S(1)}, u32[]{:S(2)}, u32[]{:S(2)}) collective-permute-start(f32[640,128]{1,0:T(8,128)S(1)} %collective-permute-done.25.refs_3_), channel_id=1, source_target_pairs={{0,1},{1,0},{2,3},{3,2},{4,5},{5,4},{6,7},{7,6},{8,9},{9,8},{10,11... | collective-permute-start | bytes 983048 | tf_op jit(solution)/shard_map/ppermute | solution.py:357

commit v3 on v2

--- a/solution.py
+++ b/solution.py
@@ -89,7 +89,7 @@
 
 
 def near_kernel(chunks, flip_high, flip_low, high, low, *outs):
-    for s in range(3):
+    for s in range(len(outs)):
 
         @pl.when(pl.program_id(0) == s)
         def _():
@@ -113,7 +113,7 @@
         grid_spec=pltpu.PrefetchScalarGridSpec(
             num_scalar_prefetch=2,
             grid=(1,),
-            in_specs=[pl.BlockSpec((BLK, W), lambda i, *p: (0, which))] * 8 + flip_specs("zy"[which], count),
+            in_specs=[whole((BLK, W))] * 8 + flip_specs("zy"[which], count),
             out_specs=[whole((count, W))] * 2 + [whole((2 * BLK, W))] * 2,
         ),
         out_shape=[pltpu.HBM((count, W), BF16)] * 2 + [jax.ShapeDtypeStruct((2 * BLK, W), F32)] * 2,
@@ -123,16 +123,16 @@
 
 
 def near_product(which, chunks, panel_high, panel_low, flip_high, flip_low):
-    count = flip_high.shape[-1]
+    count, number = flip_high.shape[-1], chunks.shape[0]
     return pl.pallas_call(
         near_kernel,
         grid_spec=pltpu.PrefetchScalarGridSpec(
             num_scalar_prefetch=1,
-            grid=(3,),
+            grid=(number,),
             in_specs=flip_specs("zy"[which], count) + [whole((count, W))] * 2,
-            out_specs=[whole((4 * BLK, W))] * 3,
+            out_specs=[whole((4 * BLK, W))] * number,
         ),
-        out_shape=[jax.ShapeDtypeStruct((4 * BLK, W), F32)] * 3,
+        out_shape=[jax.ShapeDtypeStruct((4 * BLK, W), F32)] * number,
         compiler_params=params(22),
         name="near",
     )(chunks, pinned(flip_high), pinned(flip_low), pinned(panel_high), pinned(panel_low))
@@ -306,13 +306,15 @@
     home_way = home_pairs()
 
     normal_one = mask_one * product(factor_one, inverse_one)
+    pieces_one = gather_row(normal_one)
     normal_top = product(factor_two_top, inverse_two)
     panel_two = mask_two * product(factor_two, inverse_two) - product(normal_one, normal_top)
-    pieces = gather_row(jnp.concatenate([normal_one, panel_two], axis=1))
-    trailing, pieces[0] = lax.optimization_barrier((trailing, pieces[0]))
+    pieces_two = gather_row(panel_two)
+    order = lax.optimization_barrier
+    trailing, pieces_one[0] = order((trailing, pieces_one[0]))
     flips = flipped(trailing, table([block_at(i // 4, i % 4, x, k) for i in range(16)]))
-    pieces, flips = lax.optimization_barrier((pieces, flips))
-    pieces += [lax.ppermute(piece, "col", SWAP) for piece in pieces]
+    pieces_one, flips = order((pieces_one, flips))
+    pieces_one += [lax.ppermute(piece, "col", SWAP) for piece in pieces_one]
 
     def forward(over):
         return lambda value: lax.ppermute(value, "row", row_ring(over, 1))
@@ -326,19 +328,25 @@
     def light(across, picks):
         return picks[0] + sum(lax.ppermute(picks[s], "row", row_ring(across, s)) for s in (1, 2, 3))
 
-    order = lax.optimization_barrier
-    high, low, top_one, bottom_one = far_product(0, chunks(z, [2]), places, pieces, *flips)
+    high, low, top_one, bottom_one = far_product(0, chunks(z, [2]), places, pieces_one, *flips)
+    top_one, bottom_one = forward("z")(top_one), backward("z")(bottom_one)
     panels = [high, low]
-    top_one, bottom_one = forward("z")(top_one), backward("z")(bottom_one)
-    high, low, top_two, bottom_two = far_product(1, chunks(y, [2]), places, pieces, *flips)
+    panels[0], pieces_two = order((panels[0], pieces_two))
+    pieces_two += [lax.ppermute(piece, "col", SWAP) for piece in pieces_two]
+    high, low, top_two, bottom_two = far_product(1, chunks(y, [2]), places, pieces_two, *flips)
     panels += [high, low]
     top_two, bottom_two = forward("y")(top_two), backward("y")(bottom_two)
-    ahead, behind, own_one = near_product(0, chunks(z, [1, 3, 0]), *panels[:2], *flips)
+    ahead_two, behind_two = near_product(1, chunks(y, [1, 3]), *panels[2:], *flips)
+    panels[0], ahead_two = order((panels[0], ahead_two))
+    ahead, behind = near_product(0, chunks(z, [1, 3]), *panels[:2], *flips)
+    ahead_two, behind_two = join(ahead_two, behind_two, top_two, bottom_two)
+    rest_two = (forward("y")(ahead_two), backward("y")(behind_two))
     ahead, behind = join(ahead, behind, top_one, bottom_one)
+    ahead, panels[1], panels[3] = order((ahead, panels[1], panels[3]))
     rest_one = (forward("z")(ahead), backward("z")(behind))
-    ahead, behind, own_two = near_product(1, chunks(y, [1, 3, 0]), *panels[2:], *flips)
-    ahead, behind = join(ahead, behind, top_two, bottom_two)
-    rest_two = (forward("y")(ahead), backward("y")(behind))
+    (own_one,) = near_product(0, chunks(z, [0]), *panels[:2], *flips)
+    (own_two,) = near_product(1, chunks(y, [0]), *panels[2:], *flips)
+
     own_one, own_two = order((own_one, own_two))
 
     sums_one = lax.ppermute(light("y", fold(y, own_one, *rest_one)), BOTH, home_way)

time: 211 us -> 202 us (0.957)
  waiting for transfers between devices: 60.3 us -> 35.9 us
  Pallas kernels: 45.2 us -> 52.6 us
  blocking collectives: 17.6 us -> 23.5 us
  local copies, waits for them, and re-layouts: 4.46 us -> 6.72 us
    ppermute x4, waiting for transfers between devices: 9.7 us -> 0.01 us  [backward(): return lambda value: lax.ppermute(value, 'row', row_ring(over, 3))]
    ppermute x1, waiting for transfers between devices: 12.2 us -> 4.15 us  [body(): lax.ppermute(light('z', fold(z, own_two, *rest_two)), BOTH, home_way)]
    ppermute x3 -> x6, waiting for transfers between devices: 11.4 us -> 3.84 us  [gather_row(): lax.ppermute(panel, 'col', col_ring(s))]
    all_to_all x1, blocking collectives: 17.6 us -> 23.5 us  [body(): part = lax.all_to_all(part, 'col', 0, 0, tiled=True)]
    pallas_call x2 -> x4, Pallas kernels: 16.4 us -> 22 us  [near_product(): pl.pallas_call(near_kernel, grid_spec=pltpu.PrefetchScalarGridSpec(num_sc...]
    ppermute x4, waiting for transfers between devices: 6.19 us -> 10.3 us  [forward(): return lambda value: lax.ppermute(value, 'row', row_ring(over, 1))]
    ppermute x1, starting transfers between devices: 6.95 us -> 3.05 us  [body(): lax.ppermute(light('z', fold(z, own_two, *rest_two)), BOTH, home_way)]
    ppermute x4 -> x8, waiting for transfers between devices: 3.32 us -> 0.02 us  [the longest x4 0.01 us: body(): pieces_two += [lax.ppermute(piece, 'col', SWAP) for piece in pieces_two]]
  transfers between devices with their start and end apart: 32 -> 39, of which waited for: 15 -> 9; matrix products, arithmetic and copies ran while one was open for 5% -> 6% of each run, Pallas kernels for 16% -> 23%
where the time goes in v3:
time: 202 us; the launch traced here: 201 us
  starting transfers between devices  64.2 us (32%)
  Pallas kernels  52.6 us (26%)
  waiting for transfers between devices  35.9 us (18%)
  blocking collectives  23.5 us (12%)
  matrix products  11.5 us (6%)
  local copies, waits for them, and re-layouts  6.72 us (3%)
  other arithmetic  4.49 us (2%)
  between operations  2.36 us (1%)
    all_to_all x1, blocking collectives, body(): part = lax.all_to_all(part, 'col', 0, 0, tiled=True)  23.5 us
    pallas_call x4, Pallas kernels, near_product(): pl.pallas_call(near_kernel, grid_spec=pltpu.PrefetchScalarGridSpec(num_sc...  22 us
    ppermute x4, starting transfers between devices, body(): strips += [lax.ppermute(piece, 'col', SWAP) for piece in strips]  13.6 us
    pallas_call x2, Pallas kernels, far_product(): pl.pallas_call(far_kernel, grid_spec=pltpu.PrefetchScalarGridSpec(num_sca...  10.5 us
    ppermute x4, waiting for transfers between devices, forward(): return lambda value: lax.ppermute(value, 'row', row_ring(over, 1))  10.3 us
    ppermute x4, starting transfers between devices, backward(): return lambda value: lax.ppermute(value, 'row', row_ring(over, 3))  9.44 us
    ppermute x6, starting transfers between devices, gather_row(): lax.ppermute(panel, 'col', col_ring(s))  7.97 us
    ppermute x6, starting transfers between devices, light(): lax.ppermute(picks[s], 'row', row_ring(across, s))  7.34 us
  transfers between devices with their start and end apart: 39, of which 9 were waited for; matrix products, arithmetic and copies ran while one was open for 6% of the time, Pallas kernels for 23%

profile of v3, /device:TPU:1, one launch (start us, length us, event | category | flops | bytes accessed | tf_op | source)
XLA Modules:
  0.0 201.2 jit_solution(2767400903241594034)
XLA Ops:
  0.7 1.4 compare_reduce_fusion.1
  2.7 1.7 convolution_multiply_fusion.1.refs_0_
  4.4 2.1 %collective-permute-start = (f32[128,512]{1,0:T(8,128)S(1)}, f32[128,512]{1,0:T(8,128)S(1)}, u32[]{:S(2)}, u32[]{:S(2)}) collective-permute-start(f32[128,512]{1,0:T(8,128)S(1)} %convolution_multiply_fusion.1.refs_0_), channel_id=1, source_target_pairs={{0,2},{1,3},{2,4},{3,5},{4,6},{5,7},{6,0},{7,1},{8,10},{9,11},{10,... | collective-permute-start | bytes 786440 | tf_op jit(solution)/shard_map/ppermute | solution.py:192
  6.5 1.3 collective-permute-start.1
  7.9 1.6 collective-permute-start.2
  11.6 3.4 %copy-done.1 = f32[1024,2048]{1,0:T(8,128)S(1)} copy-done((f32[1024,2048]{1,0:T(8,128)S(1)}, f32[1024,2048]{1,0:T(8,128)}, u32[]{:S(2)}) %copy-start.1) | copy-done | bytes 8388632
  15.0 7.1 %flip.1 = (bf16[4,4,128,1024]{3,2,1,0:T(8,128)(2,1)}, bf16[4,4,128,1024]{3,2,1,0:T(8,128)(2,1)}) custom-call(s32[16]{0:T(128)S(1)} %stack.152.blocks, f32[1024,2048]{1,0:T(8,128)S(1)} %copy-done.1, f32[1024,2048]{1,0:T(8,128)S(1)} %copy-done.1), custom_call_target="tpu_custom_call" | custom-call | tf_op jit(solution)/shard_map/flip/pallas_call | solution.py:59
  23.6 1.6 collective-permute-start.3
  26.6 2.4 %collective-permute-start.8 = (f32[128,512]{1,0:T(8,128)S(1)}, f32[128,512]{1,0:T(8,128)S(1)}, u32[]{:S(2)}, u32[]{:S(2)}) collective-permute-start(f32[128,512]{1,0:T(8,128)S(1)} %convolution_subtract_fusion.refs_0_), channel_id=1, source_target_pairs={{0,6},{1,7},{2,0},{3,1},{4,2},{5,3},{6,4},{7,5},{8,14},{9,15},{10,... | collective-permute-start | bytes 786440 | tf_op jit(solution)/shard_map/ppermute | solution.py:192
  30.9 5.3 %far.2 = (bf16[1024,512]{1,0:T(8,128)(2,1)}, bf16[1024,512]{1,0:T(8,128)(2,1)}, f32[256,512]{1,0:T(8,128)}, f32[256,512]{1,0:T(8,128)}) custom-call(s32[1]{0:T(128)} %bitcast.18.chunks, s32[8]{0:T(128)S(1)} %stack.162.places, f32[128,512]{1,0:T(8,128)S(1)} %convolution_multiply_fusion.1.refs_0_, f32[128,512]{1,0:T(8,128)S(1)} %collective-permute-done.refs_1_, ...), custom_call_target="tpu_custom_call" | custom-call | tf_op jit(solution)/shard_map/far/pallas_call | solution.py:111
  36.2 3.8 %collective-permute-done.9.refs_3_ = f32[128,512]{1,0:T(8,128)S(1)} collective-permute-done((f32[128,512]{1,0:T(8,128)S(1)}, f32[128,512]{1,0:T(8,128)S(1)}, u32[]{:S(2)}, u32[]{:S(2)}) %collective-permute-start.9) | collective-permute-done | bytes 262176 | tf_op jit(solution)/shard_map/ppermute | solution.py:192
  40.0 1.8 collective-permute-start.10
  42.5 1.6 collective-permute-start.14
  44.1 2.7 %collective-permute-start.15 = (f32[256,512]{1,0:T(8,128)}, f32[256,512]{1,0:T(8,128)}, u32[]{:S(2)}, u32[]{:S(2)}) collective-permute-start(f32[256,512]{1,0:T(8,128)} %get-tuple-element.78), channel_id=1, source_target_pairs={{0,96},{8,104},{16,112},{24,120},{32,0},{40,8},{48,16},{56,24},{64... | collective-permute-start | bytes 1572872 | tf_op jit(solution)/shard_map/ppermute | solution.py:323
  46.8 5.2 %far.3 = (bf16[1024,512]{1,0:T(8,128)(2,1)}, bf16[1024,512]{1,0:T(8,128)(2,1)}, f32[256,512]{1,0:T(8,128)}, f32[256,512]{1,0:T(8,128)}) custom-call(s32[1]{0:T(128)} %bitcast.29.chunks, s32[8]{0:T(128)S(1)} %stack.162.places, f32[128,512]{1,0:T(8,128)S(1)} %convolution_subtract_fusion.refs_0_, f32[128,512]{1,0:T(8,128)S(1)} %collective-permute-done.7.refs_1_, ...), custom_call_target="tpu_custom_call" | custom-call | tf_op jit(solution)/shard_map/far/pallas_call | solution.py:111
  53.3 1.4 collective-permute-start.23
  54.9 6.4 %near.4 = (f32[512,512]{1,0:T(8,128)S(1)}, f32[512,512]{1,0:T(8,128)S(1)}) custom-call(s32[2]{0:T(128)S(1)} %pad_add_fusion.chunks, bf16[4,4,128,1024]{3,2,1,0:T(8,128)(2,1)} %get-tuple-element.58.refs_8_.flip_high, bf16[4,4,128,1024]{3,2,1,0:T(8,128)(2,1)} %get-tuple-element.59.refs_9_.flip_low, bf16[1024,512]{1,0:T(8,128)(2,1)} %get-tuple-element.70.high.high_two, ...), custom_call_target="tpu_custom_call" | custom-call | tf_op jit(solution)/shard_map/near/pallas_call | solution.py:127
  61.3 7.7 %near.5 = (f32[512,512]{1,0:T(8,128)}, f32[512,512]{1,0:T(8,128)}) custom-call(s32[2]{0:T(128)S(1)} %pad_add_fusion.1.chunks, bf16[4,4,128,1024]{3,2,1,0:T(8,128)(2,1)} %get-tuple-element.58.refs_8_.flip_high, bf16[4,4,128,1024]{3,2,1,0:T(8,128)(2,1)} %get-tuple-element.59.refs_9_.flip_low, bf16[1024,512]{1,0:T(8,128)(2,1)} %get-tuple-element.73.high.high_one, ...), custom_call_target="tpu_custom_call" | custom-call | tf_op jit(solution)/shard_map/near/pallas_call | solution.py:127
  69.0 2.6 %join.2 = (f32[512,512]{1,0:T(8,128)}, f32[512,512]{1,0:T(8,128)}) custom-call(f32[512,512]{1,0:T(8,128)} %get-tuple-element.75.ahead, f32[512,512]{1,0:T(8,128)} %get-tuple-element.76.behind, f32[256,512]{1,0:T(8,128)} %collective-permute-done.14.top, f32[256,512]{1,0:T(8,128)} %collective-permute-done.15.bottom), custom_call_target="tpu_custom_call", output_to_operand_aliasing={{0}: (0, {}), {1}: (1, {})} | custom-call | tf_op jit(solution)/shard_map/join/pallas_call | solution.py:149
  71.6 2.7 %collective-permute-start.17 = (f32[512,512]{1,0:T(8,128)}, f32[512,512]{1,0:T(8,128)}, u32[]{:S(2)}, u32[]{:S(2)}) collective-permute-start(f32[512,512]{1,0:T(8,128)} %get-tuple-element.84), channel_id=1, source_target_pairs={{0,96},{8,104},{16,112},{24,120},{32,0},{40,8},{48,16},{56,24},{64... | collective-permute-start | bytes 3145736 | tf_op jit(solution)/shard_map/ppermute | solution.py:323
  74.3 1.4 join.3
  75.8 2.7 %collective-permute-start.25 = (f32[512,512]{1,0:T(8,128)S(1)}, f32[512,512]{1,0:T(8,128)}, u32[]{:S(2)}, u32[]{:S(2)}) collective-permute-start(f32[512,512]{1,0:T(8,128)S(1)} %get-tuple-element.95), channel_id=1, source_target_pairs={{0,24},{8,0},{16,8},{24,16},{32,56},{40,32},{48,40},{56,48},{64,88... | collective-permute-start | bytes 3145736 | tf_op jit(solution)/shard_map/ppermute | solution.py:323
  78.4 4.0 %near.7.own = f32[512,512]{1,0:T(8,128)S(1)} custom-call(s32[1]{0:T(128)} %bitcast.32.chunks, bf16[4,4,128,1024]{3,2,1,0:T(8,128)(2,1)} %get-tuple-element.58.refs_8_.flip_high, bf16[4,4,128,1024]{3,2,1,0:T(8,128)(2,1)} %get-tuple-element.59.refs_9_.flip_low, bf16[1024,512]{1,0:T(8,128)(2,1)} %get-tuple-element.70.high.high_two, ...), custom_call_target="tpu_custom_call" | custom-call | tf_op jit(solution)/shard_map/near/pallas_call | solution.py:127
  82.4 4.0 %near.6.own = f32[512,512]{1,0:T(8,128)S(1)} custom-call(s32[1]{0:T(128)} %bitcast.1.chunks, bf16[4,4,128,1024]{3,2,1,0:T(8,128)(2,1)} %get-tuple-element.58.refs_8_.flip_high, bf16[4,4,128,1024]{3,2,1,0:T(8,128)(2,1)} %get-tuple-element.59.refs_9_.flip_low, bf16[1024,512]{1,0:T(8,128)(2,1)} %get-tuple-element.73.high.high_one, ...), custom_call_target="tpu_custom_call" | custom-call | tf_op jit(solution)/shard_map/near/pallas_call | solution.py:127
  86.3 10.3 %collective-permute-done.16.one = f32[512,512]{1,0:T(8,128)} collective-permute-done((f32[512,512]{1,0:T(8,128)}, f32[512,512]{1,0:T(8,128)}, u32[]{:S(2)}, u32[]{:S(2)}) %collective-permute-start.16) | collective-permute-done | bytes 1048608 | tf_op jit(solution)/shard_map/ppermute | solution.py:320
  96.6 1.8 fold.2
  98.6 2.6 %collective-permute-start.19 = (f32[128,512]{1,0:T(8,128)S(1)}, f32[128,512]{1,0:T(8,128)S(1)}, u32[]{:S(2)}, u32[]{:S(2)}) collective-permute-start(f32[128,512]{1,0:T(8,128)S(1)} %get-tuple-element.87), channel_id=1, source_target_pairs={{0,16},{8,24},{16,0},{24,8},{32,48},{40,56},{48,32},{56,40},{64,80... | collective-permute-start | bytes 786440 | tf_op jit(solution)/shard_map/ppermute | solution.py:329
  102.2 1.8 fold.3
  104.1 3.6 %collective-permute-start.27 = (f32[128,512]{1,0:T(8,128)S(1)}, f32[128,512]{1,0:T(8,128)S(1)}, u32[]{:S(2)}, u32[]{:S(2)}) collective-permute-start(f32[128,512]{1,0:T(8,128)S(1)} %get-tuple-element.98), channel_id=1, source_target_pairs={{0,64},{8,72},{16,80},{24,88},{32,96},{40,104},{48,112},{56,120},{... | collective-permute-start | bytes 786440 | tf_op jit(solution)/shard_map/ppermute | solution.py:329
  107.7 3.3 %collective-permute-done.19 = f32[128,512]{1,0:T(8,128)S(1)} collective-permute-done((f32[128,512]{1,0:T(8,128)S(1)}, f32[128,512]{1,0:T(8,128)S(1)}, u32[]{:S(2)}, u32[]{:S(2)}) %collective-permute-start.19) | collective-permute-done | bytes 262176 | tf_op jit(solution)/shard_map/ppermute | solution.py:329
  110.9 1.7 collective-permute-done.20
  112.7 5.3 %collective-permute-start.21 = (f32[128,512]{1,0:T(8,128)S(1)}, f32[128,512]{1,0:T(8,128)S(1)}, u32[]{:S(2)}, u32[]{:S(2)}) collective-permute-start(f32[128,512]{1,0:T(8,128)S(1)} %add_add_fusion.1), channel_id=1, source_target_pairs={{0,0},{1,25},{2,34},{3,59},{4,68},{5,93},{6,102},{7,127},{8,8},{9,... | collective-permute-start | bytes 786440 | tf_op jit(solution)/shard_map/ppermute | solution.py:352
  118.2 3.1 %collective-permute-start.29 = (f32[128,512]{1,0:T(8,128)S(1)}, f32[128,512]{1,0:T(8,128)S(1)}, u32[]{:S(2)}, u32[]{:S(2)}) collective-permute-start(f32[128,512]{1,0:T(8,128)S(1)} %add_add_fusion), channel_id=1, source_target_pairs={{0,0},{1,25},{2,34},{3,59},{4,68},{5,93},{6,102},{7,127},{8,8},{9,... | collective-permute-start | bytes 786440 | tf_op jit(solution)/shard_map/ppermute | solution.py:353
  121.2 1.7 collective-permute-done.21
  123.1 4.2 %collective-permute-done.29 = f32[128,512]{1,0:T(8,128)S(1)} collective-permute-done((f32[128,512]{1,0:T(8,128)S(1)}, f32[128,512]{1,0:T(8,128)S(1)}, u32[]{:S(2)}, u32[]{:S(2)}) %collective-permute-start.29) | collective-permute-done | bytes 262176 | tf_op jit(solution)/shard_map/ppermute | solution.py:353
  127.9 23.5 %all_to_all.15.part = f32[8,128,128]{2,1,0:T(8,128)S(1)} all-to-all(f32[8,128,128]{2,1,0:T(8,128)S(1)} %fusion), channel_id=1, replica_groups=mesh['row'=16,'col'=8] {'col'}, dimensions={0} | all-to-all | bytes 1048576 | tf_op jit(solution)/shard_map/all_to_all | solution.py:362
  151.5 2.6 %strip.1 = f32[640,128]{1,0:T(8,128)} custom-call(s32[1]{0:T(128)} %bitcast.33.col, f32[8,128,128]{2,1,0:T(8,128)S(1)} %all_to_all.15.part, bf16[1024,512]{1,0:T(8,128)(2,1)S(1)} %copy-done.2, bf16[1024,512]{1,0:T(8,128)(2,1)S(1)} %copy-done.3, bf16[1024,512]{1,0:T(8,128)(2,1)S(1)} %copy-done.4, bf16[1024,512]{1,0:T(8,128)(2,1)S(1)} %copy-done.5), custom_call_target="tpu_custom_call" | custom-call | tf_op jit(solution)/shard_map/strip/pallas_call | solution.py:237
  154.1 3.6 %all-to-all-start.1 = ((f32[16,40,128]{2,1,0:T(8,128)}), f32[16,40,128]{2,1,0:T(8,128)S(1)}, u32[]{:S(2)}, u32[]{:S(2)}) async-start(f32[16,40,128]{2,1,0:T(8,128)} %bitcast.43), calls=%async_computation.1 | async-start | bytes 655360 | tf_op jit(solution)/shard_map/all_to_all | solution.py:250
  158.7 7.0 %all-to-all-done.1 = f32[16,40,128]{2,1,0:T(8,128)S(1)} async-done(((f32[16,40,128]{2,1,0:T(8,128)}), f32[16,40,128]{2,1,0:T(8,128)S(1)}, u32[]{:S(2)}, u32[]{:S(2)}) %all-to-all-start.1) | async-done | bytes 327712 | tf_op jit(solution)/shard_map/all_to_all | solution.py:250
  166.5 3.5 %all-to-all-start.2 = ((f32[16,40,128]{2,1,0:T(8,128)}), f32[16,40,128]{2,1,0:T(8,128)S(1)}, u32[]{:S(2)}, u32[]{:S(2)}) async-start(f32[16,40,128]{2,1,0:T(8,128)} %broadcast_in_dim.2), calls=%async_computation.2 | async-start | bytes 655360 | tf_op jit(solution)/shard_map/all_to_all | solution.py:252
  170.0 2.0 fusion.11
  172.0 2.2 %fusion.10.refs_9_ = f32[512,512]{1,0:T(8,128)S(1)} fusion(f32[512,512]{1,0:T(8,128)S(1)} %fusion.9.refs_8_, f32[512,512]{1,0:T(8,128)} %copy-done.8), kind=kOutput, calls=%fused_computation.30 | convolution fusion | flops 805306368 | bytes 3145728 | tf_op jit(solution)/shard_map/dot_general | solution.py:19
  174.3 3.6 %all-to-all-done.2 = f32[16,40,128]{2,1,0:T(8,128)S(1)} async-done(((f32[16,40,128]{2,1,0:T(8,128)}), f32[16,40,128]{2,1,0:T(8,128)S(1)}, u32[]{:S(2)}, u32[]{:S(2)}) %all-to-all-start.2) | async-done | bytes 327712 | tf_op jit(solution)/shard_map/all_to_all | solution.py:252
  178.2 2.4 %collective-permute-start.31 = (f32[640,128]{1,0:T(8,128)S(1)}, f32[640,128]{1,0:T(8,128)S(1)}, u32[]{:S(2)}, u32[]{:S(2)}) collective-permute-start(f32[640,128]{1,0:T(8,128)S(1)} %bitcast.86), channel_id=1, source_target_pairs={{0,6},{1,7},{2,0},{3,1},{4,2},{5,3},{6,4},{7,5},{8,14},{9,15},{10,... | collective-permute-start | bytes 983048 | tf_op jit(solution)/shard_map/ppermute | solution.py:364
  180.6 2.6 %convolution_add_fusion.refs_10_ = f32[512,512]{1,0:T(8,128)S(1)} fusion(f32[512,512]{1,0:T(8,128)} %fusion.11, f32[512,512]{1,0:T(8,128)} %copy-done.8, f32[512,512]{1,0:T(8,128)S(1)} %fusion.10.refs_9_), kind=kOutput, calls=%fused_computation | convolution fusion | flops 805568512 | bytes 4194304 | tf_op jit(solution)/shard_map/dot_general | solution.py:23
  183.2 4.1 %collective-permute-start.33 = (f32[640,128]{1,0:T(8,128)S(1)}, f32[640,128]{1,0:T(8,128)S(1)}, u32[]{:S(2)}, u32[]{:S(2)}) collective-permute-start(f32[640,128]{1,0:T(8,128)S(1)} %bitcast.88), channel_id=1, source_target_pairs={{0,1},{1,0},{2,3},{3,2},{4,5},{5,4},{6,7},{7,6},{8,9},{9,8},{10,11... | collective-permute-start | bytes 983048 | tf_op jit(solution)/shard_map/ppermute | solution.py:365
  187.3 9.0 %collective-permute-start.34 = (f32[640,128]{1,0:T(8,128)S(1)}, f32[640,128]{1,0:T(8,128)S(1)}, u32[]{:S(2)}, u32[]{:S(2)}) collective-permute-start(f32[640,128]{1,0:T(8,128)S(1)} %collective-permute-done.30.refs_1_), channel_id=1, source_target_pairs={{0,1},{1,0},{2,3},{3,2},{4,5},{5,4},{6,7},{7,6},{8,9},{9,8},{10,11... | collective-permute-start | bytes 983048 | tf_op jit(solution)/shard_map/ppermute | solution.py:365
  198.4 2.8 %finish.1 = (f32[512,512]{1,0:T(8,128)}, f32[512,512]{1,0:T(8,128)}, f32[512,512]{1,0:T(8,128)}) custom-call(s32[8]{0:T(128)S(1)} %stack.162.places, f32[640,128]{1,0:T(8,128)S(1)} %bitcast.89, f32[640,128]{1,0:T(8,128)S(1)} %collective-permute-done.30.refs_1_, f32[640,128]{1,0:T(8,128)S(1)} %collective-permute-done.31.refs_2_, ...), custom_call_target="tpu_custom_call" | custom-call | tf_op jit(solution)/shard_map/finish/pallas_call | solution.py:279
  (104 shorter events, 14.8 us)
Async XLA Ops:
  0.6 21.5 %copy-start = (f32[512,512]{1,0:T(8,128)S(1)}, f32[512,512]{1,0:T(8,128)}, u32[]{:S(2)}) copy-start(f32[512,512]{1,0:T(8,128)} %param.13) | copy-start | bytes 3145732
  4.4 19.2 %collective-permute-start = (f32[128,512]{1,0:T(8,128)S(1)}, f32[128,512]{1,0:T(8,128)S(1)}, u32[]{:S(2)}, u32[]{:S(2)}) collective-permute-start(f32[128,512]{1,0:T(8,128)S(1)} %convolution_multiply_fusion.1.refs_0_), channel_id=1, source_target_pairs={{0,2},{1,3},{2,4},{3,5},{4,6},{5,7},{6,0},{7,1},{8,10},{9,11},{10,... | collective-permute-start | bytes 786440 | tf_op jit(solution)/shard_map/ppermute | solution.py:192
  6.5 17.1 %collective-permute-start.1 = (f32[128,512]{1,0:T(8,128)S(1)}, f32[128,512]{1,0:T(8,128)S(1)}, u32[]{:S(2)}, u32[]{:S(2)}) collective-permute-start(f32[128,512]{1,0:T(8,128)S(1)} %convolution_multiply_fusion.1.refs_0_), channel_id=1, source_target_pairs={{0,6},{1,7},{2,0},{3,1},{4,2},{5,3},{6,4},{7,5},{8,14},{9,15},{10,... | collective-permute-start | bytes 786440 | tf_op jit(solution)/shard_map/ppermute | solution.py:192
  7.9 15.7 %collective-permute-start.2 = (f32[128,512]{1,0:T(8,128)S(1)}, f32[128,512]{1,0:T(8,128)S(1)}, u32[]{:S(2)}, u32[]{:S(2)}) collective-permute-start(f32[128,512]{1,0:T(8,128)S(1)} %convolution_multiply_fusion.1.refs_0_), channel_id=1, source_target_pairs={{0,4},{1,5},{2,6},{3,7},{4,0},{5,1},{6,2},{7,3},{8,12},{9,13},{10,... | collective-permute-start | bytes 786440 | tf_op jit(solution)/shard_map/ppermute | solution.py:192
  15.0 8.2 %copy-start.15 = (f32[128,512]{1,0:T(8,128)S(1)}, f32[128,512]{1,0:T(8,128)}, u32[]{:S(2)}) copy-start(f32[128,512]{1,0:T(8,128)} %param.12) | copy-start | bytes 786436
  23.6 3.0 %collective-permute-start.3 = (f32[128,512]{1,0:T(8,128)S(1)}, f32[128,512]{1,0:T(8,128)S(1)}, u32[]{:S(2)}, u32[]{:S(2)}) collective-permute-start(f32[128,512]{1,0:T(8,128)S(1)} %convolution_multiply_fusion.1.refs_0_), channel_id=1, source_target_pairs={{0,1},{1,0},{2,3},{3,2},{4,5},{5,4},{6,7},{7,6},{8,9},{9,8},{10,11... | collective-permute-start | bytes 786440 | tf_op jit(solution)/shard_map/ppermute | solution.py:317
  25.2 3.8 %collective-permute-start.4 = (f32[128,512]{1,0:T(8,128)S(1)}, f32[128,512]{1,0:T(8,128)S(1)}, u32[]{:S(2)}, u32[]{:S(2)}) collective-permute-start(f32[128,512]{1,0:T(8,128)S(1)} %collective-permute-done.refs_1_), channel_id=1, source_target_pairs={{0,1},{1,0},{2,3},{3,2},{4,5},{5,4},{6,7},{7,6},{8,9},{9,8},{10,11... | collective-permute-start | bytes 786440 | tf_op jit(solution)/shard_map/ppermute | solution.py:317
  25.3 4.6 %collective-permute-start.5 = (f32[128,512]{1,0:T(8,128)S(1)}, f32[128,512]{1,0:T(8,128)}, u32[]{:S(2)}, u32[]{:S(2)}) collective-permute-start(f32[128,512]{1,0:T(8,128)S(1)} %collective-permute-done.1.refs_2_), channel_id=1, source_target_pairs={{0,1},{1,0},{2,3},{3,2},{4,5},{5,4},{6,7},{7,6},{8,9},{9,8},{10,11... | collective-permute-start | bytes 786440 | tf_op jit(solution)/shard_map/ppermute | solution.py:317
  25.7 4.2 %collective-permute-start.6 = (f32[128,512]{1,0:T(8,128)S(1)}, f32[128,512]{1,0:T(8,128)}, u32[]{:S(2)}, u32[]{:S(2)}) collective-permute-start(f32[128,512]{1,0:T(8,128)S(1)} %collective-permute-done.2.refs_3_), channel_id=1, source_target_pairs={{0,1},{1,0},{2,3},{3,2},{4,5},{5,4},{6,7},{7,6},{8,9},{9,8},{10,11... | collective-permute-start | bytes 786440 | tf_op jit(solution)/shard_map/ppermute | solution.py:317
  26.3 9.9 %collective-permute-start.7 = (f32[128,512]{1,0:T(8,128)S(1)}, f32[128,512]{1,0:T(8,128)S(1)}, u32[]{:S(2)}, u32[]{:S(2)}) collective-permute-start(f32[128,512]{1,0:T(8,128)S(1)} %convolution_subtract_fusion.refs_0_), channel_id=1, source_target_pairs={{0,2},{1,3},{2,4},{3,5},{4,6},{5,7},{6,0},{7,1},{8,10},{9,11},{10,... | collective-permute-start | bytes 786440 | tf_op jit(solution)/shard_map/ppermute | solution.py:192
  26.6 9.6 %collective-permute-start.8 = (f32[128,512]{1,0:T(8,128)S(1)}, f32[128,512]{1,0:T(8,128)S(1)}, u32[]{:S(2)}, u32[]{:S(2)}) collective-permute-start(f32[128,512]{1,0:T(8,128)S(1)} %convolution_subtract_fusion.refs_0_), channel_id=1, source_target_pairs={{0,6},{1,7},{2,0},{3,1},{4,2},{5,3},{6,4},{7,5},{8,14},{9,15},{10,... | collective-permute-start | bytes 786440 | tf_op jit(solution)/shard_map/ppermute | solution.py:192
  29.7 10.3 %collective-permute-start.9 = (f32[128,512]{1,0:T(8,128)S(1)}, f32[128,512]{1,0:T(8,128)S(1)}, u32[]{:S(2)}, u32[]{:S(2)}) collective-permute-start(f32[128,512]{1,0:T(8,128)S(1)} %convolution_subtract_fusion.refs_0_), channel_id=1, source_target_pairs={{0,4},{1,5},{2,6},{3,7},{4,0},{5,1},{6,2},{7,3},{8,12},{9,13},{10,... | collective-permute-start | bytes 786440 | tf_op jit(solution)/shard_map/ppermute | solution.py:192
  40.0 4.1 %collective-permute-start.10 = (f32[128,512]{1,0:T(8,128)S(1)}, f32[128,512]{1,0:T(8,128)S(1)}, u32[]{:S(2)}, u32[]{:S(2)}) collective-permute-start(f32[128,512]{1,0:T(8,128)S(1)} %convolution_subtract_fusion.refs_0_), channel_id=1, source_target_pairs={{0,1},{1,0},{2,3},{3,2},{4,5},{5,4},{6,7},{7,6},{8,9},{9,8},{10,11... | collective-permute-start | bytes 786440 | tf_op jit(solution)/shard_map/ppermute | solution.py:335
  41.9 4.9 %collective-permute-start.11 = (f32[128,512]{1,0:T(8,128)S(1)}, f32[128,512]{1,0:T(8,128)S(1)}, u32[]{:S(2)}, u32[]{:S(2)}) collective-permute-start(f32[128,512]{1,0:T(8,128)S(1)} %collective-permute-done.7.refs_1_), channel_id=1, source_target_pairs={{0,1},{1,0},{2,3},{3,2},{4,5},{5,4},{6,7},{7,6},{8,9},{9,8},{10,11... | collective-permute-start | bytes 786440 | tf_op jit(solution)/shard_map/ppermute | solution.py:335
  42.0 4.8 %collective-permute-start.12 = (f32[128,512]{1,0:T(8,128)S(1)}, f32[128,512]{1,0:T(8,128)S(1)}, u32[]{:S(2)}, u32[]{:S(2)}) collective-permute-start(f32[128,512]{1,0:T(8,128)S(1)} %collective-permute-done.8.refs_2_), channel_id=1, source_target_pairs={{0,1},{1,0},{2,3},{3,2},{4,5},{5,4},{6,7},{7,6},{8,9},{9,8},{10,11... | collective-permute-start | bytes 786440 | tf_op jit(solution)/shard_map/ppermute | solution.py:335
  42.4 4.4 %collective-permute-start.13 = (f32[128,512]{1,0:T(8,128)S(1)}, f32[128,512]{1,0:T(8,128)S(1)}, u32[]{:S(2)}, u32[]{:S(2)}) collective-permute-start(f32[128,512]{1,0:T(8,128)S(1)} %collective-permute-done.9.refs_3_), channel_id=1, source_target_pairs={{0,1},{1,0},{2,3},{3,2},{4,5},{5,4},{6,7},{7,6},{8,9},{9,8},{10,11... | collective-permute-start | bytes 786440 | tf_op jit(solution)/shard_map/ppermute | solution.py:335
  42.5 26.5 %collective-permute-start.14 = (f32[256,512]{1,0:T(8,128)}, f32[256,512]{1,0:T(8,128)}, u32[]{:S(2)}, u32[]{:S(2)}) collective-permute-start(f32[256,512]{1,0:T(8,128)} %get-tuple-element.77), channel_id=1, source_target_pairs={{0,32},{8,40},{16,48},{24,56},{32,64},{40,72},{48,80},{56,88},{64,... | collective-permute-start | bytes 1572872 | tf_op jit(solution)/shard_map/ppermute | solution.py:320
  44.1 24.9 %collective-permute-start.15 = (f32[256,512]{1,0:T(8,128)}, f32[256,512]{1,0:T(8,128)}, u32[]{:S(2)}, u32[]{:S(2)}) collective-permute-start(f32[256,512]{1,0:T(8,128)} %get-tuple-element.78), channel_id=1, source_target_pairs={{0,96},{8,104},{16,112},{24,120},{32,0},{40,8},{48,16},{56,24},{64... | collective-permute-start | bytes 1572872 | tf_op jit(solution)/shard_map/ppermute | solution.py:323
  52.0 22.3 %collective-permute-start.22 = (f32[256,512]{1,0:T(8,128)}, f32[256,512]{1,0:T(8,128)}, u32[]{:S(2)}, u32[]{:S(2)}) collective-permute-start(f32[256,512]{1,0:T(8,128)} %get-tuple-element.92), channel_id=1, source_target_pairs={{0,8},{8,16},{16,24},{24,0},{32,40},{40,48},{48,56},{56,32},{64,72... | collective-permute-start | bytes 1572872 | tf_op jit(solution)/shard_map/ppermute | solution.py:320
  53.3 21.0 %collective-permute-start.23 = (f32[256,512]{1,0:T(8,128)}, f32[256,512]{1,0:T(8,128)}, u32[]{:S(2)}, u32[]{:S(2)}) collective-permute-start(f32[256,512]{1,0:T(8,128)} %get-tuple-element.93), channel_id=1, source_target_pairs={{0,24},{8,0},{16,8},{24,16},{32,56},{40,32},{48,40},{56,48},{64,88... | collective-permute-start | bytes 1572872 | tf_op jit(solution)/shard_map/ppermute | solution.py:323
  71.6 25.0 %collective-permute-start.16 = (f32[512,512]{1,0:T(8,128)}, f32[512,512]{1,0:T(8,128)}, u32[]{:S(2)}, u32[]{:S(2)}) collective-permute-start(f32[512,512]{1,0:T(8,128)} %get-tuple-element.83), channel_id=1, source_target_pairs={{0,32},{8,40},{16,48},{24,56},{32,64},{40,72},{48,80},{56,88},{64,... | collective-permute-start | bytes 3145736 | tf_op jit(solution)/shard_map/ppermute | solution.py:320
  71.6 25.0 %collective-permute-start.17 = (f32[512,512]{1,0:T(8,128)}, f32[512,512]{1,0:T(8,128)}, u32[]{:S(2)}, u32[]{:S(2)}) collective-permute-start(f32[512,512]{1,0:T(8,128)} %get-tuple-element.84), channel_id=1, source_target_pairs={{0,96},{8,104},{16,112},{24,120},{32,0},{40,8},{48,16},{56,24},{64... | collective-permute-start | bytes 3145736 | tf_op jit(solution)/shard_map/ppermute | solution.py:323
  75.7 26.5 %collective-permute-start.24 = (f32[512,512]{1,0:T(8,128)S(1)}, f32[512,512]{1,0:T(8,128)}, u32[]{:S(2)}, u32[]{:S(2)}) collective-permute-start(f32[512,512]{1,0:T(8,128)S(1)} %get-tuple-element.94), channel_id=1, source_target_pairs={{0,8},{8,16},{16,24},{24,0},{32,40},{40,48},{48,56},{56,32},{64,72... | collective-permute-start | bytes 3145736 | tf_op jit(solution)/shard_map/ppermute | solution.py:320
  75.8 26.4 %collective-permute-start.25 = (f32[512,512]{1,0:T(8,128)S(1)}, f32[512,512]{1,0:T(8,128)}, u32[]{:S(2)}, u32[]{:S(2)}) collective-permute-start(f32[512,512]{1,0:T(8,128)S(1)} %get-tuple-element.95), channel_id=1, source_target_pairs={{0,24},{8,0},{16,8},{24,16},{32,56},{40,32},{48,40},{56,48},{64,88... | collective-permute-start | bytes 3145736 | tf_op jit(solution)/shard_map/ppermute | solution.py:323
  98.4 53.0 %copy-start.2 = (bf16[1024,512]{1,0:T(8,128)(2,1)S(1)}, bf16[1024,512]{1,0:T(8,128)(2,1)}, u32[]{:S(2)}) copy-start(bf16[1024,512]{1,0:T(8,128)(2,1)} %get-tuple-element.73.high.high_one) | copy-start | bytes 3145732
  98.4 53.0 %copy-start.3 = (bf16[1024,512]{1,0:T(8,128)(2,1)S(1)}, bf16[1024,512]{1,0:T(8,128)(2,1)}, u32[]{:S(2)}) copy-start(bf16[1024,512]{1,0:T(8,128)(2,1)} %get-tuple-element.80.low.low_one) | copy-start | bytes 3145732
  98.5 53.0 %copy-start.4 = (bf16[1024,512]{1,0:T(8,128)(2,1)S(1)}, bf16[1024,512]{1,0:T(8,128)(2,1)}, u32[]{:S(2)}) copy-start(bf16[1024,512]{1,0:T(8,128)(2,1)} %get-tuple-element.70.high.high_two) | copy-start | bytes 3145732
  98.5 53.0 %copy-start.5 = (bf16[1024,512]{1,0:T(8,128)(2,1)S(1)}, bf16[1024,512]{1,0:T(8,128)(2,1)}, u32[]{:S(2)}) copy-start(bf16[1024,512]{1,0:T(8,128)(2,1)} %get-tuple-element.81.low.low_two) | copy-start | bytes 3145732
  98.5 9.2 %collective-permute-start.18 = (f32[128,512]{1,0:T(8,128)S(1)}, f32[128,512]{1,0:T(8,128)S(1)}, u32[]{:S(2)}, u32[]{:S(2)}) collective-permute-start(f32[128,512]{1,0:T(8,128)S(1)} %get-tuple-element.86), channel_id=1, source_target_pairs={{0,8},{8,16},{16,24},{24,0},{32,40},{40,48},{48,56},{56,32},{64,72... | collective-permute-start | bytes 786440 | tf_op jit(solution)/shard_map/ppermute | solution.py:329
  98.6 12.4 %collective-permute-start.19 = (f32[128,512]{1,0:T(8,128)S(1)}, f32[128,512]{1,0:T(8,128)S(1)}, u32[]{:S(2)}, u32[]{:S(2)}) collective-permute-start(f32[128,512]{1,0:T(8,128)S(1)} %get-tuple-element.87), channel_id=1, source_target_pairs={{0,16},{8,24},{16,0},{24,8},{32,48},{40,56},{48,32},{56,40},{64,80... | collective-permute-start | bytes 786440 | tf_op jit(solution)/shard_map/ppermute | solution.py:329
  101.1 11.5 %collective-permute-start.20 = (f32[128,512]{1,0:T(8,128)S(1)}, f32[128,512]{1,0:T(8,128)S(1)}, u32[]{:S(2)}, u32[]{:S(2)}) collective-permute-start(f32[128,512]{1,0:T(8,128)S(1)} %get-tuple-element.88), channel_id=1, source_target_pairs={{0,24},{8,0},{16,8},{24,16},{32,56},{40,32},{48,40},{56,48},{64,88... | collective-permute-start | bytes 786440 | tf_op jit(solution)/shard_map/ppermute | solution.py:329
  104.0 14.1 %collective-permute-start.26 = (f32[128,512]{1,0:T(8,128)S(1)}, f32[128,512]{1,0:T(8,128)S(1)}, u32[]{:S(2)}, u32[]{:S(2)}) collective-permute-start(f32[128,512]{1,0:T(8,128)S(1)} %get-tuple-element.97), channel_id=1, source_target_pairs={{0,32},{8,40},{16,48},{24,56},{32,64},{40,72},{48,80},{56,88},{64,... | collective-permute-start | bytes 786440 | tf_op jit(solution)/shard_map/ppermute | solution.py:329
  104.1 14.0 %collective-permute-start.27 = (f32[128,512]{1,0:T(8,128)S(1)}, f32[128,512]{1,0:T(8,128)S(1)}, u32[]{:S(2)}, u32[]{:S(2)}) collective-permute-start(f32[128,512]{1,0:T(8,128)S(1)} %get-tuple-element.98), channel_id=1, source_target_pairs={{0,64},{8,72},{16,80},{24,88},{32,96},{40,104},{48,112},{56,120},{... | collective-permute-start | bytes 786440 | tf_op jit(solution)/shard_map/ppermute | solution.py:329
  107.6 10.4 %collective-permute-start.28 = (f32[128,512]{1,0:T(8,128)S(1)}, f32[128,512]{1,0:T(8,128)S(1)}, u32[]{:S(2)}, u32[]{:S(2)}) collective-permute-start(f32[128,512]{1,0:T(8,128)S(1)} %get-tuple-element.99), channel_id=1, source_target_pairs={{0,96},{8,104},{16,112},{24,120},{32,0},{40,8},{48,16},{56,24},{64... | collective-permute-start | bytes 786440 | tf_op jit(solution)/shard_map/ppermute | solution.py:329
  112.7 10.3 %collective-permute-start.21 = (f32[128,512]{1,0:T(8,128)S(1)}, f32[128,512]{1,0:T(8,128)S(1)}, u32[]{:S(2)}, u32[]{:S(2)}) collective-permute-start(f32[128,512]{1,0:T(8,128)S(1)} %add_add_fusion.1), channel_id=1, source_target_pairs={{0,0},{1,25},{2,34},{3,59},{4,68},{5,93},{6,102},{7,127},{8,8},{9,... | collective-permute-start | bytes 786440 | tf_op jit(solution)/shard_map/ppermute | solution.py:352
  118.2 39.5 %copy-start.9 = (f32[512,512]{1,0:T(8,128)S(1)}, f32[512,512]{1,0:T(8,128)}, u32[]{:S(2)}) copy-start(f32[512,512]{1,0:T(8,128)} %param.10) | copy-start | bytes 3145732
  118.2 9.0 %collective-permute-start.29 = (f32[128,512]{1,0:T(8,128)S(1)}, f32[128,512]{1,0:T(8,128)S(1)}, u32[]{:S(2)}, u32[]{:S(2)}) collective-permute-start(f32[128,512]{1,0:T(8,128)S(1)} %add_add_fusion), channel_id=1, source_target_pairs={{0,0},{1,25},{2,34},{3,59},{4,68},{5,93},{6,102},{7,127},{8,8},{9,... | collective-permute-start | bytes 786440 | tf_op jit(solution)/shard_map/ppermute | solution.py:353
  154.1 11.6 %all-to-all-start.1 = ((f32[16,40,128]{2,1,0:T(8,128)}), f32[16,40,128]{2,1,0:T(8,128)S(1)}, u32[]{:S(2)}, u32[]{:S(2)}) async-start(f32[16,40,128]{2,1,0:T(8,128)} %bitcast.43), calls=%async_computation.1 | async-start | bytes 655360 | tf_op jit(solution)/shard_map/all_to_all | solution.py:250
  166.5 11.4 %all-to-all-start.2 = ((f32[16,40,128]{2,1,0:T(8,128)}), f32[16,40,128]{2,1,0:T(8,128)S(1)}, u32[]{:S(2)}, u32[]{:S(2)}) async-start(f32[16,40,128]{2,1,0:T(8,128)} %broadcast_in_dim.2), calls=%async_computation.2 | async-start | bytes 655360 | tf_op jit(solution)/shard_map/all_to_all | solution.py:252
  177.9 18.9 %copy-start.12 = (f32[128,512]{1,0:T(8,128)S(1)}, f32[128,512]{1,0:T(8,128)}, u32[]{:S(2)}) copy-start(f32[128,512]{1,0:T(8,128)} %copy-done.11) | copy-start | bytes 786436
  177.9 19.6 %copy-start.14 = (f32[128,512]{1,0:T(8,128)S(1)}, f32[128,512]{1,0:T(8,128)}, u32[]{:S(2)}) copy-start(f32[128,512]{1,0:T(8,128)} %copy-done.13) | copy-start | bytes 786436
  177.9 9.4 %collective-permute-start.30 = (f32[640,128]{1,0:T(8,128)S(1)}, f32[640,128]{1,0:T(8,128)S(1)}, u32[]{:S(2)}, u32[]{:S(2)}) collective-permute-start(f32[640,128]{1,0:T(8,128)S(1)} %bitcast.85), channel_id=1, source_target_pairs={{0,2},{1,3},{2,4},{3,5},{4,6},{5,7},{6,0},{7,1},{8,10},{9,11},{10,... | collective-permute-start | bytes 983048 | tf_op jit(solution)/shard_map/ppermute | solution.py:364
  178.2 18.1 %collective-permute-start.31 = (f32[640,128]{1,0:T(8,128)S(1)}, f32[640,128]{1,0:T(8,128)S(1)}, u32[]{:S(2)}, u32[]{:S(2)}) collective-permute-start(f32[640,128]{1,0:T(8,128)S(1)} %bitcast.86), channel_id=1, source_target_pairs={{0,6},{1,7},{2,0},{3,1},{4,2},{5,3},{6,4},{7,5},{8,14},{9,15},{10,... | collective-permute-start | bytes 983048 | tf_op jit(solution)/shard_map/ppermute | solution.py:364
  180.6 15.7 %collective-permute-start.32 = (f32[640,128]{1,0:T(8,128)S(1)}, f32[640,128]{1,0:T(8,128)S(1)}, u32[]{:S(2)}, u32[]{:S(2)}) collective-permute-start(f32[640,128]{1,0:T(8,128)S(1)} %bitcast.87), channel_id=1, source_target_pairs={{0,4},{1,5},{2,6},{3,7},{4,0},{5,1},{6,2},{7,3},{8,12},{9,13},{10,... | collective-permute-start | bytes 983048 | tf_op jit(solution)/shard_map/ppermute | solution.py:364
  183.2 15.1 %collective-permute-start.33 = (f32[640,128]{1,0:T(8,128)S(1)}, f32[640,128]{1,0:T(8,128)S(1)}, u32[]{:S(2)}, u32[]{:S(2)}) collective-permute-start(f32[640,128]{1,0:T(8,128)S(1)} %bitcast.88), channel_id=1, source_target_pairs={{0,1},{1,0},{2,3},{3,2},{4,5},{5,4},{6,7},{7,6},{8,9},{9,8},{10,11... | collective-permute-start | bytes 983048 | tf_op jit(solution)/shard_map/ppermute | solution.py:365
  187.3 11.0 %collective-permute-start.34 = (f32[640,128]{1,0:T(8,128)S(1)}, f32[640,128]{1,0:T(8,128)S(1)}, u32[]{:S(2)}, u32[]{:S(2)}) collective-permute-start(f32[640,128]{1,0:T(8,128)S(1)} %collective-permute-done.30.refs_1_), channel_id=1, source_target_pairs={{0,1},{1,0},{2,3},{3,2},{4,5},{5,4},{6,7},{7,6},{8,9},{9,8},{10,11... | collective-permute-start | bytes 983048 | tf_op jit(solution)/shard_map/ppermute | solution.py:365
  196.2 2.0 collective-permute-start.35
  196.3 2.2 %collective-permute-start.36 = (f32[640,128]{1,0:T(8,128)S(1)}, f32[640,128]{1,0:T(8,128)S(1)}, u32[]{:S(2)}, u32[]{:S(2)}) collective-permute-start(f32[640,128]{1,0:T(8,128)S(1)} %collective-permute-done.32.refs_3_), channel_id=1, source_target_pairs={{0,1},{1,0},{2,3},{3,2},{4,5},{5,4},{6,7},{7,6},{8,9},{9,8},{10,11... | collective-permute-start | bytes 983048 | tf_op jit(solution)/shard_map/ppermute | solution.py:365
  (7 other events, 23.0 us)

commit v4 on v3

--- a/solution.py
+++ b/solution.py
@@ -331,18 +331,17 @@
     high, low, top_one, bottom_one = far_product(0, chunks(z, [2]), places, pieces_one, *flips)
     top_one, bottom_one = forward("z")(top_one), backward("z")(bottom_one)
     panels = [high, low]
-    panels[0], pieces_two = order((panels[0], pieces_two))
+    ahead, behind = near_product(0, chunks(z, [1, 3]), *panels[:2], *flips)
+    behind, pieces_two = order((behind, pieces_two))
     pieces_two += [lax.ppermute(piece, "col", SWAP) for piece in pieces_two]
     high, low, top_two, bottom_two = far_product(1, chunks(y, [2]), places, pieces_two, *flips)
     panels += [high, low]
     top_two, bottom_two = forward("y")(top_two), backward("y")(bottom_two)
     ahead_two, behind_two = near_product(1, chunks(y, [1, 3]), *panels[2:], *flips)
-    panels[0], ahead_two = order((panels[0], ahead_two))
-    ahead, behind = near_product(0, chunks(z, [1, 3]), *panels[:2], *flips)
     ahead_two, behind_two = join(ahead_two, behind_two, top_two, bottom_two)
     rest_two = (forward("y")(ahead_two), backward("y")(behind_two))
     ahead, behind = join(ahead, behind, top_one, bottom_one)
-    ahead, panels[1], panels[3] = order((ahead, panels[1], panels[3]))
+    ahead, ahead_two, panels[1], panels[3] = order((ahead, ahead_two, panels[1], panels[3]))
     rest_one = (forward("z")(ahead), backward("z")(behind))
     (own_one,) = near_product(0, chunks(z, [0]), *panels[:2], *flips)
     (own_two,) = near_product(1, chunks(y, [0]), *panels[2:], *flips)

time: 202 us -> 202 us (level)
  waiting for transfers between devices: 35.9 us -> 40.2 us
  blocking collectives: 23.5 us -> 19.2 us
    ppermute x4, waiting for transfers between devices: 0.01 us -> 7.96 us  [backward(): return lambda value: lax.ppermute(value, 'row', row_ring(over, 3))]
    all_to_all x1, blocking collectives: 23.5 us -> 19.2 us  [body(): part = lax.all_to_all(part, 'col', 0, 0, tiled=True)]
    ppermute x6, waiting for transfers between devices: 3.84 us -> 0.05 us  [gather_row(): lax.ppermute(panel, 'col', col_ring(s))]
    all_to_all x1, starting transfers between devices: 3.55 us -> 6.97 us  [sum_over_rows(): lax.all_to_all(part.reshape(16, piece, BLK), 'row', 0, 0, tiled=True)]
    ppermute x4, waiting for transfers between devices: 10.3 us -> 7.06 us  [forward(): return lambda value: lax.ppermute(value, 'row', row_ring(over, 1))]
    ppermute x1, waiting for transfers between devices: 4.15 us -> 7.37 us  [body(): lax.ppermute(light('z', fold(z, own_two, *rest_two)), BOTH, home_way)]
    ppermute x1, starting transfers between devices: 3.05 us -> 6 us  [body(): lax.ppermute(light('z', fold(z, own_two, *rest_two)), BOTH, home_way)]
    ppermute x4, starting transfers between devices: 9.44 us -> 7.38 us  [backward(): return lambda value: lax.ppermute(value, 'row', row_ring(over, 3))]
  transfers between devices with their start and end apart: 39 -> 39, of which waited for: 9 -> 9; matrix products, arithmetic and copies ran while one was open for 6% -> 7% of each run, Pallas kernels for 23% -> 23%
where the time goes in v4:
time: 202 us; the launch traced here: 201 us
  starting transfers between devices  66.2 us (33%)
  Pallas kernels  52.1 us (26%)
  waiting for transfers between devices  40.2 us (20%)
  blocking collectives  19.2 us (10%)
  matrix products  11.5 us (6%)
  local copies, waits for them, and re-layouts  5.07 us (3%)
  other arithmetic  4.55 us (2%)
  between operations  2.36 us (1%)
    pallas_call x4, Pallas kernels, near_product(): pl.pallas_call(near_kernel, grid_spec=pltpu.PrefetchScalarGridSpec(num_sc...  22 us
    all_to_all x1, blocking collectives, body(): part = lax.all_to_all(part, 'col', 0, 0, tiled=True)  19.2 us
    ppermute x4, starting transfers between devices, body(): strips += [lax.ppermute(piece, 'col', SWAP) for piece in strips]  13.6 us
    pallas_call x2, Pallas kernels, far_product(): pl.pallas_call(far_kernel, grid_spec=pltpu.PrefetchScalarGridSpec(num_sca...  9.99 us
    ppermute x6, starting transfers between devices, gather_row(): lax.ppermute(panel, 'col', col_ring(s))  8 us
    ppermute x4, waiting for transfers between devices, backward(): return lambda value: lax.ppermute(value, 'row', row_ring(over, 3))  7.96 us
    ppermute x4, starting transfers between devices, backward(): return lambda value: lax.ppermute(value, 'row', row_ring(over, 3))  7.38 us
    ppermute x1, waiting for transfers between devices, body(): lax.ppermute(light('z', fold(z, own_two, *rest_two)), BOTH, home_way)  7.37 us
  transfers between devices with their start and end apart: 39, of which 9 were waited for; matrix products, arithmetic and copies ran while one was open for 7% of the time, Pallas kernels for 23%

profile of v4, /device:TPU:1, one launch (start us, length us, event | category | flops | bytes accessed | tf_op | source)
XLA Modules:
  0.0 201.1 jit_solution(17861710924618389929)
XLA Ops:
  0.7 1.4 compare_reduce_fusion.1
  2.7 1.7 convolution_multiply_fusion.1.refs_0_
  4.4 2.1 %collective-permute-start = (f32[128,512]{1,0:T(8,128)S(1)}, f32[128,512]{1,0:T(8,128)S(1)}, u32[]{:S(2)}, u32[]{:S(2)}) collective-permute-start(f32[128,512]{1,0:T(8,128)S(1)} %convolution_multiply_fusion.1.refs_0_), channel_id=1, source_target_pairs={{0,2},{1,3},{2,4},{3,5},{4,6},{5,7},{6,0},{7,1},{8,10},{9,11},{10,... | collective-permute-start | bytes 786440 | tf_op jit(solution)/shard_map/ppermute | solution.py:192
  6.5 1.3 collective-permute-start.1
  7.9 1.6 collective-permute-start.2
  9.5 1.4 compare_reduce_fusion
  11.6 3.4 %copy-done.1 = f32[1024,2048]{1,0:T(8,128)S(1)} copy-done((f32[1024,2048]{1,0:T(8,128)S(1)}, f32[1024,2048]{1,0:T(8,128)}, u32[]{:S(2)}) %copy-start.1) | copy-done | bytes 8388632
  15.0 7.1 %flip.1 = (bf16[4,4,128,1024]{3,2,1,0:T(8,128)(2,1)}, bf16[4,4,128,1024]{3,2,1,0:T(8,128)(2,1)}) custom-call(s32[16]{0:T(128)S(1)} %stack.152.blocks, f32[1024,2048]{1,0:T(8,128)S(1)} %copy-done.1, f32[1024,2048]{1,0:T(8,128)S(1)} %copy-done.1), custom_call_target="tpu_custom_call" | custom-call | tf_op jit(solution)/shard_map/flip/pallas_call | solution.py:59
  23.6 1.6 collective-permute-start.3
  26.6 2.4 %collective-permute-start.8 = (f32[128,512]{1,0:T(8,128)S(1)}, f32[128,512]{1,0:T(8,128)}, u32[]{:S(2)}, u32[]{:S(2)}) collective-permute-start(f32[128,512]{1,0:T(8,128)S(1)} %convolution_subtract_fusion.refs_0_), channel_id=1, source_target_pairs={{0,6},{1,7},{2,0},{3,1},{4,2},{5,3},{6,4},{7,5},{8,14},{9,15},{10,... | collective-permute-start | bytes 786440 | tf_op jit(solution)/shard_map/ppermute | solution.py:192
  29.3 4.3 %far.2 = (bf16[1024,512]{1,0:T(8,128)(2,1)}, bf16[1024,512]{1,0:T(8,128)(2,1)}, f32[256,512]{1,0:T(8,128)S(1)}, f32[256,512]{1,0:T(8,128)S(1)}) custom-call(s32[1]{0:T(128)} %bitcast.18.chunks, s32[8]{0:T(128)S(1)} %stack.162.places, f32[128,512]{1,0:T(8,128)S(1)} %convolution_multiply_fusion.1.refs_0_, f32[128,512]{1,0:T(8,128)S(1)} %collective-permute-done.refs_1_, ...), custom_call_target="tpu_custom_call" | custom-call | tf_op jit(solution)/shard_map/far/pallas_call | solution.py:111
  33.6 6.4 %near.4 = (f32[512,512]{1,0:T(8,128)S(1)}, f32[512,512]{1,0:T(8,128)S(1)}) custom-call(s32[2]{0:T(128)S(1)} %pad_add_fusion.chunks, bf16[4,4,128,1024]{3,2,1,0:T(8,128)(2,1)} %get-tuple-element.56.refs_8_.flip_high, bf16[4,4,128,1024]{3,2,1,0:T(8,128)(2,1)} %get-tuple-element.57.refs_9_.flip_low, bf16[1024,512]{1,0:T(8,128)(2,1)} %get-tuple-element.62.high.high_one, ...), custom_call_target="tpu_custom_call" | custom-call | tf_op jit(solution)/shard_map/near/pallas_call | solution.py:127
  40.1 1.9 collective-permute-start.12
  42.6 1.6 collective-permute-start.10
  44.2 2.8 %collective-permute-start.11 = (f32[256,512]{1,0:T(8,128)}, f32[256,512]{1,0:T(8,128)}, u32[]{:S(2)}, u32[]{:S(2)}) collective-permute-start(f32[256,512]{1,0:T(8,128)} %copy-done.6), channel_id=1, source_target_pairs={{0,96},{8,104},{16,112},{24,120},{32,0},{40,8},{48,16},{56,24},{64... | collective-permute-start | bytes 1572872 | tf_op jit(solution)/shard_map/ppermute | solution.py:323
  47.0 5.7 %far.3 = (bf16[1024,512]{1,0:T(8,128)(2,1)}, bf16[1024,512]{1,0:T(8,128)(2,1)}, f32[256,512]{1,0:T(8,128)}, f32[256,512]{1,0:T(8,128)}) custom-call(s32[1]{0:T(128)} %bitcast.31.chunks, s32[8]{0:T(128)S(1)} %stack.162.places, f32[128,512]{1,0:T(8,128)S(1)} %convolution_subtract_fusion.refs_0_, f32[128,512]{1,0:T(8,128)} %collective-permute-done.7.refs_1_, ...), custom_call_target="tpu_custom_call" | custom-call | tf_op jit(solution)/shard_map/far/pallas_call | solution.py:111
  52.8 1.3 collective-permute-start.16
  54.1 1.4 collective-permute-start.17
  55.6 7.7 %near.5 = (f32[512,512]{1,0:T(8,128)}, f32[512,512]{1,0:T(8,128)}) custom-call(s32[2]{0:T(128)S(1)} %pad_add_fusion.1.chunks, bf16[4,4,128,1024]{3,2,1,0:T(8,128)(2,1)} %get-tuple-element.56.refs_8_.flip_high, bf16[4,4,128,1024]{3,2,1,0:T(8,128)(2,1)} %get-tuple-element.57.refs_9_.flip_low, bf16[1024,512]{1,0:T(8,128)(2,1)} %get-tuple-element.74.high.high_two, ...), custom_call_target="tpu_custom_call" | custom-call | tf_op jit(solution)/shard_map/near/pallas_call | solution.py:127
  63.3 1.4 join.2
  64.7 1.4 collective-permute-start.19
  67.2 2.6 %join.3 = (f32[512,512]{1,0:T(8,128)}, f32[512,512]{1,0:T(8,128)}) custom-call(f32[512,512]{1,0:T(8,128)} %get-tuple-element.76.ahead, f32[512,512]{1,0:T(8,128)} %get-tuple-element.77.behind, f32[256,512]{1,0:T(8,128)} %collective-permute-done.16.top, f32[256,512]{1,0:T(8,128)} %collective-permute-done.17.bottom), custom_call_target="tpu_custom_call", output_to_operand_aliasing={{0}: (0, {}), {1}: (1, {})} | custom-call | tf_op jit(solution)/shard_map/join/pallas_call | solution.py:149
  70.7 1.7 collective-permute-start.25
  72.5 4.0 %near.6.own = f32[512,512]{1,0:T(8,128)S(1)} custom-call(s32[1]{0:T(128)} %bitcast.1.chunks, bf16[4,4,128,1024]{3,2,1,0:T(8,128)(2,1)} %get-tuple-element.56.refs_8_.flip_high, bf16[4,4,128,1024]{3,2,1,0:T(8,128)(2,1)} %get-tuple-element.57.refs_9_.flip_low, bf16[1024,512]{1,0:T(8,128)(2,1)} %get-tuple-element.62.high.high_one, ...), custom_call_target="tpu_custom_call" | custom-call | tf_op jit(solution)/shard_map/near/pallas_call | solution.py:127
  76.4 4.0 %near.7.own = f32[512,512]{1,0:T(8,128)S(1)} custom-call(s32[1]{0:T(128)} %bitcast.32.chunks, bf16[4,4,128,1024]{3,2,1,0:T(8,128)(2,1)} %get-tuple-element.56.refs_8_.flip_high, bf16[4,4,128,1024]{3,2,1,0:T(8,128)(2,1)} %get-tuple-element.57.refs_9_.flip_low, bf16[1024,512]{1,0:T(8,128)(2,1)} %get-tuple-element.74.high.high_two, ...), custom_call_target="tpu_custom_call" | custom-call | tf_op jit(solution)/shard_map/near/pallas_call | solution.py:127
  80.4 7.9 %collective-permute-done.19.other = f32[512,512]{1,0:T(8,128)} collective-permute-done((f32[512,512]{1,0:T(8,128)S(1)}, f32[512,512]{1,0:T(8,128)}, u32[]{:S(2)}, u32[]{:S(2)}) %collective-permute-start.19) | collective-permute-done | bytes 1048608 | tf_op jit(solution)/shard_map/ppermute | solution.py:323
  88.4 5.9 %collective-permute-done.18.one = f32[512,512]{1,0:T(8,128)} collective-permute-done((f32[512,512]{1,0:T(8,128)S(1)}, f32[512,512]{1,0:T(8,128)}, u32[]{:S(2)}, u32[]{:S(2)}) %collective-permute-start.18) | collective-permute-done | bytes 1048608 | tf_op jit(solution)/shard_map/ppermute | solution.py:320
  94.3 1.8 fold.2
  96.1 2.1 %collective-permute-start.22 = (f32[128,512]{1,0:T(8,128)S(1)}, f32[128,512]{1,0:T(8,128)S(1)}, u32[]{:S(2)}, u32[]{:S(2)}) collective-permute-start(f32[128,512]{1,0:T(8,128)S(1)} %get-tuple-element.89), channel_id=1, source_target_pairs={{0,24},{8,0},{16,8},{24,16},{32,56},{40,32},{48,40},{56,48},{64,88... | collective-permute-start | bytes 786440 | tf_op jit(solution)/shard_map/ppermute | solution.py:329
  99.6 1.8 fold.3
  103.3 5.1 %collective-permute-done.20 = f32[128,512]{1,0:T(8,128)S(1)} collective-permute-done((f32[128,512]{1,0:T(8,128)S(1)}, f32[128,512]{1,0:T(8,128)S(1)}, u32[]{:S(2)}, u32[]{:S(2)}) %collective-permute-start.20) | collective-permute-done | bytes 262176 | tf_op jit(solution)/shard_map/ppermute | solution.py:329
  108.6 4.1 %collective-permute-start.23 = (f32[128,512]{1,0:T(8,128)S(1)}, f32[128,512]{1,0:T(8,128)S(1)}, u32[]{:S(2)}, u32[]{:S(2)}) collective-permute-start(f32[128,512]{1,0:T(8,128)S(1)} %add_add_fusion.1), channel_id=1, source_target_pairs={{0,0},{1,25},{2,34},{3,59},{4,68},{5,93},{6,102},{7,127},{8,8},{9,... | collective-permute-start | bytes 786440 | tf_op jit(solution)/shard_map/ppermute | solution.py:351
  112.8 6.0 %collective-permute-start.29 = (f32[128,512]{1,0:T(8,128)S(1)}, f32[128,512]{1,0:T(8,128)S(1)}, u32[]{:S(2)}, u32[]{:S(2)}) collective-permute-start(f32[128,512]{1,0:T(8,128)S(1)} %add_add_fusion), channel_id=1, source_target_pairs={{0,0},{1,25},{2,34},{3,59},{4,68},{5,93},{6,102},{7,127},{8,8},{9,... | collective-permute-start | bytes 786440 | tf_op jit(solution)/shard_map/ppermute | solution.py:352
  118.8 1.7 collective-permute-done.23
  120.7 7.4 %collective-permute-done.29 = f32[128,512]{1,0:T(8,128)S(1)} collective-permute-done((f32[128,512]{1,0:T(8,128)S(1)}, f32[128,512]{1,0:T(8,128)S(1)}, u32[]{:S(2)}, u32[]{:S(2)}) %collective-permute-start.29) | collective-permute-done | bytes 262176 | tf_op jit(solution)/shard_map/ppermute | solution.py:352
  128.7 19.2 %all_to_all.15.part = f32[8,128,128]{2,1,0:T(8,128)S(1)} all-to-all(f32[8,128,128]{2,1,0:T(8,128)S(1)} %fusion), channel_id=1, replica_groups=mesh['row'=16,'col'=8] {'col'}, dimensions={0} | all-to-all | bytes 1048576 | tf_op jit(solution)/shard_map/all_to_all | solution.py:361
  147.9 2.6 %strip.1 = f32[640,128]{1,0:T(8,128)} custom-call(s32[1]{0:T(128)} %bitcast.33.col, f32[8,128,128]{2,1,0:T(8,128)S(1)} %all_to_all.15.part, bf16[1024,512]{1,0:T(8,128)(2,1)S(1)} %copy-done.2, bf16[1024,512]{1,0:T(8,128)(2,1)S(1)} %copy-done.3, bf16[1024,512]{1,0:T(8,128)(2,1)S(1)} %copy-done.4, bf16[1024,512]{1,0:T(8,128)(2,1)S(1)} %copy-done.5), custom_call_target="tpu_custom_call" | custom-call | tf_op jit(solution)/shard_map/strip/pallas_call | solution.py:237
  150.5 7.0 %all-to-all-start.1 = ((f32[16,40,128]{2,1,0:T(8,128)}), f32[16,40,128]{2,1,0:T(8,128)S(1)}, u32[]{:S(2)}, u32[]{:S(2)}) async-start(f32[16,40,128]{2,1,0:T(8,128)} %bitcast.43), calls=%async_computation.1 | async-start | bytes 655360 | tf_op jit(solution)/shard_map/all_to_all | solution.py:250
  158.6 7.0 %all-to-all-done.1 = f32[16,40,128]{2,1,0:T(8,128)S(1)} async-done(((f32[16,40,128]{2,1,0:T(8,128)}), f32[16,40,128]{2,1,0:T(8,128)S(1)}, u32[]{:S(2)}, u32[]{:S(2)}) %all-to-all-start.1) | async-done | bytes 327712 | tf_op jit(solution)/shard_map/all_to_all | solution.py:250
  166.3 3.5 %all-to-all-start.2 = ((f32[16,40,128]{2,1,0:T(8,128)}), f32[16,40,128]{2,1,0:T(8,128)S(1)}, u32[]{:S(2)}, u32[]{:S(2)}) async-start(f32[16,40,128]{2,1,0:T(8,128)} %broadcast_in_dim.2), calls=%async_computation.2 | async-start | bytes 655360 | tf_op jit(solution)/shard_map/all_to_all | solution.py:252
  169.9 2.0 fusion.11
  171.9 2.2 %fusion.10.refs_9_ = f32[512,512]{1,0:T(8,128)S(1)} fusion(f32[512,512]{1,0:T(8,128)S(1)} %fusion.9.refs_8_, f32[512,512]{1,0:T(8,128)} %copy-done.8), kind=kOutput, calls=%fused_computation.30 | convolution fusion | flops 805306368 | bytes 3145728 | tf_op jit(solution)/shard_map/dot_general | solution.py:19
  174.1 3.6 %all-to-all-done.2 = f32[16,40,128]{2,1,0:T(8,128)S(1)} async-done(((f32[16,40,128]{2,1,0:T(8,128)}), f32[16,40,128]{2,1,0:T(8,128)S(1)}, u32[]{:S(2)}, u32[]{:S(2)}) %all-to-all-start.2) | async-done | bytes 327712 | tf_op jit(solution)/shard_map/all_to_all | solution.py:252
  178.0 2.4 %collective-permute-start.31 = (f32[640,128]{1,0:T(8,128)S(1)}, f32[640,128]{1,0:T(8,128)S(1)}, u32[]{:S(2)}, u32[]{:S(2)}) collective-permute-start(f32[640,128]{1,0:T(8,128)S(1)} %bitcast.86), channel_id=1, source_target_pairs={{0,6},{1,7},{2,0},{3,1},{4,2},{5,3},{6,4},{7,5},{8,14},{9,15},{10,... | collective-permute-start | bytes 983048 | tf_op jit(solution)/shard_map/ppermute | solution.py:363
  180.4 2.6 %convolution_add_fusion.refs_10_ = f32[512,512]{1,0:T(8,128)S(1)} fusion(f32[512,512]{1,0:T(8,128)} %fusion.11, f32[512,512]{1,0:T(8,128)} %copy-done.8, f32[512,512]{1,0:T(8,128)S(1)} %fusion.10.refs_9_), kind=kOutput, calls=%fused_computation | convolution fusion | flops 805568512 | bytes 4194304 | tf_op jit(solution)/shard_map/dot_general | solution.py:23
  183.0 4.1 %collective-permute-start.33 = (f32[640,128]{1,0:T(8,128)S(1)}, f32[640,128]{1,0:T(8,128)S(1)}, u32[]{:S(2)}, u32[]{:S(2)}) collective-permute-start(f32[640,128]{1,0:T(8,128)S(1)} %bitcast.88), channel_id=1, source_target_pairs={{0,1},{1,0},{2,3},{3,2},{4,5},{5,4},{6,7},{7,6},{8,9},{9,8},{10,11... | collective-permute-start | bytes 983048 | tf_op jit(solution)/shard_map/ppermute | solution.py:364
  187.1 9.0 %collective-permute-start.34 = (f32[640,128]{1,0:T(8,128)S(1)}, f32[640,128]{1,0:T(8,128)S(1)}, u32[]{:S(2)}, u32[]{:S(2)}) collective-permute-start(f32[640,128]{1,0:T(8,128)S(1)} %collective-permute-done.30.refs_1_), channel_id=1, source_target_pairs={{0,1},{1,0},{2,3},{3,2},{4,5},{5,4},{6,7},{7,6},{8,9},{9,8},{10,11... | collective-permute-start | bytes 983048 | tf_op jit(solution)/shard_map/ppermute | solution.py:364
  198.3 2.8 %finish.1 = (f32[512,512]{1,0:T(8,128)}, f32[512,512]{1,0:T(8,128)}, f32[512,512]{1,0:T(8,128)}) custom-call(s32[8]{0:T(128)S(1)} %stack.162.places, f32[640,128]{1,0:T(8,128)S(1)} %bitcast.89, f32[640,128]{1,0:T(8,128)S(1)} %collective-permute-done.30.refs_1_, f32[640,128]{1,0:T(8,128)S(1)} %collective-permute-done.31.refs_2_, ...), custom_call_target="tpu_custom_call" | custom-call | tf_op jit(solution)/shard_map/finish/pallas_call | solution.py:279
  (104 shorter events, 14.6 us)
Async XLA Ops:
  0.6 21.5 %copy-start = (f32[512,512]{1,0:T(8,128)S(1)}, f32[512,512]{1,0:T(8,128)}, u32[]{:S(2)}) copy-start(f32[512,512]{1,0:T(8,128)} %param.13) | copy-start | bytes 3145732
  4.4 19.2 %collective-permute-start = (f32[128,512]{1,0:T(8,128)S(1)}, f32[128,512]{1,0:T(8,128)S(1)}, u32[]{:S(2)}, u32[]{:S(2)}) collective-permute-start(f32[128,512]{1,0:T(8,128)S(1)} %convolution_multiply_fusion.1.refs_0_), channel_id=1, source_target_pairs={{0,2},{1,3},{2,4},{3,5},{4,6},{5,7},{6,0},{7,1},{8,10},{9,11},{10,... | collective-permute-start | bytes 786440 | tf_op jit(solution)/shard_map/ppermute | solution.py:192
  6.5 17.1 %collective-permute-start.1 = (f32[128,512]{1,0:T(8,128)S(1)}, f32[128,512]{1,0:T(8,128)S(1)}, u32[]{:S(2)}, u32[]{:S(2)}) collective-permute-start(f32[128,512]{1,0:T(8,128)S(1)} %convolution_multiply_fusion.1.refs_0_), channel_id=1, source_target_pairs={{0,6},{1,7},{2,0},{3,1},{4,2},{5,3},{6,4},{7,5},{8,14},{9,15},{10,... | collective-permute-start | bytes 786440 | tf_op jit(solution)/shard_map/ppermute | solution.py:192
  7.9 15.7 %collective-permute-start.2 = (f32[128,512]{1,0:T(8,128)S(1)}, f32[128,512]{1,0:T(8,128)S(1)}, u32[]{:S(2)}, u32[]{:S(2)}) collective-permute-start(f32[128,512]{1,0:T(8,128)S(1)} %convolution_multiply_fusion.1.refs_0_), channel_id=1, source_target_pairs={{0,4},{1,5},{2,6},{3,7},{4,0},{5,1},{6,2},{7,3},{8,12},{9,13},{10,... | collective-permute-start | bytes 786440 | tf_op jit(solution)/shard_map/ppermute | solution.py:192
  15.0 8.1 %copy-start.15 = (f32[128,512]{1,0:T(8,128)S(1)}, f32[128,512]{1,0:T(8,128)}, u32[]{:S(2)}) copy-start(f32[128,512]{1,0:T(8,128)} %param.12) | copy-start | bytes 786436
  23.6 3.0 %collective-permute-start.3 = (f32[128,512]{1,0:T(8,128)S(1)}, f32[128,512]{1,0:T(8,128)S(1)}, u32[]{:S(2)}, u32[]{:S(2)}) collective-permute-start(f32[128,512]{1,0:T(8,128)S(1)} %convolution_multiply_fusion.1.refs_0_), channel_id=1, source_target_pairs={{0,1},{1,0},{2,3},{3,2},{4,5},{5,4},{6,7},{7,6},{8,9},{9,8},{10,11... | collective-permute-start | bytes 786440 | tf_op jit(solution)/shard_map/ppermute | solution.py:317
  25.2 3.8 %collective-permute-start.4 = (f32[128,512]{1,0:T(8,128)S(1)}, f32[128,512]{1,0:T(8,128)S(1)}, u32[]{:S(2)}, u32[]{:S(2)}) collective-permute-start(f32[128,512]{1,0:T(8,128)S(1)} %collective-permute-done.refs_1_), channel_id=1, source_target_pairs={{0,1},{1,0},{2,3},{3,2},{4,5},{5,4},{6,7},{7,6},{8,9},{9,8},{10,11... | collective-permute-start | bytes 786440 | tf_op jit(solution)/shard_map/ppermute | solution.py:317
  25.3 4.0 %collective-permute-start.5 = (f32[128,512]{1,0:T(8,128)S(1)}, f32[128,512]{1,0:T(8,128)S(1)}, u32[]{:S(2)}, u32[]{:S(2)}) collective-permute-start(f32[128,512]{1,0:T(8,128)S(1)} %collective-permute-done.1.refs_2_), channel_id=1, source_target_pairs={{0,1},{1,0},{2,3},{3,2},{4,5},{5,4},{6,7},{7,6},{8,9},{9,8},{10,11... | collective-permute-start | bytes 786440 | tf_op jit(solution)/shard_map/ppermute | solution.py:317
  25.7 3.6 %collective-permute-start.6 = (f32[128,512]{1,0:T(8,128)S(1)}, f32[128,512]{1,0:T(8,128)S(1)}, u32[]{:S(2)}, u32[]{:S(2)}) collective-permute-start(f32[128,512]{1,0:T(8,128)S(1)} %collective-permute-done.2.refs_3_), channel_id=1, source_target_pairs={{0,1},{1,0},{2,3},{3,2},{4,5},{5,4},{6,7},{7,6},{8,9},{9,8},{10,11... | collective-permute-start | bytes 786440 | tf_op jit(solution)/shard_map/ppermute | solution.py:317
  26.2 13.8 %collective-permute-start.7 = (f32[128,512]{1,0:T(8,128)S(1)}, f32[128,512]{1,0:T(8,128)}, u32[]{:S(2)}, u32[]{:S(2)}) collective-permute-start(f32[128,512]{1,0:T(8,128)S(1)} %convolution_subtract_fusion.refs_0_), channel_id=1, source_target_pairs={{0,2},{1,3},{2,4},{3,5},{4,6},{5,7},{6,0},{7,1},{8,10},{9,11},{10,... | collective-permute-start | bytes 786440 | tf_op jit(solution)/shard_map/ppermute | solution.py:192
  26.6 13.4 %collective-permute-start.8 = (f32[128,512]{1,0:T(8,128)S(1)}, f32[128,512]{1,0:T(8,128)}, u32[]{:S(2)}, u32[]{:S(2)}) collective-permute-start(f32[128,512]{1,0:T(8,128)S(1)} %convolution_subtract_fusion.refs_0_), channel_id=1, source_target_pairs={{0,6},{1,7},{2,0},{3,1},{4,2},{5,3},{6,4},{7,5},{8,14},{9,15},{10,... | collective-permute-start | bytes 786440 | tf_op jit(solution)/shard_map/ppermute | solution.py:192
  29.0 11.1 %collective-permute-start.9 = (f32[128,512]{1,0:T(8,128)S(1)}, f32[128,512]{1,0:T(8,128)}, u32[]{:S(2)}, u32[]{:S(2)}) collective-permute-start(f32[128,512]{1,0:T(8,128)S(1)} %convolution_subtract_fusion.refs_0_), channel_id=1, source_target_pairs={{0,4},{1,5},{2,6},{3,7},{4,0},{5,1},{6,2},{7,3},{8,12},{9,13},{10,... | collective-permute-start | bytes 786440 | tf_op jit(solution)/shard_map/ppermute | solution.py:192
  40.1 4.1 %collective-permute-start.12 = (f32[128,512]{1,0:T(8,128)S(1)}, f32[128,512]{1,0:T(8,128)}, u32[]{:S(2)}, u32[]{:S(2)}) collective-permute-start(f32[128,512]{1,0:T(8,128)S(1)} %convolution_subtract_fusion.refs_0_), channel_id=1, source_target_pairs={{0,1},{1,0},{2,3},{3,2},{4,5},{5,4},{6,7},{7,6},{8,9},{9,8},{10,11... | collective-permute-start | bytes 786440 | tf_op jit(solution)/shard_map/ppermute | solution.py:336
  42.0 5.1 %collective-permute-start.13 = (f32[128,512]{1,0:T(8,128)}, f32[128,512]{1,0:T(8,128)}, u32[]{:S(2)}, u32[]{:S(2)}) collective-permute-start(f32[128,512]{1,0:T(8,128)} %collective-permute-done.7.refs_1_), channel_id=1, source_target_pairs={{0,1},{1,0},{2,3},{3,2},{4,5},{5,4},{6,7},{7,6},{8,9},{9,8},{10,11... | collective-permute-start | bytes 786440 | tf_op jit(solution)/shard_map/ppermute | solution.py:336
  42.1 5.0 %collective-permute-start.14 = (f32[128,512]{1,0:T(8,128)}, f32[128,512]{1,0:T(8,128)}, u32[]{:S(2)}, u32[]{:S(2)}) collective-permute-start(f32[128,512]{1,0:T(8,128)} %collective-permute-done.8.refs_2_), channel_id=1, source_target_pairs={{0,1},{1,0},{2,3},{3,2},{4,5},{5,4},{6,7},{7,6},{8,9},{9,8},{10,11... | collective-permute-start | bytes 786440 | tf_op jit(solution)/shard_map/ppermute | solution.py:336
  42.5 4.6 %collective-permute-start.15 = (f32[128,512]{1,0:T(8,128)}, f32[128,512]{1,0:T(8,128)}, u32[]{:S(2)}, u32[]{:S(2)}) collective-permute-start(f32[128,512]{1,0:T(8,128)} %collective-permute-done.9.refs_3_), channel_id=1, source_target_pairs={{0,1},{1,0},{2,3},{3,2},{4,5},{5,4},{6,7},{7,6},{8,9},{9,8},{10,11... | collective-permute-start | bytes 786440 | tf_op jit(solution)/shard_map/ppermute | solution.py:336
  42.6 20.7 %collective-permute-start.10 = (f32[256,512]{1,0:T(8,128)}, f32[256,512]{1,0:T(8,128)}, u32[]{:S(2)}, u32[]{:S(2)}) collective-permute-start(f32[256,512]{1,0:T(8,128)} %copy-done.7), channel_id=1, source_target_pairs={{0,32},{8,40},{16,48},{24,56},{32,64},{40,72},{48,80},{56,88},{64,... | collective-permute-start | bytes 1572872 | tf_op jit(solution)/shard_map/ppermute | solution.py:320
  44.2 19.1 %collective-permute-start.11 = (f32[256,512]{1,0:T(8,128)}, f32[256,512]{1,0:T(8,128)}, u32[]{:S(2)}, u32[]{:S(2)}) collective-permute-start(f32[256,512]{1,0:T(8,128)} %copy-done.6), channel_id=1, source_target_pairs={{0,96},{8,104},{16,112},{24,120},{32,0},{40,8},{48,16},{56,24},{64... | collective-permute-start | bytes 1572872 | tf_op jit(solution)/shard_map/ppermute | solution.py:323
  52.8 14.5 %collective-permute-start.16 = (f32[256,512]{1,0:T(8,128)}, f32[256,512]{1,0:T(8,128)}, u32[]{:S(2)}, u32[]{:S(2)}) collective-permute-start(f32[256,512]{1,0:T(8,128)} %get-tuple-element.78), channel_id=1, source_target_pairs={{0,8},{8,16},{16,24},{24,0},{32,40},{40,48},{48,56},{56,32},{64,72... | collective-permute-start | bytes 1572872 | tf_op jit(solution)/shard_map/ppermute | solution.py:320
  54.1 13.2 %collective-permute-start.17 = (f32[256,512]{1,0:T(8,128)}, f32[256,512]{1,0:T(8,128)}, u32[]{:S(2)}, u32[]{:S(2)}) collective-permute-start(f32[256,512]{1,0:T(8,128)} %get-tuple-element.79), channel_id=1, source_target_pairs={{0,24},{8,0},{16,8},{24,16},{32,56},{40,32},{48,40},{56,48},{64,88... | collective-permute-start | bytes 1572872 | tf_op jit(solution)/shard_map/ppermute | solution.py:323
  64.7 23.7 %collective-permute-start.19 = (f32[512,512]{1,0:T(8,128)S(1)}, f32[512,512]{1,0:T(8,128)}, u32[]{:S(2)}, u32[]{:S(2)}) collective-permute-start(f32[512,512]{1,0:T(8,128)S(1)} %get-tuple-element.85), channel_id=1, source_target_pairs={{0,96},{8,104},{16,112},{24,120},{32,0},{40,8},{48,16},{56,24},{64... | collective-permute-start | bytes 3145736 | tf_op jit(solution)/shard_map/ppermute | solution.py:323
  69.8 24.5 %collective-permute-start.18 = (f32[512,512]{1,0:T(8,128)S(1)}, f32[512,512]{1,0:T(8,128)}, u32[]{:S(2)}, u32[]{:S(2)}) collective-permute-start(f32[512,512]{1,0:T(8,128)S(1)} %get-tuple-element.84), channel_id=1, source_target_pairs={{0,32},{8,40},{16,48},{24,56},{32,64},{40,72},{48,80},{56,88},{64,... | collective-permute-start | bytes 3145736 | tf_op jit(solution)/shard_map/ppermute | solution.py:320
  69.8 29.8 %collective-permute-start.24 = (f32[512,512]{1,0:T(8,128)}, f32[512,512]{1,0:T(8,128)}, u32[]{:S(2)}, u32[]{:S(2)}) collective-permute-start(f32[512,512]{1,0:T(8,128)} %get-tuple-element.80), channel_id=1, source_target_pairs={{0,8},{8,16},{16,24},{24,0},{32,40},{40,48},{48,56},{56,32},{64,72... | collective-permute-start | bytes 3145736 | tf_op jit(solution)/shard_map/ppermute | solution.py:320
  70.7 28.8 %collective-permute-start.25 = (f32[512,512]{1,0:T(8,128)}, f32[512,512]{1,0:T(8,128)}, u32[]{:S(2)}, u32[]{:S(2)}) collective-permute-start(f32[512,512]{1,0:T(8,128)} %get-tuple-element.91), channel_id=1, source_target_pairs={{0,24},{8,0},{16,8},{24,16},{32,56},{40,32},{48,40},{56,48},{64,88... | collective-permute-start | bytes 3145736 | tf_op jit(solution)/shard_map/ppermute | solution.py:323
  96.1 51.8 %copy-start.2 = (bf16[1024,512]{1,0:T(8,128)(2,1)S(1)}, bf16[1024,512]{1,0:T(8,128)(2,1)}, u32[]{:S(2)}) copy-start(bf16[1024,512]{1,0:T(8,128)(2,1)} %get-tuple-element.62.high.high_one) | copy-start | bytes 3145732
  96.1 51.8 %copy-start.3 = (bf16[1024,512]{1,0:T(8,128)(2,1)S(1)}, bf16[1024,512]{1,0:T(8,128)(2,1)}, u32[]{:S(2)}) copy-start(bf16[1024,512]{1,0:T(8,128)(2,1)} %get-tuple-element.81.low.low_one) | copy-start | bytes 3145732
  96.1 51.8 %copy-start.4 = (bf16[1024,512]{1,0:T(8,128)(2,1)S(1)}, bf16[1024,512]{1,0:T(8,128)(2,1)}, u32[]{:S(2)}) copy-start(bf16[1024,512]{1,0:T(8,128)(2,1)} %get-tuple-element.74.high.high_two) | copy-start | bytes 3145732
  96.1 51.8 %copy-start.5 = (bf16[1024,512]{1,0:T(8,128)(2,1)S(1)}, bf16[1024,512]{1,0:T(8,128)(2,1)}, u32[]{:S(2)}) copy-start(bf16[1024,512]{1,0:T(8,128)(2,1)} %get-tuple-element.82.low.low_two) | copy-start | bytes 3145732
  96.1 6.8 %collective-permute-start.22 = (f32[128,512]{1,0:T(8,128)S(1)}, f32[128,512]{1,0:T(8,128)S(1)}, u32[]{:S(2)}, u32[]{:S(2)}) collective-permute-start(f32[128,512]{1,0:T(8,128)S(1)} %get-tuple-element.89), channel_id=1, source_target_pairs={{0,24},{8,0},{16,8},{24,16},{32,56},{40,32},{48,40},{56,48},{64,88... | collective-permute-start | bytes 786440 | tf_op jit(solution)/shard_map/ppermute | solution.py:329
  98.3 10.2 %collective-permute-start.20 = (f32[128,512]{1,0:T(8,128)S(1)}, f32[128,512]{1,0:T(8,128)S(1)}, u32[]{:S(2)}, u32[]{:S(2)}) collective-permute-start(f32[128,512]{1,0:T(8,128)S(1)} %get-tuple-element.87), channel_id=1, source_target_pairs={{0,8},{8,16},{16,24},{24,0},{32,40},{40,48},{48,56},{56,32},{64,72... | collective-permute-start | bytes 786440 | tf_op jit(solution)/shard_map/ppermute | solution.py:329
  98.3 10.2 %collective-permute-start.21 = (f32[128,512]{1,0:T(8,128)S(1)}, f32[128,512]{1,0:T(8,128)S(1)}, u32[]{:S(2)}, u32[]{:S(2)}) collective-permute-start(f32[128,512]{1,0:T(8,128)S(1)} %get-tuple-element.88), channel_id=1, source_target_pairs={{0,16},{8,24},{16,0},{24,8},{32,48},{40,56},{48,32},{56,40},{64,80... | collective-permute-start | bytes 786440 | tf_op jit(solution)/shard_map/ppermute | solution.py:329
  101.4 11.3 %collective-permute-start.28 = (f32[128,512]{1,0:T(8,128)S(1)}, f32[128,512]{1,0:T(8,128)S(1)}, u32[]{:S(2)}, u32[]{:S(2)}) collective-permute-start(f32[128,512]{1,0:T(8,128)S(1)} %get-tuple-element.95), channel_id=1, source_target_pairs={{0,96},{8,104},{16,112},{24,120},{32,0},{40,8},{48,16},{56,24},{64... | collective-permute-start | bytes 786440 | tf_op jit(solution)/shard_map/ppermute | solution.py:329
  102.1 10.6 %collective-permute-start.26 = (f32[128,512]{1,0:T(8,128)S(1)}, f32[128,512]{1,0:T(8,128)S(1)}, u32[]{:S(2)}, u32[]{:S(2)}) collective-permute-start(f32[128,512]{1,0:T(8,128)S(1)} %get-tuple-element.93), channel_id=1, source_target_pairs={{0,32},{8,40},{16,48},{24,56},{32,64},{40,72},{48,80},{56,88},{64,... | collective-permute-start | bytes 786440 | tf_op jit(solution)/shard_map/ppermute | solution.py:329
  102.9 9.8 %collective-permute-start.27 = (f32[128,512]{1,0:T(8,128)S(1)}, f32[128,512]{1,0:T(8,128)S(1)}, u32[]{:S(2)}, u32[]{:S(2)}) collective-permute-start(f32[128,512]{1,0:T(8,128)S(1)} %get-tuple-element.94), channel_id=1, source_target_pairs={{0,64},{8,72},{16,80},{24,88},{32,96},{40,104},{48,112},{56,120},{... | collective-permute-start | bytes 786440 | tf_op jit(solution)/shard_map/ppermute | solution.py:329
  108.6 12.0 %collective-permute-start.23 = (f32[128,512]{1,0:T(8,128)S(1)}, f32[128,512]{1,0:T(8,128)S(1)}, u32[]{:S(2)}, u32[]{:S(2)}) collective-permute-start(f32[128,512]{1,0:T(8,128)S(1)} %add_add_fusion.1), channel_id=1, source_target_pairs={{0,0},{1,25},{2,34},{3,59},{4,68},{5,93},{6,102},{7,127},{8,8},{9,... | collective-permute-start | bytes 786440 | tf_op jit(solution)/shard_map/ppermute | solution.py:351
  112.8 44.7 %copy-start.9 = (f32[512,512]{1,0:T(8,128)S(1)}, f32[512,512]{1,0:T(8,128)}, u32[]{:S(2)}) copy-start(f32[512,512]{1,0:T(8,128)} %param.10) | copy-start | bytes 3145732
  112.8 15.2 %collective-permute-start.29 = (f32[128,512]{1,0:T(8,128)S(1)}, f32[128,512]{1,0:T(8,128)S(1)}, u32[]{:S(2)}, u32[]{:S(2)}) collective-permute-start(f32[128,512]{1,0:T(8,128)S(1)} %add_add_fusion), channel_id=1, source_target_pairs={{0,0},{1,25},{2,34},{3,59},{4,68},{5,93},{6,102},{7,127},{8,8},{9,... | collective-permute-start | bytes 786440 | tf_op jit(solution)/shard_map/ppermute | solution.py:352
  150.5 15.0 %all-to-all-start.1 = ((f32[16,40,128]{2,1,0:T(8,128)}), f32[16,40,128]{2,1,0:T(8,128)S(1)}, u32[]{:S(2)}, u32[]{:S(2)}) async-start(f32[16,40,128]{2,1,0:T(8,128)} %bitcast.43), calls=%async_computation.1 | async-start | bytes 655360 | tf_op jit(solution)/shard_map/all_to_all | solution.py:250
  166.3 11.4 %all-to-all-start.2 = ((f32[16,40,128]{2,1,0:T(8,128)}), f32[16,40,128]{2,1,0:T(8,128)S(1)}, u32[]{:S(2)}, u32[]{:S(2)}) async-start(f32[16,40,128]{2,1,0:T(8,128)} %broadcast_in_dim.2), calls=%async_computation.2 | async-start | bytes 655360 | tf_op jit(solution)/shard_map/all_to_all | solution.py:252
  177.7 18.9 %copy-start.12 = (f32[128,512]{1,0:T(8,128)S(1)}, f32[128,512]{1,0:T(8,128)}, u32[]{:S(2)}) copy-start(f32[128,512]{1,0:T(8,128)} %copy-done.11) | copy-start | bytes 786436
  177.7 19.6 %copy-start.14 = (f32[128,512]{1,0:T(8,128)S(1)}, f32[128,512]{1,0:T(8,128)}, u32[]{:S(2)}) copy-start(f32[128,512]{1,0:T(8,128)} %copy-done.13) | copy-start | bytes 786436
  177.7 9.4 %collective-permute-start.30 = (f32[640,128]{1,0:T(8,128)S(1)}, f32[640,128]{1,0:T(8,128)S(1)}, u32[]{:S(2)}, u32[]{:S(2)}) collective-permute-start(f32[640,128]{1,0:T(8,128)S(1)} %bitcast.85), channel_id=1, source_target_pairs={{0,2},{1,3},{2,4},{3,5},{4,6},{5,7},{6,0},{7,1},{8,10},{9,11},{10,... | collective-permute-start | bytes 983048 | tf_op jit(solution)/shard_map/ppermute | solution.py:363
  178.0 18.1 %collective-permute-start.31 = (f32[640,128]{1,0:T(8,128)S(1)}, f32[640,128]{1,0:T(8,128)S(1)}, u32[]{:S(2)}, u32[]{:S(2)}) collective-permute-start(f32[640,128]{1,0:T(8,128)S(1)} %bitcast.86), channel_id=1, source_target_pairs={{0,6},{1,7},{2,0},{3,1},{4,2},{5,3},{6,4},{7,5},{8,14},{9,15},{10,... | collective-permute-start | bytes 983048 | tf_op jit(solution)/shard_map/ppermute | solution.py:363
  180.4 15.7 %collective-permute-start.32 = (f32[640,128]{1,0:T(8,128)S(1)}, f32[640,128]{1,0:T(8,128)S(1)}, u32[]{:S(2)}, u32[]{:S(2)}) collective-permute-start(f32[640,128]{1,0:T(8,128)S(1)} %bitcast.87), channel_id=1, source_target_pairs={{0,4},{1,5},{2,6},{3,7},{4,0},{5,1},{6,2},{7,3},{8,12},{9,13},{10,... | collective-permute-start | bytes 983048 | tf_op jit(solution)/shard_map/ppermute | solution.py:363
  183.0 15.1 %collective-permute-start.33 = (f32[640,128]{1,0:T(8,128)S(1)}, f32[640,128]{1,0:T(8,128)S(1)}, u32[]{:S(2)}, u32[]{:S(2)}) collective-permute-start(f32[640,128]{1,0:T(8,128)S(1)} %bitcast.88), channel_id=1, source_target_pairs={{0,1},{1,0},{2,3},{3,2},{4,5},{5,4},{6,7},{7,6},{8,9},{9,8},{10,11... | collective-permute-start | bytes 983048 | tf_op jit(solution)/shard_map/ppermute | solution.py:364
  187.1 11.0 %collective-permute-start.34 = (f32[640,128]{1,0:T(8,128)S(1)}, f32[640,128]{1,0:T(8,128)S(1)}, u32[]{:S(2)}, u32[]{:S(2)}) collective-permute-start(f32[640,128]{1,0:T(8,128)S(1)} %collective-permute-done.30.refs_1_), channel_id=1, source_target_pairs={{0,1},{1,0},{2,3},{3,2},{4,5},{5,4},{6,7},{7,6},{8,9},{9,8},{10,11... | collective-permute-start | bytes 983048 | tf_op jit(solution)/shard_map/ppermute | solution.py:364
  196.1 2.0 collective-permute-start.35
  196.1 2.2 %collective-permute-start.36 = (f32[640,128]{1,0:T(8,128)S(1)}, f32[640,128]{1,0:T(8,128)S(1)}, u32[]{:S(2)}, u32[]{:S(2)}) collective-permute-start(f32[640,128]{1,0:T(8,128)S(1)} %collective-permute-done.32.refs_3_), channel_id=1, source_target_pairs={{0,1},{1,0},{2,3},{3,2},{4,5},{5,4},{6,7},{7,6},{8,9},{9,8},{10,11... | collective-permute-start | bytes 983048 | tf_op jit(solution)/shard_map/ppermute | solution.py:364
  (7 other events, 37.4 us)
